TPU v7x, 32 devices: a whole 2x2x4 slice. The times are simulated.
32 devices in a mesh: dp: 2 (over core), head: 2 (over x), blk: 8 (over z, y).
Axes of the slice: x: 2, y: 2, z: 4, core: 2. Of those that a mesh axis runs over, the one named last changes fastest.
Arguments:
- tokens: bfloat16 [2, 2048, 2304], P('dp', ('head', 'blk')), may hold values from -6 to 6
- cotangent: bfloat16 [2, 2048, 2304], P('dp', ('head', 'blk')), may hold values from -6 to 6
- segments: int32 [2, 2048], P('dp'), may hold values from 0 to 3, never falling along the last dimension, each value on 1 to 1024 neighbouring positions
- norm_gains: bfloat16 [2304, 4], P(('dp', 'head', 'blk')), may hold values from 0.25 to 1.75
- qkv_weight: bfloat16 [4096, 2304], P(('dp', 'head', 'blk')), may hold values from -4 to 4
- out_weight: bfloat16 [2304, 2048], P(('dp', 'head', 'blk')), may hold values from -0.125 to 0.125
- gate_up_weight: bfloat16 [9216, 4608], P(('dp', 'head', 'blk')), may hold values from -0.125 to 0.125
- down_weight: bfloat16 [9216, 2304], P(('dp', 'head', 'blk')), may hold values from -0.0625 to 0.0625
Outputs:
- layer_out: bfloat16 [2, 2048, 2304], P('dp', ('head', 'blk'))
- tokens_grad: bfloat16 [2, 2048, 2304], P('dp', ('head', 'blk'))
- norm_gains_grad: float32 [2304, 4], P(('dp', 'head', 'blk'))
- qkv_grad: float32 [4096, 2304], P(('dp', 'head', 'blk'))
- out_grad: float32 [2304, 2048], P(('dp', 'head', 'blk'))
- gate_up_grad: float32 [9216, 4608], P(('dp', 'head', 'blk'))
- down_grad: float32 [9216, 2304], P(('dp', 'head', 'blk'))
Inputs may be any that keep to these rules, and one draw needn't show every extreme that they name: `segments`: document ids never fall along a sequence; every id appears, and one document has exactly 1024 tokens.
All inputs are finite; a program needn't handle non-finite values.
Results may differ from a plain program's by a relative error of at most 0.024.
Values may be sent and summed in bfloat16 or wider, within the bound.
A program may use at most 256 MiB of HBM per device.

v0:
```python
import math

import jax
import jax.numpy as jnp
from jax import lax
from jax.sharding import PartitionSpec as P

HEADS = 8
KV_HEADS = 4
HEAD_DIM = 256


SOFT_CAP = 50.0
NORM_EPS = 1e-06
ROPE_BASE = 10000.0


def passed_along(value, axis, steps):
    count = lax.axis_size(axis)
    first, last = (max(0, -steps), min(count, count - steps))
    return lax.ppermute(value, axis, [(source, source + steps) for source in range(first, last)])


def shortened(value):
    return jax.tree.map(lambda a: a.astype(jnp.bfloat16) if a.dtype == jnp.float32 else a, value)


def shifted(value, axis, by):
    length = lax.axis_size(axis)
    return lax.ppermute(value, axis, [(i, (i + by) % length) for i in range(length)])


def rms_scale(values, gain_row):
    return (
        values * lax.rsqrt(jnp.mean(values * values, axis=-1, keepdims=True) + NORM_EPS) * gain_row
    )


def gelu_tanh(values):
    return jax.nn.gelu(values, approximate=True)


def rope_tables(positions, head_width):
    half_width = head_width // 2
    frequency = jnp.exp(
        jnp.arange(half_width, dtype=jnp.float32) * (-2.0 * math.log(ROPE_BASE) / head_width)
    )
    angles = positions.astype(jnp.float32)[:, None] * frequency[None, :]
    cosine = jnp.concatenate([jnp.cos(angles), jnp.cos(angles)], axis=-1)
    sine_table = jnp.concatenate([jnp.sin(angles), jnp.sin(angles)], axis=-1)
    return (cosine[:, None, None, :], sine_table[:, None, None, :])


def rotate(values, cosine, sine_table):
    half_width = values.shape[-1] // 2
    turned = jnp.concatenate([-values[..., half_width:], values[..., :half_width]], axis=-1)
    return values * cosine + turned * sine_table


def right_product(left_rows, portion):
    return lax.dot_general(
        left_rows, portion, (((1,), (1,)), ((), ())), preferred_element_type=jnp.float32
    )


def first_product(left_rows, portion):
    return lax.dot_general(
        left_rows, portion, (((0,), (0,)), ((), ())), preferred_element_type=jnp.float32
    )


def gather_rows(weight, row_func):
    return row_func(lax.all_gather(weight, ("dp", "head", "blk"), axis=0, tiled=True), jnp.int32(0))


def fold_rows(weight, row_func, initial):
    return row_func(
        initial, lax.all_gather(weight, ("dp", "head", "blk"), axis=0, tiled=True), jnp.int32(0)
    )


def weight_terms(row_func, shard_rows):
    return lax.psum_scatter(
        row_func(jnp.int32(0), lax.axis_size(("dp", "head", "blk")) * shard_rows),
        ("dp", "head", "blk"),
        scatter_dimension=0,
        tiled=True,
    )


def score_terms(queries, key_block, query_pos, query_doc, key_pos, key_doc):
    score_scale = queries.shape[-1] ** (-0.5)
    raw_score = jnp.einsum(
        "qgjd,kgd->gjqk", queries, key_block[:, :, 0], preferred_element_type=jnp.float32
    )
    capped = jnp.tanh(raw_score * (score_scale / SOFT_CAP))
    visible = (key_pos[None, :] <= query_pos[:, None]) & (key_doc[None, :] == query_doc[:, None])
    exp_weights = jnp.where(visible, jnp.exp(SOFT_CAP * capped), 0.0)
    return (capped, exp_weights, score_scale)


def forward_terms(queries, key_block, query_pos, query_doc, key_pos, key_doc):
    capped, exp_weights, score_scale = score_terms(
        queries, key_block, query_pos, query_doc, key_pos, key_doc
    )
    part_sums = jnp.einsum(
        "gjqk,kgd->qgjd",
        exp_weights.astype(jnp.bfloat16),
        key_block[:, :, 1],
        preferred_element_type=jnp.float32,
    )
    part_total = jnp.transpose(jnp.sum(exp_weights, axis=-1), (2, 0, 1))
    return (part_sums, part_total)


def backward_terms(
    queries, key_block, query_pos, query_doc, key_pos, key_doc, sums_grad, total_grad
):
    capped, exp_weights, score_scale = score_terms(
        queries, key_block, query_pos, query_doc, key_pos, key_doc
    )
    exp_grad = jnp.einsum(
        "qgjd,kgd->gjqk", sums_grad, key_block[:, :, 1], preferred_element_type=jnp.float32
    )
    cap_grad = exp_weights * (exp_grad + jnp.transpose(total_grad, (1, 2, 0))[..., None])
    raw_grad = (cap_grad * (1.0 - capped * capped) * score_scale).astype(jnp.bfloat16)
    query_grad = jnp.einsum(
        "gjqk,kgd->qgjd", raw_grad, key_block[:, :, 0], preferred_element_type=jnp.float32
    )
    key_grad = jnp.einsum("gjqk,qgjd->kgd", raw_grad, queries, preferred_element_type=jnp.float32)
    value_grad = jnp.einsum(
        "gjqk,qgjd->kgd",
        exp_weights.astype(jnp.bfloat16),
        sums_grad,
        preferred_element_type=jnp.float32,
    )
    return (query_grad, jnp.stack([key_grad, value_grad], axis=2))


def shards(
    tokens, cotangent, segments, norm_gains, qkv_weight, out_weight, gate_up_weight, down_weight
):
    tok_rows = tokens.shape[1]
    model_width = tokens.shape[2]
    rep_count = HEADS // KV_HEADS
    head_count = lax.axis_size("head")
    blk_count = lax.axis_size("blk")
    own_index = lax.axis_index("head") * blk_count + lax.axis_index("blk")
    doc_ids = segments[0]
    inputs = tokens[0].astype(jnp.float32)
    first_query = own_index * tok_rows
    positions = first_query + jnp.arange(tok_rows, dtype=jnp.int32)
    cosine, sine_table = rope_tables(positions, HEAD_DIM)
    chain_size = head_count * blk_count

    def pass_keys(values):
        return passed_along(values, ("head", "blk"), 1)

    def pass_grads(values):
        return shifted(shortened(values), ("head", "blk"), 1).astype(values.dtype)

    reach_steps = chain_size - 1
    home_steps = (chain_size - reach_steps) % chain_size
    gain_rows = gather_rows(
        norm_gains, lambda portion, offset: jnp.transpose(portion).astype(jnp.float32)
    )
    norm_one_low = rms_scale(inputs, gain_rows[0]).astype(jnp.bfloat16)
    projected_rows = gather_rows(
        qkv_weight, lambda portion, offset: right_product(norm_one_low, portion)
    )
    projected_rows = projected_rows.reshape(tok_rows, KV_HEADS, rep_count + 2, HEAD_DIM)
    turned = rotate(projected_rows[:, :, : rep_count + 1], cosine, sine_table)
    sent_rows = jnp.concatenate([turned, projected_rows[:, :, rep_count + 1 :]], axis=2).astype(
        jnp.bfloat16
    )
    grouped = sent_rows.reshape(tok_rows, -1)
    span_rows = grouped.shape[0]
    grouped = grouped.reshape(span_rows, -1, rep_count + 2, HEAD_DIM)
    queries = grouped[:, :, :rep_count]
    key_values = grouped[:, :, rep_count:]
    row_iota = jnp.arange(tok_rows, dtype=jnp.int32)
    zero_sums = jnp.zeros(queries.shape, jnp.float32)
    zero_total = jnp.zeros(queries.shape[:3], jnp.float32)

    def block_info(part_number, chain_pos):
        block_id = part_number * chain_size + chain_pos
        first_row = block_id * tok_rows
        return (
            block_id,
            first_row + row_iota,
            lax.dynamic_slice_in_dim(doc_ids, first_row, tok_rows, 0),
        )

    def forward_piece(partial_state, held_keys, anchor):
        row_sums, row_total = partial_state
        query_id, query_pos, query_doc = block_info(0, own_index)
        acc_sums = row_sums
        acc_total = row_total
        key_id, key_pos, key_doc = block_info(0, anchor)
        add_sums, add_total = forward_terms(
            queries, held_keys, query_pos, query_doc, key_pos, key_doc
        )
        acc_sums = acc_sums + add_sums
        acc_total = acc_total + add_total
        new_sums = [acc_sums]
        new_total = [acc_total]
        return (jnp.concatenate(new_sums, axis=0), jnp.concatenate(new_total, axis=0))

    def forward_step(chain_step, carry_state):
        held_keys, row_sums, row_total = carry_state
        anchor = (own_index - chain_step + chain_size) % chain_size
        row_sums, row_total = forward_piece((row_sums, row_total), held_keys, anchor)
        return (pass_keys(held_keys), row_sums, row_total)

    held_keys, row_sums, row_total = lax.fori_loop(
        0, reach_steps, forward_step, (key_values, zero_sums, zero_total)
    )
    row_sums, row_total = forward_piece(
        (row_sums, row_total), held_keys, (own_index - reach_steps + chain_size) % chain_size
    )
    attended = row_sums / row_total[..., None]
    attention_result = attended.astype(jnp.bfloat16).reshape(span_rows, -1)
    residual_branch = gather_rows(
        out_weight, lambda portion, offset: right_product(attention_result, portion)
    )
    middle = inputs + rms_scale(residual_branch, gain_rows[1])
    norm_three = rms_scale(middle, gain_rows[2]).astype(jnp.bfloat16)
    gate_up_all, down_all = (
        lax.all_gather(gate_up_weight, ("dp", "head"), axis=0, tiled=True),
        lax.all_gather(down_weight, ("dp", "head"), axis=0, tiled=True),
    )

    def partial_out(row_func, shard_rows):
        return lax.psum_scatter(
            row_func(jnp.int32(0), shard_rows * lax.axis_size("blk")).astype(jnp.bfloat16),
            "blk",
            scatter_dimension=0,
            tiled=True,
        ).astype(jnp.float32)

    gate_all = gate_up_all[:, :model_width]
    up_all = gate_up_all[:, model_width:]
    hidden_portion = lax.all_gather(norm_three, "blk", axis=0, tiled=True)
    gate_activation = right_product(hidden_portion, gate_all)
    up_activation = right_product(hidden_portion, up_all)
    hidden_state = (gelu_tanh(gate_activation) * up_activation).astype(jnp.bfloat16)

    def down_rows(offset, amount):
        return jnp.dot(hidden_state, down_all, preferred_element_type=jnp.float32)

    feedforward_result = partial_out(down_rows, tok_rows)
    result = middle + rms_scale(feedforward_result, gain_rows[3])
    output = result.astype(jnp.bfloat16)[None]
    out_grad_in = cotangent[0].astype(jnp.float32)
    _, post_ffn_back = jax.vjp(rms_scale, feedforward_result, gain_rows[3])
    ffn_grad, gain_grad_four = post_ffn_back(out_grad_in)
    ffn_grad_low = ffn_grad.astype(jnp.bfloat16)
    grad_part = lax.all_gather(ffn_grad_low, "blk", axis=0, tiled=True)
    norm_part = lax.all_gather(norm_three, "blk", axis=0, tiled=True)
    gate_activation = right_product(norm_part, gate_all)
    up_activation = right_product(norm_part, up_all)
    activated, gelu_back = jax.vjp(gelu_tanh, gate_activation)
    hidden_part = (activated * up_activation).astype(jnp.bfloat16)
    hidden_grad = right_product(grad_part, down_all)
    gate_grad = gelu_back(hidden_grad * up_activation)[0].astype(jnp.bfloat16)
    up_grad = (hidden_grad * activated).astype(jnp.bfloat16)
    grad_down = first_product(hidden_part, grad_part)
    grad_gate_up = jnp.concatenate(
        [first_product(gate_grad, norm_part), first_product(up_grad, norm_part)], axis=1
    )
    grad_gate_up, grad_down, keep_gate, keep_up = (grad_gate_up, grad_down, gate_grad, up_grad)

    def input_rows(offset, amount):
        gate_rows = jnp.dot(keep_gate, gate_all, preferred_element_type=jnp.float32)
        return gate_rows + jnp.dot(keep_up, up_all, preferred_element_type=jnp.float32)

    norm_three_grad = partial_out(input_rows, tok_rows)
    gate_up_grad = lax.psum_scatter(
        grad_gate_up.astype(jnp.bfloat16), ("dp", "head"), scatter_dimension=0, tiled=True
    ).astype(jnp.float32)
    down_grad = lax.psum_scatter(
        grad_down.astype(jnp.bfloat16), ("dp", "head"), scatter_dimension=0, tiled=True
    ).astype(jnp.float32)
    _, pre_ffn_back = jax.vjp(rms_scale, middle, gain_rows[2])
    middle_part, gain_grad_three = pre_ffn_back(norm_three_grad)
    middle_grad = out_grad_in + middle_part
    _, post_attn_back = jax.vjp(rms_scale, residual_branch, gain_rows[1])
    branch_grad, gain_grad_two = post_attn_back(middle_grad)
    branch_low = branch_grad.astype(jnp.bfloat16)
    out_grad = weight_terms(
        lambda offset, amount: first_product(branch_low, attention_result), out_weight.shape[0]
    )
    attn_grad = fold_rows(
        out_weight,
        lambda running, portion, offset: jnp.dot(
            branch_low, portion, preferred_element_type=jnp.float32
        ),
        jnp.zeros((tok_rows, attention_result.shape[1]), jnp.float32),
    )
    grouped_grad = attn_grad.astype(jnp.bfloat16).reshape(attended.shape).astype(jnp.float32)
    total_grad = -jnp.sum(grouped_grad * attended, axis=-1) / row_total
    sums_grad = (grouped_grad / row_total[..., None]).astype(jnp.bfloat16)
    zero_query = jnp.zeros(queries.shape, jnp.float32)

    def backward_piece(partial_state, held_keys, anchor):
        query_grad, held_grad = partial_state
        key_parts = [held_grad]
        query_id, query_pos, query_doc = block_info(0, own_index)
        acc_query = query_grad
        key_id, key_pos, key_doc = block_info(0, anchor)
        add_query, add_keys = backward_terms(
            queries, held_keys, query_pos, query_doc, key_pos, key_doc, sums_grad, total_grad
        )
        acc_query = acc_query + add_query
        key_parts[0] = key_parts[0] + add_keys
        new_query = [acc_query]
        return (jnp.concatenate(new_query, axis=0), jnp.concatenate(key_parts, axis=0))

    def backward_step(chain_step, carry_state):
        held_keys, held_grad, query_grad = carry_state
        anchor = (own_index - chain_step + chain_size) % chain_size
        query_grad, held_grad = backward_piece((query_grad, held_grad), held_keys, anchor)
        return (pass_keys(held_keys), pass_grads(held_grad), query_grad)

    zero_keys = jnp.zeros(key_values.shape, jnp.float32)
    held_keys, held_grad, query_grad = lax.fori_loop(
        0, reach_steps, backward_step, (key_values, zero_keys, zero_query)
    )
    query_grad, held_grad = backward_piece(
        (query_grad, held_grad), held_keys, (own_index - reach_steps + chain_size) % chain_size
    )
    held_grad = shifted(held_grad.astype(jnp.bfloat16), ("head", "blk"), home_steps).astype(
        held_grad.dtype
    )
    sent_grad = jnp.concatenate([query_grad, held_grad], axis=2).astype(jnp.bfloat16)
    sent_back = (
        sent_grad.reshape(span_rows, -1)
        .reshape(tok_rows, KV_HEADS, rep_count + 2, HEAD_DIM)
        .astype(jnp.float32)
    )
    unturned = rotate(sent_back[:, :, : rep_count + 1], cosine, -sine_table)
    proj_grad = (
        jnp.concatenate([unturned, sent_back[:, :, rep_count + 1 :]], axis=2)
        .astype(jnp.bfloat16)
        .reshape(tok_rows, -1)
    )
    qkv_grad = weight_terms(
        lambda offset, amount: first_product(proj_grad, norm_one_low), qkv_weight.shape[0]
    )
    norm_one_grad = fold_rows(
        qkv_weight,
        lambda running, portion, offset: jnp.dot(
            proj_grad, portion, preferred_element_type=jnp.float32
        ),
        jnp.zeros((tok_rows, model_width), jnp.float32),
    )
    _, pre_attn_back = jax.vjp(rms_scale, inputs, gain_rows[0])
    input_part, gain_grad_one = pre_attn_back(norm_one_grad)
    tokens_grad = (middle_grad + input_part).astype(jnp.bfloat16)[None]
    gain_terms = jnp.stack([gain_grad_one, gain_grad_two, gain_grad_three, gain_grad_four], axis=1)
    gains_grad = weight_terms(lambda offset, amount: gain_terms, norm_gains.shape[0])
    return (output, tokens_grad, gains_grad, qkv_grad, out_grad, gate_up_grad, down_grad)


def solution(mesh):
    return jax.shard_map(
        shards,
        mesh=mesh,
        in_specs=(
            P("dp", ("head", "blk"), None),
            P("dp", ("head", "blk"), None),
            P("dp", None),
            P(("dp", "head", "blk"), None),
            P(("dp", "head", "blk"), None),
            P(("dp", "head", "blk"), None),
            P(("dp", "head", "blk"), None),
            P(("dp", "head", "blk"), None),
        ),
        out_specs=(
            P("dp", ("head", "blk"), None),
            P("dp", ("head", "blk"), None),
            P(("dp", "head", "blk"), None),
            P(("dp", "head", "blk"), None),
            P(("dp", "head", "blk"), None),
            P(("dp", "head", "blk"), None),
            P(("dp", "head", "blk"), None),
        ),
        check_vma=False,
    )
```

profile of v0, /device:TPU:20, one launch (start us, length us, event | category | flops | bytes accessed | tf_op | source)
XLA Modules:
  0.0 1898.1 jit_solution(5496548673207650503)
XLA Ops:
  9.6 68.4 %all-gather = bf16[32,72,4]{1,2,0:T(4,128)(2,1)S(1)} all-gather(bf16[1,72,4]{1,2,0:T(4,128)(2,1)S(1)} %bitcast.327), channel_id=1, replica_groups=mesh['dp'=2,'head'=2,'blk'=8] {'dp','head','blk'}, dimensions={0}, use_global_device_ids=true | all-gather | bytes 19008 | tf_op jit(solution)/shard_map/all_gather | solution.py:73
  80.3 54.8 %all-gather.8.cloned.1.call-done = bf16[4096,2304]{1,0:T(8,128)(2,1)} async-done(((bf16[128,2304]{1,0:T(8,128)(2,1)}), bf16[4096,2304]{1,0:T(8,128)(2,1)}) %all-gather.8.cloned.1.call-update) | async-done | bytes 18874384 | tf_op jit(solution)/shard_map/all_gather | solution.py:73
  135.1 13.9 fusion.98
  153.5 260.1 %while.42 = (s32[]{:T(128)}, bf16[128,4,2,256]{3,0,1,2:T(8,128)(2,1)S(1)}, f32[128,4,2,256]{3,0,2,1:T(8,128)S(1)}, f32[128,4,2]{0,2,1:T(2,128)S(1)}, s32[]{:T(12...) while((s32[]{:T(128)}, ...), condition=%wide.region_3.4_spmd.clone.clone, body=%wide.region_1.3_spmd.clone.clone.sunk | while | flops 135447824 | bytes 6869375 | solution.py:215
  157.9 17.5 collective-permute-done
  199.7 24.7 %collective-permute-done = bf16[128,4,2,256]{3,0,1,2:T(8,128)(2,1)S(1)} collective-permute-done((bf16[128,4,2,256]{3,0,1,2:T(8,128)(2,1)S(1)}, bf16[128,4,2,256]{3,0,1,2:T(8,128)(2,1)S(1)}, u32[]{:S(2)}, u32[]{:S(2)}) %collective-permute-start) | collective-permute-done | bytes 524320 | tf_op jit(solution)/shard_map/while/body/eval_jaxpr/ppermute | solution.py:21
  231.8 13.8 collective-permute-done
  429.5 88.4 %all-gather.12.cloned.1.call-done = bf16[1024,2304]{1,0:T(8,128)(2,1)} async-done(((bf16[128,2304]{1,0:T(8,128)(2,1)}), bf16[1024,2304]{1,0:T(8,128)(2,1)}) %all-gather.12.cloned.1.call-update) | async-done | bytes 4718608 | tf_op jit(solution)/shard_map/all_gather | solution.py:243
  518.0 9.9 fusion.48
  538.6 21.5 %all-gather.16.cloned.1.call-done = bf16[1152,2304]{1,0:T(8,128)(2,1)} async-done(((bf16[288,2304]{1,0:T(8,128)(2,1)}), bf16[1152,2304]{1,0:T(8,128)(2,1)}) %all-gather.16.cloned.1.call-update) | async-done | bytes 5308432 | tf_op jit(solution)/shard_map/all_gather | solution.py:230
  560.2 10.5 convolution_convert_fusion.3
  570.7 95.4 %reduce-scatter.8.cloned.1.call-done = bf16[128,2304]{1,0:T(8,128)(2,1)} async-done(((bf16[1024,2304]{1,0:T(8,128)(2,1)}), bf16[128,2304]{1,0:T(8,128)(2,1)}) %reduce-scatter.8.cloned.1.call-update) | async-done | bytes 589840 | tf_op jit(solution)/shard_map/reduce_scatter | solution.py:234
  671.8 77.6 %all-gather.18.cloned.1.call-done = bf16[1024,2304]{1,0:T(8,128)(2,1)} async-done(((bf16[128,2304]{1,0:T(8,128)(2,1)}), bf16[1024,2304]{1,0:T(8,128)(2,1)}) %all-gather.18.cloned.1.call-update) | async-done | bytes 4718608 | tf_op jit(solution)/shard_map/all_gather | solution.py:258
  749.4 15.1 multiply_convert_fusion
  773.2 10.3 add_convert_fusion
  817.6 61.4 %reduce-scatter.10.cloned.1.call-done = bf16[128,2304]{1,0:T(8,128)(2,1)} async-done(((bf16[1024,2304]{1,0:T(8,128)(2,1)}), bf16[128,2304]{1,0:T(8,128)(2,1)}) %reduce-scatter.10.cloned.1.call-update) | async-done | bytes 589840 | tf_op jit(solution)/shard_map/reduce_scatter | solution.py:234
  906.5 427.0 %while.43 = (s32[]{:T(128)}, bf16[128,4,2,256]{3,0,1,2:T(8,128)(2,1)}, f32[128,4,2,256]{3,0,1,2:T(8,128)S(1)}, f32[128,4,2,256]{3,0,2,1:T(8,128)}, s32[]{:T(128)...) while((s32[]{:T(128)}, ...), condition=%wide.region_15.16_spmd.clone.clone, body=%wide.region_14.15_spmd.clone.clone.sunk | while | flops 339132672 | bytes 26272236 | solution.py:326
  916.5 11.4 collective-permute-done.2
  948.1 10.6 collective-permute-done.2
  1350.3 17.9 fusion.100
  1368.3 11.8 fusion.85
  1380.1 51.7 %all-reduce = f32[2304,4]{0,1:T(4,128)S(1)} all-reduce(f32[2304,4]{0,1:T(4,128)S(1)} %pad_maximum_fusion.4), channel_id=4, replica_groups=mesh['dp'=2,'head'=2,'blk'=8] {'dp','head','blk'}, use_global_device_ids=true, to_apply=%region_21.22.clone | all-reduce | flops 9216 | bytes 73728
  1442.8 92.8 %reduce-scatter.14.cloned.1.call-done = f32[72,2048]{1,0:T(8,128)} async-done(((f32[2304,2048]{1,0:T(8,128)}), f32[72,2048]{1,0:T(8,128)}) %reduce-scatter.14.cloned.1.call-update) | async-done | bytes 589840 | tf_op jit(solution)/shard_map/reduce_scatter | solution.py:83
  1535.6 355.2 %reduce-scatter.12.cloned.1.call-done = f32[128,2304]{1,0:T(8,128)} async-done(((f32[4096,2304]{1,0:T(8,128)}), f32[128,2304]{1,0:T(8,128)}) %reduce-scatter.12.cloned.1.call-update) | async-done | bytes 1179664 | tf_op jit(solution)/shard_map/reduce_scatter | solution.py:83
  (635 shorter events, 745.4 us)
Async XLA Ops:
  7.2 127.9 %all-gather.8.cloned.1.call-start = ((), (), s32[]{:S(2)}) async-start(), calls=%async_computation.6 | async-start | bytes 19464192 | tf_op jit(solution)/shard_map/all_gather | solution.py:73
  7.9 410.2 %all-gather.10.cloned.1.call-start = ((), (), s32[]{:S(2)}) async-start(), calls=%async_computation.7 | async-start | bytes 9732096 | tf_op jit(solution)/shard_map/all_gather | solution.py:73
  8.7 420.8 %all-gather.14.cloned.1.call-start = ((), (), s32[]{:S(2)}) async-start(), calls=%async_computation.9 | async-start | bytes 13271040 | tf_op jit(solution)/shard_map/all_gather | solution.py:229
  9.4 508.6 %all-gather.12.cloned.1.call-start = ((), (), s32[]{:S(2)}) async-start(), calls=%async_computation.8 | async-start | bytes 5308416 | tf_op jit(solution)/shard_map/all_gather | solution.py:243
  153.6 21.9 %collective-permute-start = (bf16[128,4,2,256]{3,0,1,2:T(8,128)(2,1)S(1)}, bf16[128,4,2,256]{3,0,1,2:T(8,128)(2,1)S(1)}, u32[]{:S(2)}, u32[]{:S(2)}) collective-permute-start(bf16[128,4,2,256]{3,0,1,2:T(8,128)(2,1)S(1)} %copy.133), channel_id=1, source_target_pairs={{0,1},{1,2},{2,3},{3,4},{4,5},{5,6},{6,7},{7,8},{8,9},{9,10},{10,1... | collective-permute-start | bytes 1572872 | tf_op jit(solution)/shard_map/while/body/eval_jaxpr/ppermute | solution.py:21
  192.6 31.8 %collective-permute-start = (bf16[128,4,2,256]{3,0,1,2:T(8,128)(2,1)S(1)}, bf16[128,4,2,256]{3,0,1,2:T(8,128)(2,1)S(1)}, u32[]{:S(2)}, u32[]{:S(2)}) collective-permute-start(bf16[128,4,2,256]{3,0,1,2:T(8,128)(2,1)S(1)} %copy.133), channel_id=1, source_target_pairs={{0,1},{1,2},{2,3},{3,4},{4,5},{5,6},{6,7},{7,8},{8,9},{9,10},{10,1... | collective-permute-start | bytes 1572872 | tf_op jit(solution)/shard_map/while/body/eval_jaxpr/ppermute | solution.py:21
  224.4 21.2 %collective-permute-start = (bf16[128,4,2,256]{3,0,1,2:T(8,128)(2,1)S(1)}, bf16[128,4,2,256]{3,0,1,2:T(8,128)(2,1)S(1)}, u32[]{:S(2)}, u32[]{:S(2)}) collective-permute-start(bf16[128,4,2,256]{3,0,1,2:T(8,128)(2,1)S(1)} %copy.133), channel_id=1, source_target_pairs={{0,1},{1,2},{2,3},{3,4},{4,5},{5,6},{6,7},{7,8},{8,9},{9,10},{10,1... | collective-permute-start | bytes 1572872 | tf_op jit(solution)/shard_map/while/body/eval_jaxpr/ppermute | solution.py:21
  379.9 18.3 collective-permute-start
  428.4 131.8 %all-gather.16.cloned.1.call-start = ((), (), s32[]{:S(2)}) async-start(), calls=%async_computation.10 | async-start | bytes 6635520 | tf_op jit(solution)/shard_map/all_gather | solution.py:230
  429.0 237.2 %reduce-scatter.8.cloned.1.call-start = ((), (), s32[]{:S(2)}) async-start(), calls=%async_computation.11 | async-start | bytes 5308416 | tf_op jit(solution)/shard_map/reduce_scatter | solution.py:234
  570.7 178.7 %all-gather.18.cloned.1.call-start = ((), (), s32[]{:S(2)}) async-start(), calls=%async_computation.12 | async-start | bytes 5308416 | tf_op jit(solution)/shard_map/all_gather | solution.py:258
  671.6 207.4 %reduce-scatter.10.cloned.1.call-start = ((), (), s32[]{:S(2)}) async-start(), calls=%async_computation.13 | async-start | bytes 5308416 | tf_op jit(solution)/shard_map/reduce_scatter | solution.py:234
  783.5 651.5 %reduce-scatter.18.cloned.1.call-start = ((), (), s32[]{:S(2)}) async-start(), calls=%async_computation.17 | async-start | bytes 6635520 | tf_op jit(solution)/shard_map/reduce_scatter | solution.py:281
  794.9 643.1 %reduce-scatter.16.cloned.1.call-start = ((), (), s32[]{:S(2)}) async-start(), calls=%async_computation.16 | async-start | bytes 13271040 | tf_op jit(solution)/shard_map/reduce_scatter | solution.py:278
  817.5 718.1 %reduce-scatter.14.cloned.1.call-start = ((), (), s32[]{:S(2)}) async-start(), calls=%async_computation.15 | async-start | bytes 19464192 | tf_op jit(solution)/shard_map/reduce_scatter | solution.py:83
  906.2 984.6 %reduce-scatter.12.cloned.1.call-start = ((), (), s32[]{:S(2)}) async-start(), calls=%async_computation.14 | async-start | bytes 38928384 | tf_op jit(solution)/shard_map/reduce_scatter | solution.py:83
  912.8 24.7 %collective-permute-start.1 = (bf16[128,4,2,256]{3,0,1,2:T(8,128)(2,1)S(1)}, bf16[128,4,2,256]{3,0,1,2:T(8,128)(2,1)}, u32[]{:S(2)}, u32[]{:S(2)}) collective-permute-start(bf16[128,4,2,256]{3,0,1,2:T(8,128)(2,1)S(1)} %copy.145), channel_id=1, source_target_pairs={{0,1},{1,2},{2,3},{3,4},{4,5},{5,6},{6,7},{7,8},{8,9},{9,10},{10,1... | collective-permute-start | bytes 1572872 | tf_op jit(solution)/shard_map/while/body/eval_jaxpr/ppermute | solution.py:21
  944.8 22.7 %collective-permute-start.1 = (bf16[128,4,2,256]{3,0,1,2:T(8,128)(2,1)S(1)}, bf16[128,4,2,256]{3,0,1,2:T(8,128)(2,1)}, u32[]{:S(2)}, u32[]{:S(2)}) collective-permute-start(bf16[128,4,2,256]{3,0,1,2:T(8,128)(2,1)S(1)} %copy.145), channel_id=1, source_target_pairs={{0,1},{1,2},{2,3},{3,4},{4,5},{5,6},{6,7},{7,8},{8,9},{9,10},{10,1... | collective-permute-start | bytes 1572872 | tf_op jit(solution)/shard_map/while/body/eval_jaxpr/ppermute | solution.py:21
  976.0 21.2 %collective-permute-start.1 = (bf16[128,4,2,256]{3,0,1,2:T(8,128)(2,1)S(1)}, bf16[128,4,2,256]{3,0,1,2:T(8,128)(2,1)}, u32[]{:S(2)}, u32[]{:S(2)}) collective-permute-start(bf16[128,4,2,256]{3,0,1,2:T(8,128)(2,1)S(1)} %copy.145), channel_id=1, source_target_pairs={{0,1},{1,2},{2,3},{3,4},{4,5},{5,6},{6,7},{7,8},{8,9},{9,10},{10,1... | collective-permute-start | bytes 1572872 | tf_op jit(solution)/shard_map/while/body/eval_jaxpr/ppermute | solution.py:21
  1006.4 20.1 %collective-permute-start.1 = (bf16[128,4,2,256]{3,0,1,2:T(8,128)(2,1)S(1)}, bf16[128,4,2,256]{3,0,1,2:T(8,128)(2,1)}, u32[]{:S(2)}, u32[]{:S(2)}) collective-permute-start(bf16[128,4,2,256]{3,0,1,2:T(8,128)(2,1)S(1)} %copy.145), channel_id=1, source_target_pairs={{0,1},{1,2},{2,3},{3,4},{4,5},{5,6},{6,7},{7,8},{8,9},{9,10},{10,1... | collective-permute-start | bytes 1572872 | tf_op jit(solution)/shard_map/while/body/eval_jaxpr/ppermute | solution.py:21
  1037.7 19.2 %collective-permute-start.1 = (bf16[128,4,2,256]{3,0,1,2:T(8,128)(2,1)S(1)}, bf16[128,4,2,256]{3,0,1,2:T(8,128)(2,1)}, u32[]{:S(2)}, u32[]{:S(2)}) collective-permute-start(bf16[128,4,2,256]{3,0,1,2:T(8,128)(2,1)S(1)} %copy.145), channel_id=1, source_target_pairs={{0,1},{1,2},{2,3},{3,4},{4,5},{5,6},{6,7},{7,8},{8,9},{9,10},{10,1... | collective-permute-start | bytes 1572872 | tf_op jit(solution)/shard_map/while/body/eval_jaxpr/ppermute | solution.py:21
  1068.6 19.2 %collective-permute-start.1 = (bf16[128,4,2,256]{3,0,1,2:T(8,128)(2,1)S(1)}, bf16[128,4,2,256]{3,0,1,2:T(8,128)(2,1)}, u32[]{:S(2)}, u32[]{:S(2)}) collective-permute-start(bf16[128,4,2,256]{3,0,1,2:T(8,128)(2,1)S(1)} %copy.145), channel_id=1, source_target_pairs={{0,1},{1,2},{2,3},{3,4},{4,5},{5,6},{6,7},{7,8},{8,9},{9,10},{10,1... | collective-permute-start | bytes 1572872 | tf_op jit(solution)/shard_map/while/body/eval_jaxpr/ppermute | solution.py:21
  1099.0 18.6 collective-permute-start.1
  1315.4 18.1 collective-permute-start.1
  (105 other events, 2577.1 us)
Sparse Core Ops, SparseCore 0:
  10.9 124.1 all-gather.7
  138.0 105.6 all-gather.9
  245.2 72.9 all-gather.13
  428.5 89.4 all-gather.11
  519.4 40.7 all-gather.15
  570.8 95.3 reduce-scatter.7
  671.7 77.6 all-gather.17
  783.6 95.2 reduce-scatter.9
  882.1 51.7 reduce-scatter.17
  936.4 127.3 reduce-scatter.15
  1070.8 464.8 reduce-scatter.13
  1542.5 348.2 reduce-scatter.11
where the time goes:
time: 1910 us; the launch traced here: 1900 us
  waiting for transfers between devices  1150 us (60%)
  starting transfers between devices  248 us (13%)
  matrix products  233 us (12%)
  blocking collectives  120 us (6%)
  other arithmetic  68.7 us (4%)
  local copies, waits for them, and re-layouts  57.4 us (3%)
    reduce_scatter x2, waiting for transfers between devices, weight_terms(): lax.psum_scatter(row_func(jnp.int32(0), lax.axis_size(('dp', 'head', 'blk...  448 us
    ppermute x30, waiting for transfers between devices, passed_along(): lax.ppermute(value, axis, [(source, source + steps) for source in range(f...  226 us
    ppermute x30, starting transfers between devices, passed_along(): lax.ppermute(value, axis, [(source, source + steps) for source in range(f...  182 us
    reduce_scatter x2, waiting for transfers between devices, partial_out(): lax.psum_scatter(row_func(jnp.int32(0), shard_rows * lax.axis_size('blk')...  157 us
    all_gather x1, waiting for transfers between devices, shards(): hidden_portion = lax.all_gather(norm_three, 'blk', axis=0, tiled=True)  88.4 us
    all_gather x1, waiting for transfers between devices, shards(): grad_part = lax.all_gather(ffn_grad_low, 'blk', axis=0, tiled=True)  77.6 us
    ppermute x16, waiting for transfers between devices, shifted(): lax.ppermute(value, axis, [(i, (i + by) % length) for i in range(length)])  77.3 us
    all_gather x1, blocking collectives, gather_rows(): lax.all_gather(weight, ('dp', 'head', 'blk'), axis=0, tiled=True)  68.4 us
  transfers between devices with their start and end apart: 58, of which 54 were waited for; matrix products, arithmetic and copies ran while one was open for 16% of the time, Pallas kernels for 0%

commit v1 on v0

v1 whole, which is shorter than its diff:
```python
import functools
import math

import jax
import jax.numpy as jnp
from jax import lax
from jax.experimental import pallas as pl
from jax.experimental.pallas import tpu as pltpu
from jax.sharding import PartitionSpec as P

HEADS = 8
KV_HEADS = 4
HEAD_DIM = 256
REPS = HEADS // KV_HEADS
GROUPS = 4
SOFT_CAP = 50.0
NORM_EPS = 1e-06
ROPE_BASE = 10000.0
SCORE_SCALE = HEAD_DIM ** (-0.5)

MESH = pl.DeviceIdType.MESH
VMEM_LIMIT = 60 * 1024 * 1024


class Place:
    def __init__(self, count):
        self.count = count
        self.inner = 4 if count >= 32 else 2
        self.outer = count // self.inner
        self.here = lax.axis_index("blk")
        self.line = self.here // self.inner
        self.side = lax.rem(self.here, self.inner)
        self.core = lax.axis_index("dp")
        self.half = lax.axis_index("head")
        self.group = 2 * self.core + self.half

    def at(self, line, side):
        return {"blk": line * self.inner + side}

    def beside(self, step):
        return lax.rem(self.side + step, self.inner)

    def partner(self):
        return {"dp": 1 - self.core}

    def across(self):
        return {"head": 1 - self.half}

    def corner(self):
        return {"dp": 1 - self.core, "head": 1 - self.half}


def remote(src, dst, sent, came, device):
    return pltpu.make_async_remote_copy(
        src_ref=src, dst_ref=dst, send_sem=sent, recv_sem=came, device_id=device, device_id_type=MESH
    )


def greet(place, blk=False, core=False, half=False, corner=False):
    sem = pltpu.get_barrier_semaphore()
    amount = jnp.int32(0)

    def hello(device):
        pl.semaphore_signal(sem, inc=1, device_id=device, device_id_type=MESH)

    if blk:
        up, down = place.line < place.outer - 1, place.line > 0
        pl.when(up)(lambda: hello(place.at(place.line + 1, place.side)))
        pl.when(down)(lambda: hello(place.at(place.line - 1, place.side)))
        amount = amount + up.astype(jnp.int32) + down.astype(jnp.int32) + (place.inner - 1)
        for step in range(1, place.inner):
            hello(place.at(place.line, place.beside(step)))
    for wanted, device in (
        (core, place.partner()),
        (half, place.across()),
        (corner, place.corner()),
    ):
        if wanted:
            hello(device)
            amount = amount + 1
    pl.semaphore_wait(sem, amount)


def together(*tasks):
    tasks = list(tasks)
    while tasks:
        for task in list(tasks):
            try:
                next(task)
            except StopIteration:
                tasks.remove(task)


def gather_blk_sems(place_count):
    inner = 4 if place_count >= 32 else 2
    return [
        pltpu.SemaphoreType.DMA((1 + inner, place_count)),
        pltpu.SemaphoreType.DMA((place_count,)),
        pltpu.SemaphoreType.DMA,
    ]


def gather_blk(place, src, out, sent, came, own):
    outer, inner, line, side = place.outer, place.inner, place.line, place.side
    copy = pltpu.make_async_copy(src, out.at[place.here], own)
    copy.start()
    finishing = []
    is_below, is_above = line < outer - 1, line > 0

    def spread(what, piece, up, down):
        def send(kind, device):
            return remote(what, out.at[piece], sent.at[kind, piece], came.at[piece], device)

        if up is not None:
            pl.when(up)(lambda: send(0, place.at(line + 1, side)).start())
            finishing.append((up, lambda: send(0, place.at(line + 1, side)).wait_send()))
        if down is not None:
            pl.when(down)(lambda: send(1, place.at(line - 1, side)).start())
            finishing.append((down, lambda: send(1, place.at(line - 1, side)).wait_send()))
        for step in range(1, inner):
            send(1 + step, place.at(line, place.beside(step))).start()
            finishing.append(
                (None, lambda step=step: send(1 + step, place.at(line, place.beside(step))).wait_send())
            )

    def arrived(piece):
        remote(
            src, out.at[piece], sent.at[0, piece], came.at[piece], place.at(line, place.beside(1))
        ).wait_recv()

    spread(src, place.here, is_below, is_above)
    yield
    ends = []
    for away in range(1, outer):
        for sign in (-1, 1):
            there = line + sign * away
            fits = (there >= 0) if sign < 0 else (there < outer)
            piece = there * inner + side

            @pl.when(fits)
            def _(piece=piece, sign=sign):
                arrived(piece)
                mark = len(finishing)
                if sign < 0:
                    spread(out.at[piece], piece, is_below, None)
                else:
                    spread(out.at[piece], piece, None, is_above)
                later = finishing[mark:]
                del finishing[mark:]
                ends.append(later)

        yield

    for there in range(outer):
        for step in range(1, inner):
            arrived(there * inner + place.beside(step))
    for needed, finish in finishing:
        if needed is None:
            finish()
        else:
            pl.when(needed)(finish)
    index = 0
    for away in range(1, outer):
        for sign in (-1, 1):
            there = line + sign * away
            fits = (there >= 0) if sign < 0 else (there < outer)
            later = ends[index]
            index += 1

            @pl.when(fits)
            def _(later=later):
                for needed, finish in later:
                    if needed is None:
                        finish()
                    else:
                        pl.when(needed)(finish)

    copy.wait()


def add_into(out, *terms):
    def one(i, carry):
        total = terms[0][i].astype(jnp.float32)
        for term in terms[1:]:
            total = total + term[i].astype(jnp.float32)
        out[i] = total.astype(out.dtype)
        return carry

    lax.fori_loop(0, out.shape[0], one, 0)


def reduce_blk_scratch(place_count, piece, dtype):
    inner = 4 if place_count >= 32 else 2
    outer = place_count // inner
    return [
        pltpu.VMEM((outer, inner - 1) + piece, dtype),
        pltpu.VMEM((outer + 1,) + piece, dtype),
        pltpu.VMEM((outer,) + piece, dtype),
        pltpu.SemaphoreType.DMA((outer, inner - 1)),
        pltpu.SemaphoreType.DMA((outer, inner - 1)),
        pltpu.SemaphoreType.DMA((outer,)),
        pltpu.SemaphoreType.DMA((outer + 1,)),
    ]


def reduce_blk(place, part, out, beside, along, held, side_sent, side_came, line_sent, line_came):
    outer, inner, line, side = place.outer, place.inner, place.line, place.side

    def side_copy(there, step):
        to = place.beside(step)
        return remote(
            part.at[there * inner + to],
            beside.at[there, inner - step - 1],
            side_sent.at[there, step - 1],
            side_came.at[there, inner - step - 1],
            place.at(line, to),
        )

    def line_copy(there, slot, to):
        return remote(
            held.at[there], along.at[slot], line_sent.at[there], line_came.at[slot], place.at(to, side)
        )

    def each(away, act):
        for sign in (-1, 1) if away else (0,):
            there = line + sign * away
            if away == 0:
                act(there, 0)
            else:
                fits = (there >= 0) if sign < 0 else (there < outer)
                pl.when(fits)(functools.partial(act, there, sign))

    def send_aside(there, sign):
        for step in range(1, inner):
            side_copy(there, step).start()

    def side_terms(there):
        for step in range(1, inner):
            side_copy(there, step).wait_recv()
        return [part.at[there * inner + side]] + [beside.at[there, k] for k in range(inner - 1)]

    def pass_on(there, sign):
        terms = side_terms(there)
        starts = (line == outer - 1) if sign < 0 else (line == 0)

        @pl.when(starts)
        def _():
            add_into(held.at[there], *terms)

        @pl.when(jnp.logical_not(starts))
        def _():
            line_copy(there, there, line + sign).wait_recv()
            add_into(held.at[there], along.at[there], *terms)

        slot = there if sign < 0 else jnp.where(there == line + 1, outer, there)
        line_copy(there, slot, line + sign).start()

    for away in range(outer - 1, -1, -1):
        each(away, send_aside)
    yield
    for away in range(outer - 1, 0, -1):
        each(away, pass_on)
        yield
    terms = side_terms(line)
    below, above = line > 0, line < outer - 1
    from_above, from_below = along.at[line], along.at[outer]

    @pl.when(above)
    def _():
        line_copy(line, line, line + 1).wait_recv()

    @pl.when(below)
    def _():
        line_copy(line, outer, line - 1).wait_recv()

    @pl.when(above & below)
    def _():
        add_into(out, from_above, from_below, *terms)

    @pl.when(above & jnp.logical_not(below))
    def _():
        add_into(out, from_above, *terms)

    @pl.when(jnp.logical_not(above) & below)
    def _():
        add_into(out, from_below, *terms)

    yield

    def end_line(there, sign):
        line_copy(there, there, line + sign).wait_send()

    for away in range(outer - 1, 0, -1):
        each(away, end_line)
    for there in range(outer):
        for step in range(1, inner):
            side_copy(there, step).wait_send()


def gather_group_sems():
    return [pltpu.SemaphoreType.DMA((3,)), pltpu.SemaphoreType.DMA((4,)), pltpu.SemaphoreType.DMA]


def gather_group(place, src, out, sent, came, own):
    copy = pltpu.make_async_copy(src, out.at[place.group], own)
    copy.start()
    mine, other = place.group, 2 * place.core + (1 - place.half)
    to_half = remote(src, out.at[mine], sent.at[0], came.at[mine], place.across())
    to_core = remote(src, out.at[mine], sent.at[1], came.at[mine], place.partner())
    to_half.start()
    to_core.start()
    yield
    remote(src, out.at[other], sent.at[0], came.at[other], place.across()).wait_recv()
    relay = remote(out.at[other], out.at[other], sent.at[2], came.at[other], place.partner())
    relay.start()
    yield
    for half in (0, 1):
        slot = 2 * (1 - place.core) + half
        remote(src, out.at[slot], sent.at[0], came.at[slot], place.partner()).wait_recv()
    to_half.wait_send()
    to_core.wait_send()
    relay.wait_send()
    copy.wait()


def reduce_group_scratch(piece, dtype):
    return [
        pltpu.VMEM((2,) + piece, dtype),
        pltpu.VMEM(piece, dtype),
        pltpu.VMEM(piece, dtype),
        pltpu.SemaphoreType.DMA((3,)),
        pltpu.SemaphoreType.DMA((3,)),
    ]


def reduce_group(place, part, out, from_core, from_half, held, sent, came):
    far = 2 * (1 - place.core) + (1 - place.half)
    near = 2 * (1 - place.core) + place.half
    first = remote(part.at[far], from_core.at[1], sent.at[0], came.at[0], place.partner())
    second = remote(part.at[near], from_core.at[0], sent.at[1], came.at[1], place.partner())
    first.start()
    second.start()
    yield
    first.wait_recv()
    add_into(held, part.at[2 * place.core + (1 - place.half)], from_core.at[1])
    third = remote(held, from_half, sent.at[2], came.at[2], place.across())
    third.start()
    yield
    second.wait_recv()
    third.wait_recv()
    add_into(out, part.at[place.group], from_core.at[0], from_half)
    first.wait_send()
    second.wait_send()
    third.wait_send()


def exchange_group_sems():
    return [pltpu.SemaphoreType.DMA((3,)), pltpu.SemaphoreType.DMA((4,)), pltpu.SemaphoreType.DMA]


def exchange_group(place, src, out, sent, came, own):
    mine = place.group
    copy = pltpu.make_async_copy(src.at[mine], out.at[mine], own)
    copy.start()
    core, half = place.core, place.half
    links = (
        (2 * (1 - core) + (1 - half), place.corner()),
        (2 * core + (1 - half), place.across()),
        (2 * (1 - core) + half, place.partner()),
    )
    copies = [
        remote(src.at[to], out.at[mine], sent.at[k], came.at[mine], device)
        for k, (to, device) in enumerate(links)
    ]
    for one in copies:
        one.start()
    yield
    for k, (peer, device) in enumerate(links):
        remote(src.at[peer], out.at[peer], sent.at[k], came.at[peer], device).wait_recv()
    for one in copies:
        one.wait_send()
    copy.wait()


def transfer(name, number, body, ins, outs, scratch, moved, out_spaces=None):
    spaces = out_spaces or [pl.ANY] * len(outs)
    return pl.pallas_call(
        body,
        name=name,
        out_shape=outs,
        in_specs=[pl.BlockSpec(memory_space=pltpu.VMEM)] * len(ins),
        out_specs=[pl.BlockSpec(memory_space=space) for space in spaces],
        scratch_shapes=scratch,
        compiler_params=pltpu.CompilerParams(
            collective_id=number, has_side_effects=True, vmem_limit_bytes=VMEM_LIMIT
        ),
        cost_estimate=pl.CostEstimate(flops=0, bytes_accessed=moved * 40, transcendentals=0),
    )(*ins)


def shape(dims, dtype):
    return jax.ShapeDtypeStruct(tuple(dims), dtype)


def slabs(rows):
    return math.gcd(rows, 16)


def all_gather_blk(value, count, number):
    def body(src, out, *sems):
        place = Place(count)
        greet(place, blk=True)
        together(gather_blk(place, src, out, *sems))

    return transfer(
        f"gather{number}",
        number,
        body,
        [value],
        [shape((count,) + value.shape, value.dtype)],
        gather_blk_sems(count),
        value.size * 2 * count,
    )[0]


def reduce_scatter_blk(value, count, number):
    piece = value.shape[1:]

    def body(part, out, *scratch):
        place = Place(count)
        greet(place, blk=True)
        together(reduce_blk(place, part, out, *scratch))

    return transfer(
        f"reduce{number}",
        number,
        body,
        [value],
        [shape(piece, jnp.float32)],
        reduce_blk_scratch(count, piece, value.dtype),
        value.size * 2,
        [pltpu.VMEM],
    )[0]


def gather_first(qkv, out_parts, tokens, gains, docs, count, number):
    names = 5

    def body(*refs):
        qkv_ref, out_ref, tok_ref, gain_ref, doc_ref = refs[:names]
        qkv_all, out_all, tok_all, gain_all, doc_all = refs[names : 2 * names]
        out_mine, gain_mine = refs[2 * names : 2 * names + 2]
        sems = list(refs[2 * names + 2 :])

        def take(amount):
            taken = sems[:amount]
            del sems[:amount]
            return taken

        place = Place(count)
        greet(place, blk=True, core=True, half=True, corner=True)

        def gain_task(near, far):
            yield from gather_blk(place, gain_ref, gain_mine, *near)
            yield from gather_group(place, gain_mine, gain_all, *far)

        def out_task(near, far):
            yield from exchange_group(place, out_ref, out_mine, *near)
            yield from gather_blk(place, out_mine, out_all, *far)

        def doc_task(sent, came, own):
            copy = pltpu.make_async_copy(doc_ref, doc_all.at[place.core], own)
            copy.start()
            send = remote(doc_ref, doc_all.at[place.core], sent, came, place.partner())
            send.start()
            yield
            remote(doc_ref, doc_all.at[1 - place.core], sent, came, place.partner()).wait_recv()
            send.wait_send()
            copy.wait()

        together(
            gain_task(take(3), take(3)),
            doc_task(*take(3)),
            gather_group(place, tok_ref, tok_all, *take(3)),
            gather_blk(place, qkv_ref, qkv_all, *take(3)),
            out_task(take(3), take(3)),
        )

    ins = [qkv, out_parts, tokens, gains, docs]
    return transfer(
        f"first{number}",
        number,
        body,
        ins,
        [
            shape((count,) + qkv.shape, qkv.dtype),
            shape((count,) + out_parts.shape, out_parts.dtype),
            shape((GROUPS,) + tokens.shape, tokens.dtype),
            shape((GROUPS, count) + gains.shape, gains.dtype),
            shape((2,) + docs.shape, docs.dtype),
        ],
        [
            pltpu.VMEM(out_parts.shape, out_parts.dtype),
            pltpu.VMEM((count,) + gains.shape, gains.dtype),
        ]
        + gather_blk_sems(count)
        + gather_group_sems()
        + [pltpu.SemaphoreType.DMA] * 3
        + gather_group_sems()
        + gather_blk_sems(count)
        + exchange_group_sems()
        + gather_blk_sems(count),
        (qkv.size + out_parts.size) * 2 * count,
    )


def reduce_last(qkv_part, out_part, norm_part, gain_part, count, number):
    out_piece, gain_piece = out_part.shape[1:], gain_part.shape[1:]
    qkv_piece, norm_piece = qkv_part.shape[1:], norm_part.shape[1:]

    def body(*refs):
        qkv_ref, out_ref, norm_ref, gain_ref = refs[:4]
        qkv_sum, out_sum, norm_sum, gain_sum = refs[4:8]
        out_mine, gain_mine = refs[8:10]
        rest = list(refs[10:])

        def take(amount):
            taken = rest[:amount]
            del rest[:amount]
            return taken

        place = Place(count)
        greet(place, blk=True, core=True, half=True, corner=True)

        def out_task(near, far):
            yield from reduce_blk(place, out_ref, out_mine, *near)
            yield from exchange_group(place, out_mine, out_sum, *far)

        def gain_task(near, far):
            yield from reduce_blk(place, gain_ref, gain_mine, *near)
            yield from reduce_group(place, gain_mine, gain_sum, *far)

        together(
            gain_task(take(7), take(5)),
            reduce_group(place, norm_ref, norm_sum, *take(5)),
            out_task(take(7), take(3)),
            reduce_blk(place, qkv_ref, qkv_sum, *take(7)),
        )

    return transfer(
        f"last{number}",
        number,
        body,
        [qkv_part, out_part, norm_part, gain_part],
        [
            shape(qkv_piece, jnp.float32),
            shape(out_piece, jnp.bfloat16),
            shape(norm_piece, jnp.float32),
            shape(gain_piece[1:], jnp.float32),
        ],
        [pltpu.VMEM(out_piece, jnp.bfloat16), pltpu.VMEM(gain_piece, jnp.float32)]
        + reduce_blk_scratch(count, gain_piece, jnp.float32)
        + reduce_group_scratch(gain_piece[1:], jnp.float32)
        + reduce_group_scratch(norm_piece, jnp.bfloat16)
        + reduce_blk_scratch(count, out_piece, jnp.bfloat16)
        + exchange_group_sems()
        + reduce_blk_scratch(count, qkv_piece, jnp.bfloat16),
        (qkv_part.size + out_part.size) * 2,
        [pltpu.VMEM] * 4,
    )


def all_gather_group(value, number):
    def body(src, out, *sems):
        place = Place(lax.axis_size("blk"))
        greet(place, core=True, half=True)
        together(gather_group(place, src, out, *sems))

    return transfer(
        f"group{number}",
        number,
        body,
        [value],
        [shape((GROUPS,) + value.shape, value.dtype)],
        gather_group_sems(),
        value.size * 8,
    )[0]


def reduce_scatter_group(value, number):
    piece = value.shape[1:]

    def body(part, out, *scratch):
        place = Place(lax.axis_size("blk"))
        greet(place, core=True, half=True)
        together(reduce_group(place, part, out, *scratch))

    return transfer(
        f"fold{number}",
        number,
        body,
        [value],
        [shape(piece, jnp.float32)],
        reduce_group_scratch(piece, value.dtype),
        value.size * 2,
        [pltpu.VMEM],
    )[0]


def attention_scores(q2, k, query_pos, query_doc, key_block, key_doc, rows):
    raw = lax.dot_general(q2, k, (((1,), (1,)), ((), ())), preferred_element_type=jnp.float32)
    capped = jnp.tanh(raw * (SCORE_SCALE / SOFT_CAP))
    key_pos = key_block * rows + lax.broadcasted_iota(jnp.int32, (1, rows), 1)
    visible = (key_pos <= query_pos) & (key_doc == query_doc)
    return capped, jnp.where(visible, jnp.exp(SOFT_CAP * capped), 0.0)


def attention_query(q_ref, doc_ref, here, count, rows):
    half = pl.program_id(1)
    block = half * count + here
    q2 = jnp.concatenate([q_ref[0, :, :HEAD_DIM], q_ref[0, :, HEAD_DIM:]], axis=0)
    inside = lax.broadcasted_iota(jnp.int32, (rows, 1), 0)
    position = block * rows + jnp.concatenate([inside, inside], axis=0)
    doc = jnp.concatenate([doc_ref[0], doc_ref[0]], axis=0)
    return block, q2, position, doc


def attention_forward_kernel(
    count, here_ref, q_ref, kv_ref, doc_ref, key_doc_ref, attn_ref, full_ref, total_ref, acc, tot
):
    rows = q_ref.shape[1]
    block, q2, position, doc = attention_query(q_ref, doc_ref, here_ref[0], count, rows)
    acc[...] = jnp.zeros_like(acc)
    tot[...] = jnp.zeros_like(tot)

    def one(key_block, carry):
        key_half = (key_block >= count).astype(jnp.int32)
        kv = kv_ref.at[key_block - key_half * count, key_half]
        _, weights = attention_scores(
            q2, kv[:, :HEAD_DIM], position, doc, key_block, key_doc_ref[0, key_block], rows
        )
        tot[...] += jnp.sum(weights, axis=-1, keepdims=True)
        acc[...] += jnp.dot(
            weights.astype(jnp.bfloat16), kv[:, HEAD_DIM:], preferred_element_type=jnp.float32
        )
        return carry

    lax.fori_loop(jnp.maximum(block - count, 0), block + 1, one, 0)
    attended = acc[...] / tot[...]
    attended = jnp.concatenate([attended[:rows], attended[rows:]], axis=1)
    full_ref[0] = attended
    attn_ref[0] = attended.astype(jnp.bfloat16)
    total_ref[0] = tot[...]


def attention_backward_kernel(
    count,
    here_ref,
    q_ref,
    kv_ref,
    doc_ref,
    key_doc_ref,
    grad_ref,
    full_ref,
    total_ref,
    dq_ref,
    dkv_ref,
    acc,
    key_acc,
):
    rows = q_ref.shape[1]
    half = pl.program_id(1)
    block, q2, position, doc = attention_query(q_ref, doc_ref, here_ref[0], count, rows)
    total = total_ref[0]
    grad = grad_ref[0].astype(jnp.float32)
    grad2 = jnp.concatenate([grad[:, :HEAD_DIM], grad[:, HEAD_DIM:]], axis=0)
    full2 = jnp.concatenate([full_ref[0, :, :HEAD_DIM], full_ref[0, :, HEAD_DIM:]], axis=0)
    total_grad = -jnp.sum(grad2 * full2, axis=-1, keepdims=True) / total
    sums_grad = (grad2 / total).astype(jnp.bfloat16)
    acc[...] = jnp.zeros_like(acc)

    @pl.when(half == 0)
    def _():
        def clear(i, carry):
            key_acc[i] = jnp.zeros(key_acc.shape[1:], jnp.float32)
            return carry

        lax.fori_loop(0, key_acc.shape[0], clear, 0)

    def one(key_block, carry):
        key_half = (key_block >= count).astype(jnp.int32)
        inner = key_block - key_half * count
        kv = kv_ref.at[inner, key_half]
        keys = kv[:, :HEAD_DIM]
        capped, weights = attention_scores(
            q2, keys, position, doc, key_block, key_doc_ref[0, key_block], rows
        )
        exp_grad = lax.dot_general(
            sums_grad, kv[:, HEAD_DIM:], (((1,), (1,)), ((), ())), preferred_element_type=jnp.float32
        )
        raw_grad = (
            weights * (exp_grad + total_grad) * (1.0 - capped * capped) * SCORE_SCALE
        ).astype(jnp.bfloat16)
        acc[...] += jnp.dot(raw_grad, keys, preferred_element_type=jnp.float32)
        over_rows = (((0,), (0,)), ((), ()))
        slot = inner * 2 + key_half
        key_acc[slot, :, :HEAD_DIM] += lax.dot_general(
            raw_grad, q2, over_rows, preferred_element_type=jnp.float32
        )
        key_acc[slot, :, HEAD_DIM:] += lax.dot_general(
            weights.astype(jnp.bfloat16), sums_grad, over_rows, preferred_element_type=jnp.float32
        )
        return carry

    lax.fori_loop(jnp.maximum(block - count, 0), block + 1, one, 0)
    dq = acc[...]
    dq_ref[0] = jnp.concatenate([dq[:rows], dq[rows:]], axis=1).astype(jnp.bfloat16)

    @pl.when(half == 1)
    def _():
        def put(i, carry):
            for k in (0, 1):
                dkv_ref[i, k] = key_acc[i * 2 + k].astype(jnp.bfloat16)
            return carry

        lax.fori_loop(0, count, put, 0)


def attention_specs(count, rows, width):
    query = pl.BlockSpec((1, rows, width), lambda s, h, here: (2 * s + h, 0, 0))
    keys = pl.BlockSpec((count, 2, rows, 2 * HEAD_DIM), lambda s, h, here: (0, s, 0, 0))
    doc = pl.BlockSpec((1, rows, 1), lambda s, h, here: (2 * s + h, 0, 0))
    key_doc = pl.BlockSpec((1, 2 * count, 1, rows), lambda s, h, here: (s, 0, 0, 0))
    total = pl.BlockSpec((1, REPS * rows, 1), lambda s, h, here: (2 * s + h, 0, 0))
    return query, keys, doc, key_doc, total


def attention_forward(here, q, kv, doc, key_doc):
    count, _, rows, _ = kv.shape
    width = REPS * HEAD_DIM
    query, keys, doc_spec, key_doc_spec, total = attention_specs(count, rows, width)
    return pl.pallas_call(
        functools.partial(attention_forward_kernel, count),
        name="attend",
        grid_spec=pltpu.PrefetchScalarGridSpec(
            num_scalar_prefetch=1,
            grid=(2, 2),
            in_specs=[query, keys, doc_spec, key_doc_spec],
            out_specs=[query, query, total],
            scratch_shapes=[
                pltpu.VMEM((REPS * rows, HEAD_DIM), jnp.float32),
                pltpu.VMEM((REPS * rows, 1), jnp.float32),
            ],
        ),
        out_shape=[
            shape((GROUPS, rows, width), jnp.bfloat16),
            shape((GROUPS, rows, width), jnp.float32),
            shape((GROUPS, REPS * rows, 1), jnp.float32),
        ],
        compiler_params=pltpu.CompilerParams(vmem_limit_bytes=VMEM_LIMIT),
        cost_estimate=pl.CostEstimate(flops=10**9, bytes_accessed=40 * 2**20, transcendentals=0),
    )(here, q, kv, doc, key_doc)


def attention_backward(here, q, kv, doc, key_doc, grad, full, totals):
    count, _, rows, _ = kv.shape
    width = REPS * HEAD_DIM
    query, keys, doc_spec, key_doc_spec, total = attention_specs(count, rows, width)
    return pl.pallas_call(
        functools.partial(attention_backward_kernel, count),
        name="attend_back",
        grid_spec=pltpu.PrefetchScalarGridSpec(
            num_scalar_prefetch=1,
            grid=(2, 2),
            in_specs=[query, keys, doc_spec, key_doc_spec, query, query, total],
            out_specs=[query, keys],
            scratch_shapes=[
                pltpu.VMEM((REPS * rows, HEAD_DIM), jnp.float32),
                pltpu.VMEM((2 * count, rows, 2 * HEAD_DIM), jnp.float32),
            ],
        ),
        out_shape=[shape((GROUPS, rows, width), jnp.bfloat16), shape(kv.shape, jnp.bfloat16)],
        compiler_params=pltpu.CompilerParams(vmem_limit_bytes=VMEM_LIMIT),
        cost_estimate=pl.CostEstimate(flops=2 * 10**9, bytes_accessed=80 * 2**20, transcendentals=0),
    )(here, q, kv, doc, key_doc, grad, full, totals)


def rms_scale(values, gain_row):
    return (
        values * lax.rsqrt(jnp.mean(values * values, axis=-1, keepdims=True) + NORM_EPS) * gain_row
    )


def gelu_tanh(values):
    return jax.nn.gelu(values, approximate=True)


def rope_tables(positions):
    half_width = HEAD_DIM // 2
    frequency = jnp.exp(
        jnp.arange(half_width, dtype=jnp.float32) * (-2.0 * math.log(ROPE_BASE) / HEAD_DIM)
    )
    angles = positions.astype(jnp.float32)[:, None] * frequency[None, :]
    cosine = jnp.concatenate([jnp.cos(angles), jnp.cos(angles)], axis=-1)
    sine = jnp.concatenate([jnp.sin(angles), jnp.sin(angles)], axis=-1)
    return cosine[:, None, :], sine[:, None, :]


def rotate(values, cosine, sine):
    half_width = HEAD_DIM // 2
    turned = jnp.concatenate([-values[..., half_width:], values[..., :half_width]], axis=-1)
    return values * cosine + turned * sine


def dot(left, right, contract):
    return lax.dot_general(left, right, (contract, ((), ())), preferred_element_type=jnp.float32)


LAST = ((1,), (1,))
PLAIN = ((1,), (0,))
FIRST = ((0,), (0,))


def shards(
    tokens, cotangent, segments, norm_gains, qkv_weight, out_weight, gate_up_weight, down_weight
):
    _, rows, width = tokens.shape
    count = lax.axis_size("blk")
    here = lax.axis_index("blk")
    mine = 2 * lax.axis_index("dp") + lax.axis_index("head")
    group_rows = GROUPS * rows
    head_width = REPS * HEAD_DIM
    bf16 = jnp.bfloat16
    slab = slabs(rows)
    piece = (rows // slab, slab, width)

    gate_up_all = lax.all_gather(gate_up_weight, ("dp", "head"), axis=0, tiled=True)
    down_all = lax.all_gather(down_weight, ("dp", "head"), axis=0, tiled=True)

    gain_rows = norm_gains.shape[0]
    gain_lanes = -(-gain_rows // 128) * 128
    gains_sent = jnp.pad(
        jnp.transpose(norm_gains).astype(jnp.float32), ((0, 4), (0, gain_lanes - gain_rows))
    )
    out_rows = out_weight.shape[0]
    out_sent = jnp.transpose(out_weight.reshape(out_rows, GROUPS, head_width), (1, 0, 2))
    qkv_rows = qkv_weight.shape[0]
    qkv_slab = slabs(qkv_rows)
    qkv_piece = (qkv_rows // qkv_slab, qkv_slab, width)
    qkv_all, out_all, tokens_all, gains_all, docs_all = gather_first(
        qkv_weight, out_sent, tokens[0], gains_sent, segments.reshape(-1, 128), count, 1
    )
    gains = jnp.transpose(gains_all[:, :, :4, :gain_rows], (2, 0, 1, 3)).reshape(4, width)
    qkv_head = qkv_all.reshape(count * qkv_rows, width)
    out_head = out_all.reshape(count, GROUPS, out_rows, head_width)
    out_head = jnp.transpose(out_head, (1, 0, 2, 3)).reshape(width, head_width)
    docs = docs_all.reshape(2, 2, count, rows)
    key_doc = docs.reshape(2, 2 * count, 1, rows)
    own_doc = lax.dynamic_index_in_dim(docs, here, 2, keepdims=False).reshape(GROUPS, rows, 1)
    here_one = here.reshape(1)

    group_tokens = tokens_all.reshape(group_rows, width).astype(jnp.float32)
    norm_one = rms_scale(group_tokens, gains[0]).astype(bf16)
    proj = dot(norm_one, qkv_head, LAST)
    inside = jnp.arange(rows, dtype=jnp.int32)
    position = jnp.concatenate([here * rows + inside, (count + here) * rows + inside])
    cosine, sine = rope_tables(jnp.concatenate([position, position]))
    proj = proj.reshape(group_rows, REPS + 2, HEAD_DIM)
    turned = rotate(proj[:, : REPS + 1], cosine, sine)
    sent = jnp.concatenate([turned, proj[:, REPS + 1 :]], axis=1).astype(bf16)
    queries = sent[:, :REPS].reshape(GROUPS, rows, head_width)
    own_kv = sent[:, REPS:].reshape(group_rows, 2 * HEAD_DIM)
    kv_slab = slabs(group_rows)
    kv_piece = (group_rows // kv_slab, kv_slab, 2 * HEAD_DIM)
    kv = all_gather_blk(own_kv, count, 2).reshape(count, GROUPS, rows, 2 * HEAD_DIM)
    attn, attended, totals = attention_forward(here_one, queries, kv, own_doc, key_doc)
    attn = attn.reshape(group_rows, head_width)
    branch_part = dot(attn, out_head, LAST).astype(bf16)
    branch = reduce_scatter_group(branch_part.reshape((GROUPS,) + piece), 3).reshape(rows, width)
    inputs = tokens[0].astype(jnp.float32)
    middle = inputs + rms_scale(branch, gains[1])
    norm_three = rms_scale(middle, gains[2]).astype(bf16)

    gate_all = gate_up_all[:, :width]
    up_all = gate_up_all[:, width:]
    norm_all = all_gather_blk(norm_three, count, 4).reshape(count * rows, width)
    gate = dot(norm_all, gate_all, LAST)
    up = dot(norm_all, up_all, LAST)
    hidden = (gelu_tanh(gate) * up).astype(bf16)
    ffn_part = dot(hidden, down_all, PLAIN).astype(bf16)
    ffn_out = reduce_scatter_blk(ffn_part.reshape((count,) + piece), count, 5).reshape(rows, width)
    output = (middle + rms_scale(ffn_out, gains[3])).astype(bf16)[None]

    out_cotangent = cotangent[0].astype(jnp.float32)
    _, post_ffn_back = jax.vjp(rms_scale, ffn_out, gains[3])
    ffn_grad, gain_grad_four = post_ffn_back(out_cotangent)
    grad_all = all_gather_blk(ffn_grad.astype(bf16), count, 6).reshape(count * rows, width)
    activated, gelu_back = jax.vjp(gelu_tanh, gate)
    hidden_grad = dot(grad_all, down_all, LAST)
    gate_grad = gelu_back(hidden_grad * up)[0].astype(bf16)
    up_grad = (hidden_grad * activated).astype(bf16)
    norm_part = dot(gate_grad, gate_all, PLAIN) + dot(up_grad, up_all, PLAIN)
    norm_three_grad = reduce_scatter_blk(
        norm_part.astype(bf16).reshape((count,) + piece), count, 7
    ).reshape(rows, width)
    down_part = dot(hidden, grad_all, FIRST).astype(bf16)
    gate_up_part = jnp.concatenate(
        [dot(gate_grad, norm_all, FIRST), dot(up_grad, norm_all, FIRST)], axis=1
    ).astype(bf16)
    gate_up_grad = lax.psum_scatter(
        gate_up_part, ("dp", "head"), scatter_dimension=0, tiled=True
    ).astype(jnp.float32)
    down_grad = lax.psum_scatter(
        down_part, ("dp", "head"), scatter_dimension=0, tiled=True
    ).astype(jnp.float32)

    _, pre_ffn_back = jax.vjp(rms_scale, middle, gains[2])
    middle_part, gain_grad_three = pre_ffn_back(norm_three_grad)
    middle_grad = out_cotangent + middle_part
    _, post_attn_back = jax.vjp(rms_scale, branch, gains[1])
    branch_grad, gain_grad_two = post_attn_back(middle_grad)
    branch_all = all_gather_group(branch_grad.astype(bf16), 8).reshape(group_rows, width)
    attn_grad = dot(branch_all, out_head, PLAIN).astype(bf16).reshape(GROUPS, rows, head_width)
    out_part = dot(branch_all, attn, FIRST).astype(bf16)
    out_part = jnp.transpose(out_part.reshape(GROUPS, count, out_rows, head_width), (1, 0, 2, 3))
    dq, dkv_part = attention_backward(
        here_one, queries, kv, own_doc, key_doc, attn_grad, attended, totals
    )
    dkv = reduce_scatter_blk(dkv_part.reshape((count,) + kv_piece), count, 9)
    sent_grad = jnp.concatenate(
        [
            dq.reshape(group_rows, REPS, HEAD_DIM),
            dkv.astype(bf16).reshape(group_rows, 2, HEAD_DIM),
        ],
        axis=1,
    ).astype(jnp.float32)
    unturned = rotate(sent_grad[:, : REPS + 1], cosine, -sine)
    proj_grad = (
        jnp.concatenate([unturned, sent_grad[:, REPS + 1 :]], axis=1)
        .astype(bf16)
        .reshape(group_rows, (REPS + 2) * HEAD_DIM)
    )
    qkv_part = dot(proj_grad, norm_one, FIRST).astype(bf16)
    norm_one_part = dot(proj_grad, qkv_head, PLAIN)
    _, gain_back = jax.vjp(lambda gain: rms_scale(group_tokens, gain), gains[0])
    (gain_grad_one,) = gain_back(norm_one_part)
    gain_part = jnp.stack([gain_grad_one, gain_grad_two, gain_grad_three, gain_grad_four])
    gain_part = jnp.transpose(gain_part.reshape(4, GROUPS, count, gain_rows), (2, 1, 0, 3))
    gain_part = jnp.pad(gain_part, ((0, 0), (0, 0), (0, 4), (0, gain_lanes - gain_rows)))
    qkv_grad, out_grad, norm_one_grad, gain_grad = reduce_last(
        qkv_part.reshape((count,) + qkv_piece),
        out_part,
        norm_one_part.astype(bf16).reshape((GROUPS,) + piece),
        gain_part[:, :, None],
        count,
        10,
    )
    qkv_grad = qkv_grad.reshape(qkv_rows, width)
    out_grad = (
        jnp.transpose(out_grad, (1, 0, 2)).reshape(out_rows, GROUPS * head_width).astype(jnp.float32)
    )
    gain_grad = jnp.transpose(gain_grad.reshape(8, gain_lanes)[:4, :gain_rows])
    _, pre_attn_back = jax.vjp(lambda values: rms_scale(values, gains[0]), inputs)
    (input_part,) = pre_attn_back(norm_one_grad.reshape(rows, width))
    tokens_grad = (middle_grad + input_part).astype(bf16)[None]
    return (output, tokens_grad, gain_grad, qkv_grad, out_grad, gate_up_grad, down_grad)


def solution(mesh):
    whole = ("dp", "head", "blk")
    return jax.shard_map(
        shards,
        mesh=mesh,
        in_specs=(
            P("dp", ("head", "blk"), None),
            P("dp", ("head", "blk"), None),
            P("dp", None),
            P(whole, None),
            P(whole, None),
            P(whole, None),
            P(whole, None),
            P(whole, None),
        ),
        out_specs=(
            P("dp", ("head", "blk"), None),
            P("dp", ("head", "blk"), None),
            P(whole, None),
            P(whole, None),
            P(whole, None),
            P(whole, None),
            P(whole, None),
        ),
        check_vma=False,
    )
```

time: 1910 us -> 845 us (0.44)
  waiting for transfers between devices: 1150 us -> 1.42 us
  Pallas kernels: 0 us -> 600 us
  starting transfers between devices: 248 us -> 0.33 us
  blocking collectives: 120 us -> 0 us
  matrix products: 233 us -> 122 us
    reduce_scatter x6 -> x2, waiting for transfers between devices: 605 us -> 0.01 us  [the longest x1 0.01 us: shards(): lax.psum_scatter(down_part, ('dp', 'head'), scatter_dimension=0, tiled=True)]
    pallas_call x0 -> x12, Pallas kernels: none -> 600 us  [the longest x10 566 us: transfer(): pl.pallas_call(body, name=name, out_shape=outs, in_specs=[pl.BlockSpec(me...]
    ppermute x46 -> x0, waiting for transfers between devices: 303 us -> none  [the longest x30 226 us: passed_along(): lax.ppermute(value, axis, [(source, source + steps) for source in range(f...]
    ppermute x46 -> x0, starting transfers between devices: 247 us -> none  [the longest x30 182 us: passed_along(): lax.ppermute(value, axis, [(source, source + steps) for source in range(f...]
    all_gather x5 -> x1, waiting for transfers between devices: 242 us -> 0.01 us  [shards(): down_all = lax.all_gather(down_weight, ('dp', 'head'), axis=0, tiled=True)]
    dot_general x127 -> x15, matrix products: 233 us -> 122 us  [dot(): lax.dot_general(left, right, (contract, ((), ())), preferred_element_type...]
    all_gather x1 -> x0, blocking collectives: 68.4 us -> none  [gather_rows(): lax.all_gather(weight, ('dp', 'head', 'blk'), axis=0, tiled=True)]
    unnamed x1 -> x0, blocking collectives: 51.7 us -> none
  transfers between devices with their start and end apart: 58 -> 4, of which waited for: 54 -> 0; matrix products, arithmetic and copies ran while one was open for 16% -> 21% of each run, Pallas kernels for 0% -> 59%
where the time goes in v1:
time: 845 us; the launch traced here: 835 us
  Pallas kernels  600 us (71%)
  matrix products  122 us (14%)
  other arithmetic  52.3 us (6%)
  local copies, waits for them, and re-layouts  44.3 us (5%)
  between operations  14.9 us (2%)
    pallas_call x10, Pallas kernels, transfer(): pl.pallas_call(body, name=name, out_shape=outs, in_specs=[pl.BlockSpec(me...  566 us
    dot_general x15, matrix products, dot(): lax.dot_general(left, right, (contract, ((), ())), preferred_element_type...  122 us
    pallas_call x1, Pallas kernels, attention_backward(): pl.pallas_call(functools.partial(attention_backward_kernel, count), name=...  19.7 us
  transfers between devices with their start and end apart: 4, of which 0 were waited for; matrix products, arithmetic and copies ran while one was open for 21% of the time, Pallas kernels for 59%

profile of v1, /device:TPU:20, one launch (start us, length us, event | category | flops | bytes accessed | tf_op | source)
XLA Modules:
  0.0 834.8 jit_solution(1853067862516642662)
XLA Ops:
  10.1 86.2 %first1.1 = (bf16[8,128,2304]{2,1,0:T(8,128)(2,1)}, bf16[8,4,72,512]{3,2,1,0:T(8,128)(2,1)}, bf16[4,128,2304]{2,1,0:T(8,128)(2,1)}, f32[4,8,8,128]{3,2,1,0:T(8,128)}, s32[2,16,128]{2,1,0:T(8,128)}) custom-call(bf16[128,2304]{1,0:T(8,128)(2,1)} %refs_0_.1, bf16[4,72,512]{2,1,0:T(8,128)(2,1)} %bitcast.212, bf16[128,2304]{1,0:T(8,128)(2,1)} %bitcast.182, ...), custom_call_target="tpu_custom_call" | custom-call | bytes 283115520 | tf_op jit(solution)/shard_map/first1/pallas_call | solution.py:387
  112.2 47.8 %gather2.1 = bf16[8,512,512]{2,1,0:T(8,128)(2,1)} custom-call(bf16[512,512]{1,0:T(8,128)(2,1)} %copy.41.src), custom_call_target="tpu_custom_call" | custom-call | bytes 167772160 | tf_op jit(solution)/shard_map/gather2/pallas_call | solution.py:387
  163.5 14.6 %attend.1 = (bf16[4,128,512]{2,1,0:T(8,128)(2,1)}, f32[4,128,512]{2,1,0:T(8,128)}, f32[4,256,1]{2,1,0:T(8,128)}) custom-call(s32[1]{0:T(128)} %bitcast.here_ref, bf16[4,128,512]{2,1,0:T(8,128)(2,1)} %copy.40.q_ref, bf16[8,4,128,512]{3,2,1,0:T(8,128)(2,1)} %bitcast.186, s32[4,128,1]{2,1,0:T(8,128)} %copy.26.doc_ref, s32[2,16,1,128]{3,2,1,0:T(1,128)} %bitcast.218), custom_call_target="tpu_custom_call" | custom-call | flops 1000000000 | bytes 41943040 | tf_op jit(solution)/shard_map/attend/pallas_call | solution.py:742
  182.0 21.2 %fold3.1 = f32[8,16,2304]{2,1,0:T(8,128)} custom-call(bf16[4,8,16,2304]{3,2,1,0:T(8,128)(2,1)} %bitcast.208), custom_call_target="tpu_custom_call" | custom-call | bytes 94371840 | tf_op jit(solution)/shard_map/fold3/pallas_call | solution.py:387
  208.9 55.7 %gather4.1 = bf16[8,128,2304]{2,1,0:T(8,128)(2,1)} custom-call(bf16[128,2304]{1,0:T(8,128)(2,1)} %multiply_convert_fusion.3.src), custom_call_target="tpu_custom_call" | custom-call | bytes 188743680 | tf_op jit(solution)/shard_map/gather4/pallas_call | solution.py:387
  265.3 9.9 %fusion.14 = f32[1024,1152]{1,0:T(8,128)S(1)} fusion(bf16[1024,2304]{1,0:T(8,128)(2,1)} %bitcast.193, bf16[1152,4608]{1,0:T(8,128)(2,1)} %all-gather.3.cloned.1.call-done), kind=kOutput, calls=%fused_computation.29 | convolution fusion | flops 5435817984 | bytes 14745600 | tf_op jit(solution)/shard_map/dot_general | solution.py:816
  277.4 8.6 %multiply_convert_fusion.1 = (bf16[1024,1152]{1,0:T(8,128)(2,1)}, f32[1024,1152]{1,0:T(8,128)}) fusion(f32[1024,1152]{1,0:T(8,128)S(1)} %fusion.14, bf16[1024,2304]{1,0:T(8,128)(2,1)S(1)} %bitcast.196, bf16[1152,4608]{1,0:T(8,128)(2,1)S(1)} %copy-done.39), kind=kOutput, calls=%fused_computation.21 | convolution fusion | flops 5447614464 | bytes 21823488 | tf_op jit(solution)/shard_map/dot_general | solution.py:816
  286.1 10.7 %convolution_convert_fusion.4 = bf16[1024,2304]{1,0:T(8,128)(2,1)} fusion(bf16[1024,1152]{1,0:T(8,128)(2,1)} %get-tuple-element.77, bf16[1152,2304]{1,0:T(8,128)(2,1)} %all-gather.5.cloned.1.call-done), kind=kOutput, calls=%fused_computation.8 | convolution fusion | flops 5438177280 | bytes 12386304 | tf_op jit(solution)/shard_map/dot_general | solution.py:816
  296.8 59.2 %reduce5.1 = f32[8,16,2304]{2,1,0:T(8,128)} custom-call(bf16[8,8,16,2304]{3,2,1,0:T(8,128)(2,1)} %bitcast.192), custom_call_target="tpu_custom_call" | custom-call | bytes 188743680 | tf_op jit(solution)/shard_map/reduce5/pallas_call | solution.py:387
  365.5 52.0 %gather6.1 = bf16[8,128,2304]{2,1,0:T(8,128)(2,1)} custom-call(bf16[128,2304]{1,0:T(8,128)(2,1)} %fusion.23.src), custom_call_target="tpu_custom_call" | custom-call | bytes 188743680 | tf_op jit(solution)/shard_map/gather6/pallas_call | solution.py:387
  417.5 10.5 %convolution_convert_fusion = bf16[1152,2304]{1,0:T(8,128)(2,1)} fusion(bf16[1024,1152]{1,0:T(8,128)(2,1)} %get-tuple-element.77, bf16[1024,2304]{1,0:T(8,128)(2,1)} %bitcast.197), kind=kOutput, calls=%fused_computation | convolution fusion | flops 5438472192 | bytes 12386304 | tf_op jit(solution)/shard_map/dot_general | solution.py:816
  428.2 15.0 %multiply_convert_fusion = (bf16[1024,1152]{1,0:T(8,128)(2,1)S(1)}, bf16[1024,1152]{1,0:T(8,128)(2,1)S(1)}) fusion(f32[1024,1152]{1,0:T(8,128)} %copy-done.44, f32[1024,1152]{1,0:T(8,128)} %get-tuple-element.78, bf16[1024,2304]{1,0:T(8,128)(2,1)} %bitcast.198, bf16[1152,2304]{1,0:T(8,128)(2,1)} %all-gather.5.cloned.1.call-done), kind=kOutput, calls=%fused_computation.20 | convolution fusion | flops 5464129536 | bytes 24182784 | tf_op jit(solution)/shard_map/dot_general | solution.py:816
  443.2 10.2 %convolution_convert_fusion.1 = bf16[1152,2304]{1,0:T(8,128)(2,1)S(1)} fusion(bf16[1024,1152]{1,0:T(8,128)(2,1)S(1)} %get-tuple-element.47, bf16[1024,2304]{1,0:T(8,128)(2,1)} %bitcast.194), kind=kOutput, calls=%fused_computation.1 | convolution fusion | flops 5438472192 | bytes 12386304 | tf_op jit(solution)/shard_map/dot_general | solution.py:816
  453.4 8.5 %convolution_convert_fusion.2 = bf16[1152,2304]{1,0:T(8,128)(2,1)S(1)} fusion(bf16[1024,1152]{1,0:T(8,128)(2,1)S(1)} %get-tuple-element.48, bf16[1024,2304]{1,0:T(8,128)(2,1)} %bitcast.195), kind=kOutput, calls=%fused_computation.2 | convolution fusion | flops 5438472192 | bytes 12386304 | tf_op jit(solution)/shard_map/dot_general | solution.py:816
  466.6 9.6 %fusion.12 = f32[1024,2304]{1,0:T(8,128)S(1)} fusion(bf16[1024,1152]{1,0:T(8,128)(2,1)} %copy-done.43, bf16[1152,4608]{1,0:T(8,128)(2,1)} %all-gather.3.cloned.1.call-done), kind=kOutput, calls=%fused_computation.27 | convolution fusion | flops 5435817984 | bytes 17104896 | tf_op jit(solution)/shard_map/dot_general | solution.py:816
  476.3 10.7 %add_convert_fusion = bf16[1024,2304]{1,0:T(8,128)(2,1)} fusion(f32[1024,2304]{1,0:T(8,128)S(1)} %fusion.12, bf16[1024,1152]{1,0:T(8,128)(2,1)S(1)} %copy-done.42, bf16[1152,4608]{1,0:T(8,128)(2,1)} %all-gather.3.cloned.1.call-done), kind=kOutput, calls=%fused_computation.4 | convolution fusion | flops 5440536576 | bytes 21823488 | tf_op jit(solution)/shard_map/dot_general | solution.py:816
  487.0 59.3 %reduce7.1 = f32[8,16,2304]{2,1,0:T(8,128)} custom-call(bf16[8,8,16,2304]{3,2,1,0:T(8,128)(2,1)} %bitcast.191), custom_call_target="tpu_custom_call" | custom-call | bytes 188743680 | tf_op jit(solution)/shard_map/reduce7/pallas_call | solution.py:387
  559.4 21.7 %group8.1 = bf16[4,128,2304]{2,1,0:T(8,128)(2,1)} custom-call(bf16[128,2304]{1,0:T(8,128)(2,1)} %fusion.31.src), custom_call_target="tpu_custom_call" | custom-call | bytes 94371840 | tf_op jit(solution)/shard_map/group8/pallas_call | solution.py:387
  585.6 19.7 %attend_back.1 = (bf16[4,128,512]{2,1,0:T(8,128)(2,1)}, bf16[8,4,128,512]{3,2,1,0:T(8,128)(2,1)}) custom-call(s32[1]{0:T(128)} %bitcast.here_ref, bf16[4,128,512]{2,1,0:T(8,128)(2,1)} %copy.40.q_ref, bf16[8,4,128,512]{3,2,1,0:T(8,128)(2,1)} %bitcast.187, s32[4,128,1]{2,1,0:T(8,128)} %copy.26.doc_ref, s32[2,16,1,128]{3,2,1,0:T(1,128)} %bitcast.219, ...), custom_call_target="tpu_custom_call" | custom-call | flops 2000000000 | bytes 83886080 | tf_op jit(solution)/shard_map/attend_back/pallas_call | solution.py:769
  605.3 56.7 %reduce9.1 = f32[32,16,512]{2,1,0:T(8,128)} custom-call(bf16[8,32,16,512]{3,2,1,0:T(8,128)(2,1)} %bitcast.200), custom_call_target="tpu_custom_call" | custom-call | bytes 167772160 | tf_op jit(solution)/shard_map/reduce9/pallas_call | solution.py:387
  689.6 6.9 fusion.8
  700.2 6.8 convolution_convert_fusion.3
  707.0 105.6 %last10.1 = (f32[8,16,2304]{2,1,0:T(8,128)}, bf16[4,72,512]{2,1,0:T(8,128)(2,1)}, f32[8,16,2304]{2,1,0:T(8,128)}, f32[1,8,128]{2,1,0:T(8,128)}) custom-call(bf16[8,8,16,2304]{3,2,1,0:T(8,128)(2,1)} %bitcast.190, bf16[8,4,72,512]{3,2,1,0:T(8,128)(2,1)} %bitcast.189, bf16[4,8,16,2304]{3,2,1,0:T(8,128)(2,1)} %bitcast.209, ...), custom_call_target="tpu_custom_call" | custom-call | bytes 283115520 | tf_op jit(solution)/shard_map/last10/pallas_call | solution.py:387
  822.0 4.9 convert_element_type.191
  (187 shorter events, 107.7 us)
Async XLA Ops:
  7.2 258.1 %all-gather.3.cloned.1.call-start = ((), (), s32[]{:S(2)}) async-start(), calls=%async_computation.2 | async-start | bytes 13271040 | tf_op jit(solution)/shard_map/all_gather | solution.py:837
  7.9 278.1 %all-gather.5.cloned.1.call-start = ((), (), s32[]{:S(2)}) async-start(), calls=%async_computation.3 | async-start | bytes 6635520 | tf_op jit(solution)/shard_map/all_gather | solution.py:838
  8.7 810.3 %reduce-scatter.5.cloned.1.call-start = ((), (), s32[]{:S(2)}) async-start(), calls=%async_computation.5 | async-start | bytes 6635520 | tf_op jit(solution)/shard_map/reduce_scatter | solution.py:913
  97.7 110.0 %copy-start.17 = (f32[2304]{0:T(1024)}, f32[2304]{0:T(1024)S(1)}, u32[]{:S(2)}) copy-start(f32[2304]{0:T(1024)S(1)} %mul.550) | copy-start | bytes 27652
  101.5 5.5 copy-start.12
  163.5 14.7 %copy-start.13 = (bf16[4,8,72,512]{3,2,1,0:T(8,128)(2,1)}, bf16[4,8,72,512]{3,2,1,0:T(8,128)(2,1)S(1)}, u32[]{:S(2)}) copy-start(bf16[4,8,72,512]{3,2,1,0:T(8,128)(2,1)S(1)} %copy.27) | copy-start | bytes 7077892
  182.0 24.0 %copy-start.1 = (bf16[1,128,2304]{2,1,0:T(8,128)(2,1)S(1)}, bf16[1,128,2304]{2,1,0:T(8,128)(2,1)}, u32[]{:S(2)}) copy-start(bf16[1,128,2304]{2,1,0:T(8,128)(2,1)} %param.8) | copy-start | bytes 1769476
  206.0 58.6 %copy-start.25 = (f32[128]{0:T(128)}, f32[128]{0:T(128)S(1)}, u32[]{:S(2)}) copy-start(f32[128]{0:T(128)S(1)} %rsqrt.67) | copy-start | bytes 1540
  207.7 57.0 %copy-start.34 = (f32[128]{0:T(128)}, f32[128]{0:T(128)S(1)}, u32[]{:S(2)}) copy-start(f32[128]{0:T(128)S(1)} %multiply_reduce_fusion.8) | copy-start | bytes 1540
  207.7 56.9 %copy-start.28 = (f32[128]{0:T(128)}, f32[128]{0:T(128)S(1)}, u32[]{:S(2)}) copy-start(f32[128]{0:T(128)S(1)} %fusion.46) | copy-start | bytes 1540
  265.3 12.1 %copy-start.10 = (bf16[8,128,2304]{2,1,0:T(8,128)(2,1)S(1)}, bf16[8,128,2304]{2,1,0:T(8,128)(2,1)}, u32[]{:S(2)}) copy-start(bf16[8,128,2304]{2,1,0:T(8,128)(2,1)} %gather4.1) | copy-start | bytes 14155780
  265.3 12.1 %copy-start.39 = (bf16[1152,4608]{1,0:T(8,128)(2,1)S(1)}, bf16[1152,4608]{1,0:T(8,128)(2,1)}, u32[]{:S(2)}) copy-start(bf16[1152,4608]{1,0:T(8,128)(2,1)} %all-gather.3.cloned.1.call-done) | copy-start | bytes 31850500
  296.8 61.3 %copy-start.7 = (bf16[1,128,2304]{2,1,0:T(8,128)(2,1)S(1)}, bf16[1,128,2304]{2,1,0:T(8,128)(2,1)}, u32[]{:S(2)}) copy-start(bf16[1,128,2304]{2,1,0:T(8,128)(2,1)} %param.9) | copy-start | bytes 1769476
  296.8 61.3 %copy-start.23 = (f32[2304]{0:T(1024)S(1)}, f32[2304]{0:T(1024)}, u32[]{:S(2)}) copy-start(f32[2304]{0:T(1024)} %mul.561) | copy-start | bytes 27652
  356.0 7.7 copy-start.3
  428.0 394.0 %reduce-scatter.3.cloned.1.call-start = ((), (), s32[]{:S(2)}) async-start(), calls=%async_computation.4 | async-start | bytes 13271040 | tf_op jit(solution)/shard_map/reduce_scatter | solution.py:910
  443.2 10.2 %copy-start.41 = (bf16[1024,1152]{1,0:T(8,128)(2,1)}, bf16[1024,1152]{1,0:T(8,128)(2,1)S(1)}, u32[]{:S(2)}) copy-start(bf16[1024,1152]{1,0:T(8,128)(2,1)S(1)} %get-tuple-element.47) | copy-start | bytes 7077892
  443.2 10.2 %copy-start.43 = (bf16[1024,1152]{1,0:T(8,128)(2,1)}, bf16[1024,1152]{1,0:T(8,128)(2,1)S(1)}, u32[]{:S(2)}) copy-start(bf16[1024,1152]{1,0:T(8,128)(2,1)S(1)} %get-tuple-element.48) | copy-start | bytes 7077892
  466.6 9.6 %copy-start.42 = (bf16[1024,1152]{1,0:T(8,128)(2,1)S(1)}, bf16[1024,1152]{1,0:T(8,128)(2,1)}, u32[]{:S(2)}) copy-start(bf16[1024,1152]{1,0:T(8,128)(2,1)} %copy-done.41) | copy-start | bytes 7077892
  487.0 59.4 %copy-start.18 = (f32[2304]{0:T(1024)S(1)}, f32[2304]{0:T(1024)}, u32[]{:S(2)}) copy-start(f32[2304]{0:T(1024)} %copy-done.17) | copy-start | bytes 27652
  487.0 59.4 %copy-start.26 = (f32[128]{0:T(128)S(1)}, f32[128]{0:T(128)}, u32[]{:S(2)}) copy-start(f32[128]{0:T(128)} %copy-done.25) | copy-start | bytes 1540
  546.4 6.4 copy-start.2
  688.9 7.7 copy-start.16
  707.0 107.8 %copy-start.22 = (f32[2304]{0:T(1024)S(1)}, f32[2304]{0:T(1024)}, u32[]{:S(2)}) copy-start(f32[2304]{0:T(1024)} %copy-done.21) | copy-start | bytes 27652
  (26 other events, 77.6 us)
Sparse Core Ops, SparseCore 0:
  9.6 80.5 all-gather.2
  91.7 41.3 all-gather.4
  428.1 52.0 reduce-scatter.4
  482.7 87.9 reduce-scatter.2

commit v2 on v1

--- a/solution.py
+++ b/solution.py
@@ -33,6 +33,13 @@
         self.core = lax.axis_index("dp")
         self.half = lax.axis_index("head")
         self.group = 2 * self.core + self.half
+
+    def near(self, k):
+        orders = [near_order(self.outer, line)[k] for line in range(self.outer)]
+        found = jnp.int32(orders[0])
+        for line in range(1, self.outer):
+            found = jnp.where(self.line == line, jnp.int32(orders[line]), found)
+        return found
 
     def at(self, line, side):
         return {"blk": line * self.inner + side}
@@ -91,6 +98,10 @@
                 tasks.remove(task)
 
 
+def near_order(outer, line):
+    return sorted(range(outer), key=lambda other: (abs(other - line), other))
+
+
 def gather_blk_sems(place_count):
     inner = 4 if place_count >= 32 else 2
     return [
@@ -100,82 +111,85 @@
     ]
 
 
-def gather_blk(place, src, out, sent, came, own):
-    outer, inner, line, side = place.outer, place.inner, place.line, place.side
-    copy = pltpu.make_async_copy(src, out.at[place.here], own)
-    copy.start()
-    finishing = []
-    is_below, is_above = line < outer - 1, line > 0
-
-    def spread(what, piece, up, down):
+class GatherBlk:
+    def __init__(self, place, src, view, sent, came, own):
+        self.place, self.src, self.view, self.sent, self.came = place, src, view, sent, came
+        self.copy = pltpu.make_async_copy(src, view(place.here), own)
+
+    def sends(self, k):
+        place = self.place
+        there = place.near(k)
+        piece = there * place.inner + place.side
+        src = self.src if k == 0 else self.view(piece)
+
         def send(kind, device):
-            return remote(what, out.at[piece], sent.at[kind, piece], came.at[piece], device)
-
-        if up is not None:
-            pl.when(up)(lambda: send(0, place.at(line + 1, side)).start())
-            finishing.append((up, lambda: send(0, place.at(line + 1, side)).wait_send()))
-        if down is not None:
-            pl.when(down)(lambda: send(1, place.at(line - 1, side)).start())
-            finishing.append((down, lambda: send(1, place.at(line - 1, side)).wait_send()))
-        for step in range(1, inner):
-            send(1 + step, place.at(line, place.beside(step))).start()
-            finishing.append(
-                (None, lambda step=step: send(1 + step, place.at(line, place.beside(step))).wait_send())
+            return remote(
+                src, self.view(piece), self.sent.at[kind, piece], self.came.at[piece], device
             )
 
-    def arrived(piece):
+        line, side = place.line, place.side
+        up = (there <= line) & (line < place.outer - 1)
+        down = (there >= line) & (line > 0)
+        return (
+            [
+                (up, lambda: send(0, place.at(line + 1, side))),
+                (down, lambda: send(1, place.at(line - 1, side))),
+            ],
+            [send(1 + step, place.at(line, place.beside(step))) for step in range(1, place.inner)],
+        )
+
+    def forward(self, k):
+        along, aside = self.sends(k)
+        for needed, make in along:
+            pl.when(needed)(lambda make=make: make().start())
+        for one in aside:
+            one.start()
+
+    def start(self):
+        self.copy.start()
+        self.forward(0)
+
+    def arrived(self, piece):
+        place = self.place
         remote(
-            src, out.at[piece], sent.at[0, piece], came.at[piece], place.at(line, place.beside(1))
+            self.src,
+            self.view(piece),
+            self.sent.at[0, piece],
+            self.came.at[piece],
+            place.at(place.line, place.beside(1)),
         ).wait_recv()
 
-    spread(src, place.here, is_below, is_above)
+    def pass_on(self, k):
+        self.arrived(self.place.near(k) * self.place.inner + self.place.side)
+        self.forward(k)
+
+    def beside_arrived(self, k):
+        for step in range(1, self.place.inner):
+            self.arrived(self.place.near(k) * self.place.inner + self.place.beside(step))
+
+    def finish(self):
+        for k in range(self.place.outer):
+            along, aside = self.sends(k)
+            for needed, make in along:
+                pl.when(needed)(lambda make=make: make().wait_send())
+            for one in aside:
+                one.wait_send()
+
+
+def gather_blk(place, src, view, sent, came, own):
+    if not callable(view):
+        out = view
+        view = lambda piece: out.at[piece]
+    work = GatherBlk(place, src, view, sent, came, own)
+    work.start()
     yield
-    ends = []
-    for away in range(1, outer):
-        for sign in (-1, 1):
-            there = line + sign * away
-            fits = (there >= 0) if sign < 0 else (there < outer)
-            piece = there * inner + side
-
-            @pl.when(fits)
-            def _(piece=piece, sign=sign):
-                arrived(piece)
-                mark = len(finishing)
-                if sign < 0:
-                    spread(out.at[piece], piece, is_below, None)
-                else:
-                    spread(out.at[piece], piece, None, is_above)
-                later = finishing[mark:]
-                del finishing[mark:]
-                ends.append(later)
-
+    for k in range(1, place.outer):
+        work.pass_on(k)
         yield
-
-    for there in range(outer):
-        for step in range(1, inner):
-            arrived(there * inner + place.beside(step))
-    for needed, finish in finishing:
-        if needed is None:
-            finish()
-        else:
-            pl.when(needed)(finish)
-    index = 0
-    for away in range(1, outer):
-        for sign in (-1, 1):
-            there = line + sign * away
-            fits = (there >= 0) if sign < 0 else (there < outer)
-            later = ends[index]
-            index += 1
-
-            @pl.when(fits)
-            def _(later=later):
-                for needed, finish in later:
-                    if needed is None:
-                        finish()
-                    else:
-                        pl.when(needed)(finish)
-
-    copy.wait()
+    for k in range(place.outer):
+        work.beside_arrived(k)
+    work.finish()
+    work.copy.wait()
 
 
 def add_into(out, *terms):
@@ -203,98 +217,122 @@
     ]
 
 
-def reduce_blk(place, part, out, beside, along, held, side_sent, side_came, line_sent, line_came):
-    outer, inner, line, side = place.outer, place.inner, place.line, place.side
-
-    def side_copy(there, step):
+class ReduceBlk:
+    def __init__(
+        self, place, view, out, beside, along, held, side_sent, side_came, line_sent, line_came
+    ):
+        self.place, self.view, self.out = place, view, out
+        self.beside, self.along, self.held = beside, along, held
+        self.side_sems, self.line_sems = (side_sent, side_came), (line_sent, line_came)
+
+    def far(self, k):
+        return self.place.near(self.place.outer - 1 - k)
+
+    def side_copy(self, there, step):
+        place = self.place
         to = place.beside(step)
         return remote(
-            part.at[there * inner + to],
-            beside.at[there, inner - step - 1],
-            side_sent.at[there, step - 1],
-            side_came.at[there, inner - step - 1],
-            place.at(line, to),
+            self.view(there * place.inner + to),
+            self.beside.at[there, place.inner - step - 1],
+            self.side_sems[0].at[there, step - 1],
+            self.side_sems[1].at[there, place.inner - step - 1],
+            place.at(place.line, to),
         )
 
-    def line_copy(there, slot, to):
+    def line_copy(self, there, slot, to):
         return remote(
-            held.at[there], along.at[slot], line_sent.at[there], line_came.at[slot], place.at(to, side)
+            self.held.at[there],
+            self.along.at[slot],
+            self.line_sems[0].at[there],
+            self.line_sems[1].at[slot],
+            self.place.at(to, self.place.side),
         )
 
-    def each(away, act):
-        for sign in (-1, 1) if away else (0,):
-            there = line + sign * away
-            if away == 0:
-                act(there, 0)
-            else:
-                fits = (there >= 0) if sign < 0 else (there < outer)
-                pl.when(fits)(functools.partial(act, there, sign))
-
-    def send_aside(there, sign):
-        for step in range(1, inner):
-            side_copy(there, step).start()
-
-    def side_terms(there):
-        for step in range(1, inner):
-            side_copy(there, step).wait_recv()
-        return [part.at[there * inner + side]] + [beside.at[there, k] for k in range(inner - 1)]
-
-    def pass_on(there, sign):
-        terms = side_terms(there)
-        starts = (line == outer - 1) if sign < 0 else (line == 0)
+    def send(self, k):
+        for step in range(1, self.place.inner):
+            self.side_copy(self.far(k), step).start()
+
+    def terms(self, there):
+        place = self.place
+        for step in range(1, place.inner):
+            self.side_copy(there, step).wait_recv()
+        own = self.view(there * place.inner + place.side)
+        return [own] + [self.beside.at[there, k] for k in range(place.inner - 1)]
+
+    def onward(self, there):
+        line, outer = self.place.line, self.place.outer
+        to = jnp.where(there < line, line - 1, line + 1)
+        slot = jnp.where(there == line + 1, outer, there)
+        return self.line_copy(there, slot, to)
+
+    def pass_on(self, k):
+        place = self.place
+        line, outer = place.line, place.outer
+        there = self.far(k)
+        terms = self.terms(there)
+        starts = ((there < line) & (line == outer - 1)) | ((there > line) & (line == 0))
 
         @pl.when(starts)
         def _():
-            add_into(held.at[there], *terms)
+            add_into(self.held.at[there], *terms)
 
         @pl.when(jnp.logical_not(starts))
         def _():
-            line_copy(there, there, line + sign).wait_recv()
-            add_into(held.at[there], along.at[there], *terms)
-
-        slot = there if sign < 0 else jnp.where(there == line + 1, outer, there)
-        line_copy(there, slot, line + sign).start()
-
-    for away in range(outer - 1, -1, -1):
-        each(away, send_aside)
+            back = jnp.where(there < line, line + 1, line - 1)
+            self.line_copy(there, there, back).wait_recv()
+            add_into(self.held.at[there], self.along.at[there], *terms)
+
+        self.onward(there).start()
+
+    def last(self):
+        place = self.place
+        line, outer = place.line, place.outer
+        terms = self.terms(line)
+        below, above = line > 0, line < outer - 1
+        from_above, from_below = self.along.at[line], self.along.at[outer]
+
+        @pl.when(above)
+        def _():
+            self.line_copy(line, line, line + 1).wait_recv()
+
+        @pl.when(below)
+        def _():
+            self.line_copy(line, outer, line - 1).wait_recv()
+
+        @pl.when(above & below)
+        def _():
+            add_into(self.out, from_above, from_below, *terms)
+
+        @pl.when(above & jnp.logical_not(below))
+        def _():
+            add_into(self.out, from_above, *terms)
+
+        @pl.when(jnp.logical_not(above) & below)
+        def _():
+            add_into(self.out, from_below, *terms)
+
+    def finish(self):
+        for k in range(self.place.outer):
+            if k < self.place.outer - 1:
+                self.onward(self.far(k)).wait_send()
+            for step in range(1, self.place.inner):
+                self.side_copy(self.far(k), step).wait_send()
+
+
+def reduce_blk(place, view, out, *scratch):
+    if not callable(view):
+        part = view
+        view = lambda piece: part.at[piece]
+    work = ReduceBlk(place, view, out, *scratch)
+    for k in range(place.outer):
+        work.send(k)
     yield
-    for away in range(outer - 1, 0, -1):
-        each(away, pass_on)
+    for k in range(place.outer - 1):
+        work.pass_on(k)
         yield
-    terms = side_terms(line)
-    below, above = line > 0, line < outer - 1
-    from_above, from_below = along.at[line], along.at[outer]
-
-    @pl.when(above)
-    def _():
-        line_copy(line, line, line + 1).wait_recv()
-
-    @pl.when(below)
-    def _():
-        line_copy(line, outer, line - 1).wait_recv()
-
-    @pl.when(above & below)
-    def _():
-        add_into(out, from_above, from_below, *terms)
-
-    @pl.when(above & jnp.logical_not(below))
-    def _():
-        add_into(out, from_above, *terms)
-
-    @pl.when(jnp.logical_not(above) & below)
-    def _():
-        add_into(out, from_below, *terms)
-
+    work.last()
     yield
-
-    def end_line(there, sign):
-        line_copy(there, there, line + sign).wait_send()
-
-    for away in range(outer - 1, 0, -1):
-        each(away, end_line)
-    for there in range(outer):
-        for step in range(1, inner):
-            side_copy(there, step).wait_send()
+    work.finish()
 
 
 def gather_group_sems():
@@ -607,6 +645,383 @@
     )[0]
 
 
+def dot(left, right, contract):
+    return lax.dot_general(left, right, (contract, ((), ())), preferred_element_type=jnp.float32)
+
+
+LAST = ((1,), (1,))
+PLAIN = ((1,), (0,))
+FIRST = ((0,), (0,))
+
+
+LANES = 128
+GELU_A = math.sqrt(2.0 / math.pi)
+GELU_B = 0.044715
+
+
+def feed_forward_fits(count, rows, width, hidden):
+    inner = 4 if count >= 32 else 2
+    outer = count // inner
+    tile = rows * width * 2
+    weights = 3 * hidden * width * 2
+    kept = count * rows * 3 * hidden * 2
+    total = weights + kept + tile * (3 * count + outer * (inner - 1) + 2 * outer + 1) + 9 * tile
+    total += 3 * LANES * (count * rows + 2 * width) * 2
+    return total < 58 * 2**20 and hidden % (3 * LANES) == 0 and width % 256 == 0
+
+
+def feed_forward_kernel(
+    count,
+    branch_ref,
+    token_ref,
+    cot_ref,
+    gain_ref,
+    gate_up_hbm,
+    down_hbm,
+    out_ref,
+    middle_grad_ref,
+    branch_grad_ref,
+    gain_grad_ref,
+    gate_up_grad_hbm,
+    down_grad_hbm,
+    w_gate_up,
+    w_down,
+    norm_all,
+    grad_all,
+    act,
+    hidden,
+    part,
+    middle,
+    norm_own,
+    grad_own,
+    total,
+    turned,
+    staged,
+    beside,
+    along,
+    held,
+    w_sems,
+    out_sems,
+    *sems,
+):
+    place = Place(count)
+    rows, width = norm_all.shape[1:]
+    units = hidden.shape[1]
+    chunks = units // LANES
+    inner, outer = place.inner, place.outer
+    slab = branch_ref.shape[1]
+    steps = rows // slab
+    columns = width // 256
+    pair = inner * rows
+    sems = list(sems)
+
+    def take(amount):
+        taken = sems[:amount]
+        del sems[:amount]
+        return taken
+
+    def weight_copies(i):
+        units_at = pl.ds(pl.multiple_of(i * LANES, LANES), LANES)
+        return [
+            pltpu.make_async_copy(
+                gate_up_hbm.at[units_at, pl.ds(0, width)],
+                w_gate_up.at[i, pl.ds(0, LANES)],
+                w_sems.at[3 * i],
+            ),
+            pltpu.make_async_copy(
+                gate_up_hbm.at[units_at, pl.ds(width, width)],
+                w_gate_up.at[i, pl.ds(LANES, LANES)],
+                w_sems.at[3 * i + 1],
+            ),
+            pltpu.make_async_copy(down_hbm.at[units_at], w_down.at[units_at], w_sems.at[3 * i + 2]),
+        ]
+
+    def start_weights(i, carry):
+        for copy in weight_copies(i):
+            copy.start()
+        return carry
+
+    def wait_weights(i, carry):
+        for copy in weight_copies(i):
+            copy.wait()
+        return carry
+
+    lax.fori_loop(0, chunks, start_weights, 0)
+
+    def scale_of(values):
+        return lax.rsqrt(jnp.mean(values * values, axis=-1, keepdims=True) + NORM_EPS)
+
+    def slab_rows(i):
+        return pl.ds(pl.multiple_of(i * slab, slab), slab)
+
+    def before(i, carry):
+        value = branch_ref[i]
+        mid = token_ref[i].astype(jnp.float32) + value * scale_of(value) * gain_ref[1:2]
+        middle[i] = mid
+        norm_own[slab_rows(i)] = (mid * scale_of(mid) * gain_ref[2:3]).astype(jnp.bfloat16)
+        return carry
+
+    lax.fori_loop(0, steps, before, 0)
+    greet(place, blk=True)
+
+    def pair_rows(k):
+        return pl.ds(pl.multiple_of(place.near(k) * pair, pair), pair)
+
+    def pair_pieces(k):
+        return pl.ds(place.near(k) * inner, inner)
+
+    def column(n):
+        return pl.ds(pl.multiple_of(n * 256, 256), 256)
+
+    def put_part(k, n, value):
+        split = value.astype(jnp.bfloat16).reshape((inner, steps, slab, 256))
+        part[pair_pieces(k), :, :, column(n)] = split
+
+    gather = GatherBlk(place, norm_own, lambda i: norm_all.at[i], *take(3))
+    gather.start()
+    lax.fori_loop(0, chunks, wait_weights, 0)
+    for k in range(outer):
+        if k == 0:
+            gather.copy.wait()
+        if k + 1 < outer:
+            gather.pass_on(k + 1)
+        gather.beside_arrived(k)
+        at = pair_rows(k)
+
+        def up_chunk(j, carry, k=k, at=at):
+            x = norm_all[pair_pieces(k)].reshape(pair, width)
+            both = dot(x, w_gate_up[j], LAST)
+            act[at, column(j)] = both.astype(jnp.bfloat16)
+            gate, up = both[:, :LANES], both[:, LANES:]
+            bent = 0.5 * gate * (1.0 + jnp.tanh(GELU_A * (gate + GELU_B * (gate * gate * gate))))
+            hidden[at, pl.ds(pl.multiple_of(j * LANES, LANES), LANES)] = (bent * up).astype(
+                jnp.bfloat16
+            )
+            return carry
+
+        lax.fori_loop(0, chunks, up_chunk, 0)
+
+        def down_chunk(n, carry, k=k, at=at):
+            put_part(k, n, dot(hidden[at, :], w_down[:, column(n)], PLAIN))
+            return carry
+
+        lax.fori_loop(0, columns, down_chunk, 0)
+    gather.finish()
+    reduce = ReduceBlk(place, lambda i: part.at[i], total, beside, along, held, *take(4))
+    for k in range(outer):
+        reduce.send(k)
+    for k in range(outer - 1):
+        reduce.pass_on(k)
+    reduce.last()
+
+    gain_grad_ref[...] = jnp.zeros_like(gain_grad_ref)
+
+    def norm_back(value, gain, incoming):
+        scale = scale_of(value)
+        lifted = incoming * gain
+        pull = jnp.mean(lifted * value, axis=-1, keepdims=True)
+        gain_grad = jnp.sum(incoming * value * scale, axis=0, keepdims=True)
+        return scale * lifted - value * (scale * scale * scale) * pull, gain_grad
+
+    def between(i, carry):
+        value, cot = total[i], cot_ref[i].astype(jnp.float32)
+        gain = gain_ref[3:4]
+        out_ref[i] = (middle[i] + value * scale_of(value) * gain).astype(jnp.bfloat16)
+        grad, gain_grad = norm_back(value, gain, cot)
+        gain_grad_ref[3:4] += gain_grad
+        grad_own[slab_rows(i)] = grad.astype(jnp.bfloat16)
+        return carry
+
+    lax.fori_loop(0, steps, between, 0)
+    reduce.finish()
+
+    gather = GatherBlk(place, grad_own, lambda i: grad_all.at[i], *take(3))
+    gather.start()
+    for k in range(outer):
+        if k == 0:
+            gather.copy.wait()
+        if k + 1 < outer:
+            gather.pass_on(k + 1)
+        gather.beside_arrived(k)
+        at = pair_rows(k)
+
+        def back_chunk(j, carry, k=k, at=at):
+            g = grad_all[pair_pieces(k)].reshape(pair, width)
+            units_at = pl.ds(pl.multiple_of(j * LANES, LANES), LANES)
+            grad = dot(g, w_down[units_at], LAST)
+            both = act[at, column(j)].astype(jnp.float32)
+            gate, up = both[:, :LANES], both[:, LANES:]
+            bend = jnp.tanh(GELU_A * (gate + GELU_B * (gate * gate * gate)))
+            bent = 0.5 * gate * (1.0 + bend)
+            slope = 0.5 * (1.0 + bend) + (0.5 * GELU_A) * gate * (1.0 - bend * bend) * (
+                1.0 + (3.0 * GELU_B) * gate * gate
+            )
+            pulled = jnp.concatenate([grad * up * slope, grad * bent], axis=1)
+            act[at, column(j)] = pulled.astype(jnp.bfloat16)
+            return carry
+
+        lax.fori_loop(0, chunks, back_chunk, 0)
+
+        def input_chunk(n, carry, k=k, at=at):
+            w = w_gate_up[:, :, column(n)].reshape(2 * units, 256)
+            put_part(k, n, dot(act[at, :], w, PLAIN))
+            return carry
+
+        lax.fori_loop(0, columns, input_chunk, 0)
+    gather.finish()
+    reduce = ReduceBlk(place, lambda i: part.at[i], total, beside, along, held, *take(4))
+    for k in range(outer):
+        reduce.send(k)
+
+    tokens = count * rows
+    slots = staged.shape[0]
+
+    def up_store(i):
+        slot = lax.rem(i, slots)
+        units_at = pl.ds(pl.multiple_of(i * LANES, LANES), LANES)
+        return [
+            pltpu.make_async_copy(
+                staged.at[slot, pl.ds(h * LANES, LANES)],
+                gate_up_grad_hbm.at[units_at, pl.ds(h * width, width)],
+                out_sems.at[slot, h],
+            )
+            for h in (0, 1)
+        ]
+
+    def up_grad(i, carry):
+        @pl.when(i >= slots)
+        def _():
+            for copy in up_store(i - slots):
+                copy.wait()
+
+        turned[pl.ds(0, 256)] = jnp.transpose(act[:, column(i)])
+
+        def one(n, c):
+            x = norm_all[:, :, column(n)].reshape(tokens, 256)
+            staged[lax.rem(i, slots), pl.ds(0, 256), column(n)] = dot(
+                turned[pl.ds(0, 256)], x, PLAIN
+            ).astype(jnp.bfloat16)
+            return c
+
+        lax.fori_loop(0, columns, one, 0)
+        for copy in up_store(i):
+            copy.start()
+        return carry
+
+    three = 3 * LANES
+
+    def down_store(i):
+        slot = lax.rem(i, slots)
+        return pltpu.make_async_copy(
+            staged.at[slot],
+            down_grad_hbm.at[pl.ds(pl.multiple_of(i * three, three), three)],
+            out_sems.at[slot, 2],
+        )
+
+    def down_grad(i, carry):
+        @pl.when(i >= slots)
+        def _():
+            down_store(i - slots).wait()
+
+        turned[...] = jnp.transpose(hidden[:, pl.ds(pl.multiple_of(i * three, three), three)])
+
+        def one(n, c):
+            x = grad_all[:, :, column(n)].reshape(tokens, 256)
+            staged[lax.rem(i, slots), :, column(n)] = dot(turned[...], x, PLAIN).astype(jnp.bfloat16)
+            return c
+
+        lax.fori_loop(0, columns, one, 0)
+        down_store(i).start()
+        return carry
+
+    bounds = [chunks * k // (outer - 1) for k in range(outer)]
+    for k in range(outer - 1):
+        lax.fori_loop(bounds[k], bounds[k + 1], up_grad, 0)
+        reduce.pass_on(k)
+    for i in range(max(0, chunks - slots), chunks):
+        for copy in up_store(i):
+            copy.wait()
+    thirds = units // three
+    lax.fori_loop(0, thirds, down_grad, 0)
+    reduce.last()
+
+    def after(i, carry):
+        value, mid, cot = branch_ref[i], middle[i], cot_ref[i].astype(jnp.float32)
+        grad, gain_grad = norm_back(mid, gain_ref[2:3], total[i])
+        gain_grad_ref[2:3] += gain_grad
+        middle_grad = cot + grad
+        middle_grad_ref[i] = middle_grad
+        grad, gain_grad = norm_back(value, gain_ref[1:2], middle_grad)
+        gain_grad_ref[1:2] += gain_grad
+        branch_grad_ref[i] = grad.astype(jnp.bfloat16)
+        return carry
+
+    lax.fori_loop(0, steps, after, 0)
+    reduce.finish()
+    for i in range(max(0, thirds - slots), thirds):
+        down_store(i).wait()
+
+
+def feed_forward(branch, tokens, cotangent, gains, gate_up_all, down_all, count, number):
+    steps, slab, width = branch.shape
+    rows = steps * slab
+    units = down_all.shape[0]
+    inner = 4 if count >= 32 else 2
+    outer = count // inner
+    piece = branch.shape
+    bf16, f32 = jnp.bfloat16, jnp.float32
+    vmem = pl.BlockSpec(memory_space=pltpu.VMEM)
+    anywhere = pl.BlockSpec(memory_space=pl.ANY)
+    slots = 2
+    line_scratch = reduce_blk_scratch(count, piece, bf16)
+    return pl.pallas_call(
+        functools.partial(feed_forward_kernel, count),
+        name="feed_forward",
+        out_shape=[
+            shape(piece, bf16),
+            shape(piece, f32),
+            shape(piece, bf16),
+            shape((4, width), f32),
+            shape(gate_up_all.shape, bf16),
+            shape(down_all.shape, bf16),
+        ],
+        in_specs=[vmem] * 4 + [anywhere] * 2,
+        out_specs=[vmem] * 4 + [anywhere] * 2,
+        scratch_shapes=[
+            pltpu.VMEM((units // LANES, 2 * LANES, width), bf16),
+            pltpu.VMEM((units, width), bf16),
+            pltpu.VMEM((count, rows, width), bf16),
+            pltpu.VMEM((count, rows, width), bf16),
+            pltpu.VMEM((count * rows, 2 * units), bf16),
+            pltpu.VMEM((count * rows, units), bf16),
+            pltpu.VMEM((count,) + piece, bf16),
+            pltpu.VMEM(piece, f32),
+            pltpu.VMEM((rows, width), bf16),
+            pltpu.VMEM((rows, width), bf16),
+            pltpu.VMEM(piece, f32),
+            pltpu.VMEM((3 * LANES, count * rows), bf16),
+            pltpu.VMEM((slots, 3 * LANES, width), bf16),
+        ]
+        + line_scratch[:3]
+        + [
+            pltpu.SemaphoreType.DMA((3 * units // LANES,)),
+            pltpu.SemaphoreType.DMA((slots, 3)),
+        ]
+        + gather_blk_sems(count)
+        + line_scratch[3:]
+        + gather_blk_sems(count)
+        + line_scratch[3:],
+        compiler_params=pltpu.CompilerParams(
+            collective_id=number, has_side_effects=True, vmem_limit_bytes=67043328
+        ),
+        cost_estimate=pl.CostEstimate(
+            flops=18 * count * rows * units * width,
+            bytes_accessed=500 * 2**20,
+            transcendentals=0,
+        ),
+    )(branch, tokens, cotangent, gains, gate_up_all, down_all)
+
+
 def attention_scores(q2, k, query_pos, query_doc, key_block, key_doc, rows):
     raw = lax.dot_general(q2, k, (((1,), (1,)), ((), ())), preferred_element_type=jnp.float32)
     capped = jnp.tanh(raw * (SCORE_SCALE / SOFT_CAP))
@@ -812,13 +1227,55 @@
     return values * cosine + turned * sine
 
 
-def dot(left, right, contract):
-    return lax.dot_general(left, right, (contract, ((), ())), preferred_element_type=jnp.float32)
-
-
-LAST = ((1,), (1,))
-PLAIN = ((1,), (0,))
-FIRST = ((0,), (0,))
+def feed_forward_apart(
+    branch_slabs, inputs, cotangent, gains, gate_up_all, down_all, count, piece
+):
+    rows, width = inputs.shape
+    bf16 = jnp.bfloat16
+    branch = branch_slabs.reshape(rows, width)
+    middle = inputs + rms_scale(branch, gains[1])
+    norm_three = rms_scale(middle, gains[2]).astype(bf16)
+    gate_all = gate_up_all[:, :width]
+    up_all = gate_up_all[:, width:]
+    norm_all = all_gather_blk(norm_three, count, 4).reshape(count * rows, width)
+    gate = dot(norm_all, gate_all, LAST)
+    up = dot(norm_all, up_all, LAST)
+    hidden = (gelu_tanh(gate) * up).astype(bf16)
+    ffn_part = dot(hidden, down_all, PLAIN).astype(bf16)
+    ffn_out = reduce_scatter_blk(ffn_part.reshape((count,) + piece), count, 5).reshape(rows, width)
+    output = (middle + rms_scale(ffn_out, gains[3])).astype(bf16)[None]
+
+    out_cotangent = cotangent[0].astype(jnp.float32)
+    _, post_ffn_back = jax.vjp(rms_scale, ffn_out, gains[3])
+    ffn_grad, gain_grad_four = post_ffn_back(out_cotangent)
+    grad_all = all_gather_blk(ffn_grad.astype(bf16), count, 6).reshape(count * rows, width)
+    activated, gelu_back = jax.vjp(gelu_tanh, gate)
+    hidden_grad = dot(grad_all, down_all, LAST)
+    gate_grad = gelu_back(hidden_grad * up)[0].astype(bf16)
+    up_grad = (hidden_grad * activated).astype(bf16)
+    norm_part = dot(gate_grad, gate_all, PLAIN) + dot(up_grad, up_all, PLAIN)
+    norm_three_grad = reduce_scatter_blk(
+        norm_part.astype(bf16).reshape((count,) + piece), count, 7
+    ).reshape(rows, width)
+    down_part = dot(hidden, grad_all, FIRST).astype(bf16)
+    gate_up_part = jnp.concatenate(
+        [dot(gate_grad, norm_all, FIRST), dot(up_grad, norm_all, FIRST)], axis=1
+    ).astype(bf16)
+    _, pre_ffn_back = jax.vjp(rms_scale, middle, gains[2])
+    middle_part, gain_grad_three = pre_ffn_back(norm_three_grad)
+    middle_grad = out_cotangent + middle_part
+    _, post_attn_back = jax.vjp(rms_scale, branch, gains[1])
+    branch_grad, gain_grad_two = post_attn_back(middle_grad)
+    return (
+        output,
+        middle_grad,
+        branch_grad.astype(bf16),
+        gain_grad_two,
+        gain_grad_three,
+        gain_grad_four,
+        gate_up_part,
+        down_part,
+    )
 
 
 def shards(
@@ -876,50 +1333,43 @@
     attn, attended, totals = attention_forward(here_one, queries, kv, own_doc, key_doc)
     attn = attn.reshape(group_rows, head_width)
     branch_part = dot(attn, out_head, LAST).astype(bf16)
-    branch = reduce_scatter_group(branch_part.reshape((GROUPS,) + piece), 3).reshape(rows, width)
+    branch_slabs = reduce_scatter_group(branch_part.reshape((GROUPS,) + piece), 3)
     inputs = tokens[0].astype(jnp.float32)
-    middle = inputs + rms_scale(branch, gains[1])
-    norm_three = rms_scale(middle, gains[2]).astype(bf16)
-
-    gate_all = gate_up_all[:, :width]
-    up_all = gate_up_all[:, width:]
-    norm_all = all_gather_blk(norm_three, count, 4).reshape(count * rows, width)
-    gate = dot(norm_all, gate_all, LAST)
-    up = dot(norm_all, up_all, LAST)
-    hidden = (gelu_tanh(gate) * up).astype(bf16)
-    ffn_part = dot(hidden, down_all, PLAIN).astype(bf16)
-    ffn_out = reduce_scatter_blk(ffn_part.reshape((count,) + piece), count, 5).reshape(rows, width)
-    output = (middle + rms_scale(ffn_out, gains[3])).astype(bf16)[None]
-
-    out_cotangent = cotangent[0].astype(jnp.float32)
-    _, post_ffn_back = jax.vjp(rms_scale, ffn_out, gains[3])
-    ffn_grad, gain_grad_four = post_ffn_back(out_cotangent)
-    grad_all = all_gather_blk(ffn_grad.astype(bf16), count, 6).reshape(count * rows, width)
-    activated, gelu_back = jax.vjp(gelu_tanh, gate)
-    hidden_grad = dot(grad_all, down_all, LAST)
-    gate_grad = gelu_back(hidden_grad * up)[0].astype(bf16)
-    up_grad = (hidden_grad * activated).astype(bf16)
-    norm_part = dot(gate_grad, gate_all, PLAIN) + dot(up_grad, up_all, PLAIN)
-    norm_three_grad = reduce_scatter_blk(
-        norm_part.astype(bf16).reshape((count,) + piece), count, 7
-    ).reshape(rows, width)
-    down_part = dot(hidden, grad_all, FIRST).astype(bf16)
-    gate_up_part = jnp.concatenate(
-        [dot(gate_grad, norm_all, FIRST), dot(up_grad, norm_all, FIRST)], axis=1
-    ).astype(bf16)
+    if feed_forward_fits(count, rows, width, down_all.shape[0]):
+        output, middle_grad, branch_grad, gain_rest, gate_up_part, down_part = feed_forward(
+            branch_slabs,
+            tokens.reshape(piece),
+            cotangent.reshape(piece),
+            gains,
+            gate_up_all,
+            down_all,
+            count,
+            4,
+        )
+        output = output.reshape(tokens.shape)
+        middle_grad = middle_grad.reshape(rows, width)
+        branch_grad = branch_grad.reshape(rows, width)
+        gain_grad_two, gain_grad_three, gain_grad_four = gain_rest[1], gain_rest[2], gain_rest[3]
+    else:
+        (
+            output,
+            middle_grad,
+            branch_grad,
+            gain_grad_two,
+            gain_grad_three,
+            gain_grad_four,
+            gate_up_part,
+            down_part,
+        ) = feed_forward_apart(
+            branch_slabs, inputs, cotangent, gains, gate_up_all, down_all, count, piece
+        )
     gate_up_grad = lax.psum_scatter(
         gate_up_part, ("dp", "head"), scatter_dimension=0, tiled=True
     ).astype(jnp.float32)
     down_grad = lax.psum_scatter(
         down_part, ("dp", "head"), scatter_dimension=0, tiled=True
     ).astype(jnp.float32)
-
-    _, pre_ffn_back = jax.vjp(rms_scale, middle, gains[2])
-    middle_part, gain_grad_three = pre_ffn_back(norm_three_grad)
-    middle_grad = out_cotangent + middle_part
-    _, post_attn_back = jax.vjp(rms_scale, branch, gains[1])
-    branch_grad, gain_grad_two = post_attn_back(middle_grad)
-    branch_all = all_gather_group(branch_grad.astype(bf16), 8).reshape(group_rows, width)
+    branch_all = all_gather_group(branch_grad, 8).reshape(group_rows, width)
     attn_grad = dot(branch_all, out_head, PLAIN).astype(bf16).reshape(GROUPS, rows, head_width)
     out_part = dot(branch_all, attn, FIRST).astype(bf16)
     out_part = jnp.transpose(out_part.reshape(GROUPS, count, out_rows, head_width), (1, 0, 2, 3))

time: 845 us -> 719 us (0.85)
  matrix products: 122 us -> 24.3 us
  other arithmetic: 52.3 us -> 18.1 us
  Pallas kernels: 600 us -> 633 us
  local copies, waits for them, and re-layouts: 44.3 us -> 22.7 us
    pallas_call x0 -> x1, Pallas kernels: none -> 258 us  [feed_forward(): pl.pallas_call(functools.partial(feed_forward_kernel, count), name='feed_...]
    pallas_call x10 -> x6, Pallas kernels: 566 us -> 341 us  [transfer(): pl.pallas_call(body, name=name, out_shape=outs, in_specs=[pl.BlockSpec(me...]
    dot_general x15 -> x6, matrix products: 122 us -> 24.3 us  [dot(): lax.dot_general(left, right, (contract, ((), ())), preferred_element_type...]
    another operation x8 -> x4, local copies, waits for them, and re-layouts: 10.3 us -> 0.24 us  [shards(): jnp.stack([gain_grad_one, gain_grad_two, gain_grad_three, gain_grad_four])]
    reduce_sum x5 -> x2, other arithmetic: 9.54 us -> 0.85 us  [rms_scale(): jnp.mean(values * values, axis=-1, keepdims=True) + NORM_EPS]
  transfers between devices with their start and end apart: 4 -> 4, of which waited for: 0 -> 0; matrix products, arithmetic and copies ran while one was open for 21% -> 7% of each run, Pallas kernels for 59% -> 52%
where the time goes in v2:
time: 719 us; the launch traced here: 714 us
  Pallas kernels  633 us (88%)
  matrix products  24.3 us (3%)
  local copies, waits for them, and re-layouts  22.7 us (3%)
  other arithmetic  18.1 us (3%)
  between operations  14.3 us (2%)
    pallas_call x6, Pallas kernels, transfer(): pl.pallas_call(body, name=name, out_shape=outs, in_specs=[pl.BlockSpec(me...  341 us
    pallas_call x1, Pallas kernels, feed_forward(): pl.pallas_call(functools.partial(feed_forward_kernel, count), name='feed_...  258 us
    dot_general x6, matrix products, dot(): lax.dot_general(left, right, (contract, ((), ())), preferred_element_type...  24.3 us
    pallas_call x1, Pallas kernels, attention_backward(): pl.pallas_call(functools.partial(attention_backward_kernel, count), name=...  19.7 us
  transfers between devices with their start and end apart: 4, of which 0 were waited for; matrix products, arithmetic and copies ran while one was open for 7% of the time, Pallas kernels for 52%

profile of v2, /device:TPU:20, one launch (start us, length us, event | category | flops | bytes accessed | tf_op | source)
XLA Modules:
  0.0 714.4 jit_solution(6516636673850512665)
XLA Ops:
  10.1 87.8 %first1.1 = (bf16[8,128,2304]{2,1,0:T(8,128)(2,1)}, bf16[8,4,72,512]{3,2,1,0:T(8,128)(2,1)}, bf16[4,128,2304]{2,1,0:T(8,128)(2,1)}, f32[4,8,8,128]{3,2,1,0:T(8,128)}, s32[2,16,128]{2,1,0:T(8,128)}) custom-call(bf16[128,2304]{1,0:T(8,128)(2,1)} %refs_0_.1, bf16[4,72,512]{2,1,0:T(8,128)(2,1)} %bitcast.119, bf16[128,2304]{1,0:T(8,128)(2,1)} %bitcast.102, ...), custom_call_target="tpu_custom_call" | custom-call | bytes 283115520 | tf_op jit(solution)/shard_map/first1/pallas_call | solution.py:425
  97.9 3.4 copy.28
  105.6 2.6 copy-done.24
  108.1 2.6 fusion.15
  116.0 50.3 %gather2.1 = bf16[8,512,512]{2,1,0:T(8,128)(2,1)} custom-call(bf16[512,512]{1,0:T(8,128)(2,1)} %copy.41.src), custom_call_target="tpu_custom_call" | custom-call | bytes 167772160 | tf_op jit(solution)/shard_map/gather2/pallas_call | solution.py:425
  166.3 13.9 %attend.1 = (bf16[4,128,512]{2,1,0:T(8,128)(2,1)}, f32[4,128,512]{2,1,0:T(8,128)}, f32[4,256,1]{2,1,0:T(8,128)}) custom-call(s32[1]{0:T(128)} %bitcast.here_ref, bf16[4,128,512]{2,1,0:T(8,128)(2,1)} %copy.40.q_ref, bf16[8,4,128,512]{3,2,1,0:T(8,128)(2,1)} %bitcast.99, s32[4,128,1]{2,1,0:T(8,128)} %copy.27.doc_ref, s32[2,16,1,128]{3,2,1,0:T(1,128)} %bitcast.127), custom_call_target="tpu_custom_call" | custom-call | flops 1000000000 | bytes 41943040 | tf_op jit(solution)/shard_map/attend/pallas_call | solution.py:1157
  180.3 3.9 convolution_convert_fusion.1
  184.1 21.5 %fold3.1.branch_ref = f32[8,16,2304]{2,1,0:T(8,128)} custom-call(bf16[4,8,16,2304]{3,2,1,0:T(8,128)(2,1)} %bitcast.114), custom_call_target="tpu_custom_call" | custom-call | bytes 94371840 | tf_op jit(solution)/shard_map/fold3/pallas_call | solution.py:425
  205.7 258.3 %feed_forward.1 = (bf16[8,16,2304]{2,1,0:T(8,128)(2,1)}, f32[8,16,2304]{2,1,0:T(8,128)}, bf16[8,16,2304]{2,1,0:T(8,128)(2,1)}, f32[4,2304]{1,0:T(4,128)}, bf16[1...) custom-call(f32[8,16,2304]{2,1,0:T(8,128)} %fold3.1.branch_ref, bf16[8,16,2304]{2,1,0:T(8,128)(2,1)} %bitcast.103, ...), custom_call_target="tpu_custom_call" | custom-call | flops 48922361856 | bytes 524288000 | tf_op jit(solution)/shard_map/feed_forward/pallas_call | solution.py:977
  465.0 23.9 %group8.1 = bf16[4,128,2304]{2,1,0:T(8,128)(2,1)} custom-call(bf16[128,2304]{1,0:T(8,128)(2,1)} %bitcast.124), custom_call_target="tpu_custom_call" | custom-call | bytes 94371840 | tf_op jit(solution)/shard_map/group8/pallas_call | solution.py:425
  488.9 4.3 convolution_convert_fusion.2
  493.3 19.7 %attend_back.1 = (bf16[4,128,512]{2,1,0:T(8,128)(2,1)}, bf16[8,4,128,512]{3,2,1,0:T(8,128)(2,1)}) custom-call(s32[1]{0:T(128)} %bitcast.here_ref, bf16[4,128,512]{2,1,0:T(8,128)(2,1)} %copy.40.q_ref, bf16[8,4,128,512]{3,2,1,0:T(8,128)(2,1)} %bitcast.100, s32[4,128,1]{2,1,0:T(8,128)} %copy.27.doc_ref, s32[2,16,1,128]{3,2,1,0:T(1,128)} %bitcast.128, ...), custom_call_target="tpu_custom_call" | custom-call | flops 2000000000 | bytes 83886080 | tf_op jit(solution)/shard_map/attend_back/pallas_call | solution.py:1184
  513.0 1.2 reshape.328
  514.9 51.8 %reduce9.1 = f32[32,16,512]{2,1,0:T(8,128)} custom-call(bf16[8,32,16,512]{3,2,1,0:T(8,128)(2,1)} %bitcast.106), custom_call_target="tpu_custom_call" | custom-call | bytes 167772160 | tf_op jit(solution)/shard_map/reduce9/pallas_call | solution.py:425
  566.7 1.3 convert_element_type.102
  572.1 6.8 fusion.1
  579.1 2.5 fusion.2
  581.5 1.6 copy.47
  584.0 4.2 convolution_convert_fusion
  588.2 105.6 %last10.1 = (f32[8,16,2304]{2,1,0:T(8,128)}, bf16[4,72,512]{2,1,0:T(8,128)(2,1)}, f32[8,16,2304]{2,1,0:T(8,128)}, f32[1,8,128]{2,1,0:T(8,128)}) custom-call(bf16[8,8,16,2304]{3,2,1,0:T(8,128)(2,1)} %bitcast.105, bf16[8,4,72,512]{3,2,1,0:T(8,128)(2,1)} %bitcast.101, bf16[4,8,16,2304]{3,2,1,0:T(8,128)(2,1)} %bitcast.115, ...), custom_call_target="tpu_custom_call" | custom-call | bytes 283115520 | tf_op jit(solution)/shard_map/last10/pallas_call | solution.py:425
  693.9 1.2 convert_bitcast_fusion
  696.8 1.2 fusion.10
  698.1 3.0 convert_element_type.117
  701.1 4.9 convert_element_type.116
  (108 shorter events, 22.5 us)
Async XLA Ops:
  7.2 2.3 copy-start.22
  7.2 198.4 %all-gather.5.cloned.1.call-start = ((), (), s32[]{:S(2)}) async-start(), calls=%async_computation.3 | async-start | bytes 6635520 | tf_op jit(solution)/shard_map/all_gather | solution.py:1295
  7.9 197.7 %all-gather.3.cloned.1.call-start = ((), (), s32[]{:S(2)}) async-start(), calls=%async_computation.2 | async-start | bytes 13271040 | tf_op jit(solution)/shard_map/all_gather | solution.py:1294
  8.7 689.4 %reduce-scatter.5.cloned.1.call-start = ((), (), s32[]{:S(2)}) async-start(), calls=%async_computation.5 | async-start | bytes 6635520 | tf_op jit(solution)/shard_map/reduce_scatter | solution.py:1369
  97.9 3.5 copy-start.20
  97.9 5.9 copy-start
  101.5 4.0 copy-start.17
  104.9 3.2 copy-start.24
  105.5 5.2 copy-start.7
  111.9 1.8 copy-start.3
  166.3 14.0 %copy-start.9 = (bf16[4,8,72,512]{3,2,1,0:T(8,128)(2,1)S(1)}, bf16[4,8,72,512]{3,2,1,0:T(8,128)(2,1)}, u32[]{:S(2)}) copy-start(bf16[4,8,72,512]{3,2,1,0:T(8,128)(2,1)} %copy.28) | copy-start | bytes 7077892
  464.0 237.1 %reduce-scatter.3.cloned.1.call-start = ((), (), s32[]{:S(2)}) async-start(), calls=%async_computation.4 | async-start | bytes 13271040 | tf_op jit(solution)/shard_map/reduce_scatter | solution.py:1366
  464.6 24.4 %copy-start.10 = (bf16[4,8,72,512]{3,2,1,0:T(8,128)(2,1)S(1)}, bf16[4,8,72,512]{3,2,1,0:T(8,128)(2,1)}, u32[]{:S(2)}) copy-start(bf16[4,8,72,512]{3,2,1,0:T(8,128)(2,1)} %copy.28) | copy-start | bytes 7077892
  570.4 1.8 copy-start.1
  570.4 1.8 copy-start.21
  572.1 6.9 copy-start.11
  581.5 2.5 copy-start.8
  588.2 107.7 %copy-start.18 = (f32[2304]{0:T(1024)S(1)}, f32[2304]{0:T(1024)}, u32[]{:S(2)}) copy-start(f32[2304]{0:T(1024)} %copy-done.17) | copy-start | bytes 27652
  693.8 2.1 copy-start.2
  693.8 2.1 copy-start.5
  693.8 2.4 copy-start.23
  693.9 3.0 copy-start.13
  701.1 4.9 copy-start.15
  701.1 5.7 copy-start.14
  (6 other events, 6.4 us)
Sparse Core Ops, SparseCore 0:
  9.6 51.1 all-gather.4
  62.3 71.7 all-gather.2
  464.1 56.7 reduce-scatter.4
  523.4 92.3 reduce-scatter.2

commit v3 on v2

--- a/solution.py
+++ b/solution.py
@@ -99,14 +99,29 @@
 
 
 def near_order(outer, line):
-    return sorted(range(outer), key=lambda other: (abs(other - line), other))
-
-
-def gather_blk_sems(place_count):
+    ends = outer == 4
+    return sorted(
+        range(outer),
+        key=lambda other: (abs(other - line), ends and other not in (0, outer - 1), other),
+    )
+
+
+def evened(place, parts):
+    return parts == 2 and place.inner == 2 and place.outer == 4
+
+
+def part_of(ref, h, parts):
+    if parts == 1:
+        return ref
+    size = ref.shape[0] // parts
+    return ref.at[pl.ds(h * size, size)]
+
+
+def gather_blk_sems(place_count, parts=2):
     inner = 4 if place_count >= 32 else 2
     return [
-        pltpu.SemaphoreType.DMA((1 + inner, place_count)),
-        pltpu.SemaphoreType.DMA((place_count,)),
+        pltpu.SemaphoreType.DMA((2 + inner, place_count, parts)),
+        pltpu.SemaphoreType.DMA((place_count, parts)),
         pltpu.SemaphoreType.DMA,
     ]
 
@@ -114,32 +129,39 @@
 class GatherBlk:
     def __init__(self, place, src, view, sent, came, own):
         self.place, self.src, self.view, self.sent, self.came = place, src, view, sent, came
+        self.parts = came.shape[1]
+        self.evened = evened(place, self.parts)
+        self.middle = (place.line > 0) & (place.line < place.outer - 1)
         self.copy = pltpu.make_async_copy(src, view(place.here), own)
 
-    def sends(self, k):
+    def sends(self, k, h):
         place = self.place
         there = place.near(k)
         piece = there * place.inner + place.side
-        src = self.src if k == 0 else self.view(piece)
+        there_view = part_of(self.view(piece), h, self.parts)
+        src = part_of(self.src, h, self.parts) if k == 0 else there_view
 
         def send(kind, device):
             return remote(
-                src, self.view(piece), self.sent.at[kind, piece], self.came.at[piece], device
+                src, there_view, self.sent.at[kind, piece, h], self.came.at[piece, h], device
             )
 
         line, side = place.line, place.side
         up = (there <= line) & (line < place.outer - 1)
         down = (there >= line) & (line > 0)
+        aside = range(1, place.inner)
+        if self.evened and h == 1 and k == place.outer - 1:
+            aside = ()
         return (
             [
                 (up, lambda: send(0, place.at(line + 1, side))),
                 (down, lambda: send(1, place.at(line - 1, side))),
             ],
-            [send(1 + step, place.at(line, place.beside(step))) for step in range(1, place.inner)],
-        )
-
-    def forward(self, k):
-        along, aside = self.sends(k)
+            [send(1 + step, place.at(line, place.beside(step))) for step in aside],
+        )
+
+    def forward(self, k, h):
+        along, aside = self.sends(k, h)
         for needed, make in along:
             pl.when(needed)(lambda make=make: make().start())
         for one in aside:
@@ -147,33 +169,68 @@
 
     def start(self):
         self.copy.start()
-        self.forward(0)
-
-    def arrived(self, piece):
+        for h in range(self.parts):
+            self.forward(0, h)
+
+    def arrived(self, piece, h):
         place = self.place
         remote(
-            self.src,
-            self.view(piece),
-            self.sent.at[0, piece],
-            self.came.at[piece],
+            part_of(self.src, h, self.parts),
+            part_of(self.view(piece), h, self.parts),
+            self.sent.at[0, piece, h],
+            self.came.at[piece, h],
             place.at(place.line, place.beside(1)),
         ).wait_recv()
 
     def pass_on(self, k):
-        self.arrived(self.place.near(k) * self.place.inner + self.place.side)
-        self.forward(k)
+        for h in range(self.parts):
+            self.arrived(self.place.near(k) * self.place.inner + self.place.side, h)
+            self.forward(k, h)
+
+    def extra(self, k):
+        place = self.place
+        piece = place.near(k) * place.inner + place.beside(1)
+        to = place.near(2 if k == 1 else 1)
+        half = part_of(self.view(piece), 1, 2)
+        return remote(
+            half,
+            half,
+            self.sent.at[place.inner + 1, piece, 1],
+            self.came.at[piece, 1],
+            place.at(to, place.side),
+        )
+
+    def pass_extra(self, k):
+        if self.evened:
+
+            @pl.when(self.middle)
+            def _():
+                self.arrived(self.place.near(k) * self.place.inner + self.place.beside(1), 1)
+                self.extra(k).start()
 
     def beside_arrived(self, k):
         for step in range(1, self.place.inner):
-            self.arrived(self.place.near(k) * self.place.inner + self.place.beside(step))
+            piece = self.place.near(k) * self.place.inner + self.place.beside(step)
+            for h in range(self.parts):
+                if self.evened and h == 1 and k in (1, self.place.outer - 1):
+                    pl.when(jnp.logical_not(self.middle))(lambda: self.arrived(piece, 1))
+                else:
+                    self.arrived(piece, h)
 
     def finish(self):
         for k in range(self.place.outer):
-            along, aside = self.sends(k)
-            for needed, make in along:
-                pl.when(needed)(lambda make=make: make().wait_send())
-            for one in aside:
-                one.wait_send()
+            for h in range(self.parts):
+                along, aside = self.sends(k, h)
+                for needed, make in along:
+                    pl.when(needed)(lambda make=make: make().wait_send())
+                for one in aside:
+                    one.wait_send()
+        if self.evened:
+
+            @pl.when(self.middle)
+            def _():
+                self.extra(1).wait_send()
+                self.extra(self.place.outer - 1).wait_send()
 
 
 def gather_blk(place, src, view, sent, came, own):
@@ -185,7 +242,11 @@
     yield
     for k in range(1, place.outer):
         work.pass_on(k)
+        if k == place.outer - 2:
+            work.pass_extra(1)
         yield
+    work.pass_extra(place.outer - 1)
+    yield
     for k in range(place.outer):
         work.beside_arrived(k)
     work.finish()
@@ -203,120 +264,249 @@
     lax.fori_loop(0, out.shape[0], one, 0)
 
 
-def reduce_blk_scratch(place_count, piece, dtype):
+def reduce_blk_scratch(place_count, piece, dtype, parts=2):
     inner = 4 if place_count >= 32 else 2
     outer = place_count // inner
+    half = (piece[0] // 2,) + tuple(piece[1:]) if parts == 2 and inner == 2 and outer == 4 else (1, 8, 128)
     return [
         pltpu.VMEM((outer, inner - 1) + piece, dtype),
         pltpu.VMEM((outer + 1,) + piece, dtype),
         pltpu.VMEM((outer,) + piece, dtype),
-        pltpu.SemaphoreType.DMA((outer, inner - 1)),
-        pltpu.SemaphoreType.DMA((outer, inner - 1)),
-        pltpu.SemaphoreType.DMA((outer,)),
-        pltpu.SemaphoreType.DMA((outer + 1,)),
+        pltpu.VMEM((4,) + half, dtype),
+        pltpu.SemaphoreType.DMA((outer, inner - 1, parts)),
+        pltpu.SemaphoreType.DMA((outer, inner - 1, parts)),
+        pltpu.SemaphoreType.DMA((outer, parts)),
+        pltpu.SemaphoreType.DMA((outer + 1, parts)),
+        pltpu.SemaphoreType.DMA((2,)),
+        pltpu.SemaphoreType.DMA((2,)),
     ]
+
+
+REDUCE_REFS = 10
 
 
 class ReduceBlk:
     def __init__(
-        self, place, view, out, beside, along, held, side_sent, side_came, line_sent, line_came
+        self,
+        place,
+        view,
+        out,
+        beside,
+        along,
+        held,
+        spare,
+        side_sent,
+        side_came,
+        line_sent,
+        line_came,
+        spare_sent,
+        spare_came,
     ):
         self.place, self.view, self.out = place, view, out
-        self.beside, self.along, self.held = beside, along, held
+        self.beside, self.along, self.held, self.spare = beside, along, held, spare
         self.side_sems, self.line_sems = (side_sent, side_came), (line_sent, line_came)
+        self.spare_sems = (spare_sent, spare_came)
+        self.parts = line_sent.shape[1]
+        self.evened = evened(place, self.parts)
+        self.middle = (place.line > 0) & (place.line < place.outer - 1)
+
+    def part(self, ref, h):
+        return part_of(ref, h, self.parts)
 
     def far(self, k):
         return self.place.near(self.place.outer - 1 - k)
 
-    def side_copy(self, there, step):
+    def alone(self, k, h):
+        return self.evened and k == 0 and h == 1
+
+    def side_copy(self, there, step, h, src=None):
         place = self.place
         to = place.beside(step)
+        if src is None:
+            src = self.part(self.view(there * place.inner + to), h)
         return remote(
-            self.view(there * place.inner + to),
-            self.beside.at[there, place.inner - step - 1],
-            self.side_sems[0].at[there, step - 1],
-            self.side_sems[1].at[there, place.inner - step - 1],
+            src,
+            self.part(self.beside.at[there, place.inner - step - 1], h),
+            self.side_sems[0].at[there, step - 1, h],
+            self.side_sems[1].at[there, place.inner - step - 1, h],
             place.at(place.line, to),
         )
 
-    def line_copy(self, there, slot, to):
+    def line_copy(self, there, slot, to, h, src=None):
         return remote(
-            self.held.at[there],
-            self.along.at[slot],
-            self.line_sems[0].at[there],
-            self.line_sems[1].at[slot],
+            self.part(self.held.at[there], h) if src is None else src,
+            self.part(self.along.at[slot], h),
+            self.line_sems[0].at[there, h],
+            self.line_sems[1].at[slot, h],
             self.place.at(to, self.place.side),
         )
 
-    def send(self, k):
+    def send(self, k, h):
         for step in range(1, self.place.inner):
-            self.side_copy(self.far(k), step).start()
-
-    def terms(self, there):
+            self.side_copy(self.far(k), step, h).start()
+
+    def terms(self, k, h):
         place = self.place
+        there = self.far(k)
+        own = [self.part(self.view(there * place.inner + place.side), h)]
+        if self.alone(k, h):
+            return own
         for step in range(1, place.inner):
-            self.side_copy(there, step).wait_recv()
-        own = self.view(there * place.inner + place.side)
-        return [own] + [self.beside.at[there, k] for k in range(place.inner - 1)]
-
-    def onward(self, there):
+            self.side_copy(there, step, h).wait_recv()
+        return own + [self.part(self.beside.at[there, j], h) for j in range(place.inner - 1)]
+
+    def onward(self, there, h, src=None):
         line, outer = self.place.line, self.place.outer
         to = jnp.where(there < line, line - 1, line + 1)
         slot = jnp.where(there == line + 1, outer, there)
-        return self.line_copy(there, slot, to)
-
-    def pass_on(self, k):
+        return self.line_copy(there, slot, to, h, src)
+
+    def starts(self, there):
+        line, outer = self.place.line, self.place.outer
+        return ((there < line) & (line == outer - 1)) | ((there > line) & (line == 0))
+
+    def pass_on(self, k, h):
         place = self.place
-        line, outer = place.line, place.outer
+        line = place.line
         there = self.far(k)
-        terms = self.terms(there)
-        starts = ((there < line) & (line == outer - 1)) | ((there > line) & (line == 0))
+        terms = self.terms(k, h)
+        held = self.part(self.held.at[there], h)
+        starts = self.starts(there)
 
         @pl.when(starts)
         def _():
-            add_into(self.held.at[there], *terms)
+            add_into(held, *terms)
 
         @pl.when(jnp.logical_not(starts))
         def _():
             back = jnp.where(there < line, line + 1, line - 1)
-            self.line_copy(there, there, back).wait_recv()
-            add_into(self.held.at[there], self.along.at[there], *terms)
-
-        self.onward(there).start()
-
-    def last(self):
+            self.line_copy(there, there, back, h).wait_recv()
+            add_into(held, self.part(self.along.at[there], h), *terms)
+
+        self.onward(there, h).start()
+
+    def last(self, h):
         place = self.place
         line, outer = place.line, place.outer
-        terms = self.terms(line)
+        terms = self.terms(outer - 1, h)
         below, above = line > 0, line < outer - 1
-        from_above, from_below = self.along.at[line], self.along.at[outer]
+        from_above = self.part(self.along.at[line], h)
+        from_below = self.part(self.along.at[outer], h)
+        out = self.part(self.out, h)
 
         @pl.when(above)
         def _():
-            self.line_copy(line, line, line + 1).wait_recv()
+            self.line_copy(line, line, line + 1, h).wait_recv()
 
         @pl.when(below)
         def _():
-            self.line_copy(line, outer, line - 1).wait_recv()
+            self.line_copy(line, outer, line - 1, h).wait_recv()
 
         @pl.when(above & below)
         def _():
-            add_into(self.out, from_above, from_below, *terms)
+            add_into(out, from_above, from_below, *terms)
 
         @pl.when(above & jnp.logical_not(below))
         def _():
-            add_into(self.out, from_above, *terms)
+            add_into(out, from_above, *terms)
 
         @pl.when(jnp.logical_not(above) & below)
         def _():
-            add_into(self.out, from_below, *terms)
+            add_into(out, from_below, *terms)
+
+
+    def spare_view(self, k):
+        place = self.place
+        return self.part(self.view(place.near(k) * place.inner + place.beside(1)), 1)
+
+    def spare_first(self):
+        return remote(
+            self.spare_view(3),
+            self.spare.at[0],
+            self.spare_sems[0].at[0],
+            self.spare_sems[1].at[0],
+            self.place.at(self.place.near(1), self.place.side),
+        )
+
+    def spare_second(self):
+        return remote(
+            self.spare.at[2],
+            self.spare.at[1],
+            self.spare_sems[0].at[1],
+            self.spare_sems[1].at[1],
+            self.place.at(self.place.near(2), self.place.side),
+        )
+
+    def spare_side(self):
+        return self.side_copy(self.far(2), 1, 1, self.spare.at[3])
+
+    def start(self):
+        outer = self.place.outer
+        if not self.evened:
+            for k in range(outer):
+                for h in range(self.parts):
+                    self.send(k, h)
+            return
+        self.send(0, 0)
+        for k, h in ((1, 0), (1, 1), (2, 0)):
+            self.send(k, h)
+
+        @pl.when(jnp.logical_not(self.middle))
+        def _():
+            self.spare_first().start()
+            there = self.far(0)
+            self.onward(
+                there, 1, self.part(self.view(there * self.place.inner + self.place.side), 1)
+            ).start()
+            for k, h in ((2, 1), (3, 0), (3, 1)):
+                self.send(k, h)
+
+    def turn(self):
+        @pl.when(self.middle)
+        def _():
+            self.spare_first().wait_recv()
+            add_into(self.spare.at[2], self.spare.at[0], self.spare_view(3))
+            self.spare_second().start()
+            self.pass_on(0, 1)
+            self.spare_second().wait_recv()
+            add_into(self.spare.at[3], self.spare.at[1], self.spare_view(1))
+            self.spare_side().start()
+            for h in (0, 1):
+                self.send(3, h)
+
+    def events(self):
+        outer, parts = self.place.outer, self.parts
+        todo = []
+        if self.evened:
+            todo.append(self.turn)
+            todo.append(lambda: self.pass_on(0, 0))
+        else:
+            for h in range(parts):
+                todo.append(lambda h=h: self.pass_on(0, h))
+        for k in range(1, outer - 1):
+            for h in range(parts):
+                todo.append(lambda k=k, h=h: self.pass_on(k, h))
+        for h in range(parts):
+            todo.append(lambda h=h: self.last(h))
+        return todo
 
     def finish(self):
         for k in range(self.place.outer):
-            if k < self.place.outer - 1:
-                self.onward(self.far(k)).wait_send()
-            for step in range(1, self.place.inner):
-                self.side_copy(self.far(k), step).wait_send()
+            for h in range(self.parts):
+                if k < self.place.outer - 1:
+                    self.onward(self.far(k), h).wait_send()
+                if not self.alone(k, h):
+                    for step in range(1, self.place.inner):
+                        self.side_copy(self.far(k), step, h).wait_send()
+        if self.evened:
+
+            @pl.when(self.middle)
+            def _():
+                self.spare_second().wait_send()
+
+            @pl.when(jnp.logical_not(self.middle))
+            def _():
+                self.spare_first().wait_send()
 
 
 def reduce_blk(place, view, out, *scratch):
@@ -324,14 +514,11 @@
         part = view
         view = lambda piece: part.at[piece]
     work = ReduceBlk(place, view, out, *scratch)
-    for k in range(place.outer):
-        work.send(k)
+    work.start()
     yield
-    for k in range(place.outer - 1):
-        work.pass_on(k)
+    for event in work.events():
+        event()
         yield
-    work.last()
-    yield
     work.finish()
 
 
@@ -481,30 +668,30 @@
     )[0]
 
 
+class Taker:
+    def __init__(self, refs):
+        self.refs = list(refs)
+
+    def __call__(self, amount):
+        taken = self.refs[:amount]
+        del self.refs[:amount]
+        return taken
+
+
 def gather_first(qkv, out_parts, tokens, gains, docs, count, number):
     names = 5
 
     def body(*refs):
         qkv_ref, out_ref, tok_ref, gain_ref, doc_ref = refs[:names]
-        qkv_all, out_all, tok_all, gain_all, doc_all = refs[names : 2 * names]
-        out_mine, gain_mine = refs[2 * names : 2 * names + 2]
-        sems = list(refs[2 * names + 2 :])
-
-        def take(amount):
-            taken = sems[:amount]
-            del sems[:amount]
-            return taken
-
+        qkv_all, out_mine, tok_all, gain_all, doc_all = refs[names : 2 * names]
+        gain_mine = refs[2 * names]
+        take = Taker(refs[2 * names + 1 :])
         place = Place(count)
         greet(place, blk=True, core=True, half=True, corner=True)
 
         def gain_task(near, far):
             yield from gather_blk(place, gain_ref, gain_mine, *near)
             yield from gather_group(place, gain_mine, gain_all, *far)
-
-        def out_task(near, far):
-            yield from exchange_group(place, out_ref, out_mine, *near)
-            yield from gather_blk(place, out_mine, out_all, *far)
 
         def doc_task(sent, came, own):
             copy = pltpu.make_async_copy(doc_ref, doc_all.at[place.core], own)
@@ -518,10 +705,10 @@
 
         together(
             gain_task(take(3), take(3)),
+            gather_blk(place, qkv_ref, qkv_all, *take(3)),
             doc_task(*take(3)),
             gather_group(place, tok_ref, tok_all, *take(3)),
-            gather_blk(place, qkv_ref, qkv_all, *take(3)),
-            out_task(take(3), take(3)),
+            exchange_group(place, out_ref, out_mine, *take(3)),
         )
 
     ins = [qkv, out_parts, tokens, gains, docs]
@@ -532,79 +719,120 @@
         ins,
         [
             shape((count,) + qkv.shape, qkv.dtype),
-            shape((count,) + out_parts.shape, out_parts.dtype),
+            shape(out_parts.shape, out_parts.dtype),
             shape((GROUPS,) + tokens.shape, tokens.dtype),
             shape((GROUPS, count) + gains.shape, gains.dtype),
             shape((2,) + docs.shape, docs.dtype),
         ],
-        [
-            pltpu.VMEM(out_parts.shape, out_parts.dtype),
-            pltpu.VMEM((count,) + gains.shape, gains.dtype),
-        ]
+        [pltpu.VMEM((count,) + gains.shape, gains.dtype)]
+        + gather_blk_sems(count, 1)
+        + gather_group_sems()
         + gather_blk_sems(count)
-        + gather_group_sems()
         + [pltpu.SemaphoreType.DMA] * 3
         + gather_group_sems()
-        + gather_blk_sems(count)
-        + exchange_group_sems()
-        + gather_blk_sems(count),
+        + exchange_group_sems(),
         (qkv.size + out_parts.size) * 2 * count,
     )
 
 
-def reduce_last(qkv_part, out_part, norm_part, gain_part, count, number):
-    out_piece, gain_piece = out_part.shape[1:], gain_part.shape[1:]
-    qkv_piece, norm_piece = qkv_part.shape[1:], norm_part.shape[1:]
-
-    def body(*refs):
-        qkv_ref, out_ref, norm_ref, gain_ref = refs[:4]
-        qkv_sum, out_sum, norm_sum, gain_sum = refs[4:8]
-        out_mine, gain_mine = refs[8:10]
-        rest = list(refs[10:])
-
-        def take(amount):
-            taken = rest[:amount]
-            del rest[:amount]
-            return taken
-
+def gather_second(kv, out_mine, count, number):
+    def body(kv_ref, out_ref, kv_all, out_all, *sems):
+        take = Taker(sems)
+        place = Place(count)
+        greet(place, blk=True)
+        together(
+            gather_blk(place, kv_ref, kv_all, *take(3)),
+            gather_blk(place, out_ref, lambda i: out_all.at[:, i], *take(3)),
+        )
+
+    groups, rows, width = out_mine.shape
+    return transfer(
+        f"gather{number}",
+        number,
+        body,
+        [kv, out_mine],
+        [
+            shape((count,) + kv.shape, kv.dtype),
+            shape((groups, count, rows, width), out_mine.dtype),
+        ],
+        gather_blk_sems(count) + gather_blk_sems(count),
+        (kv.size + out_mine.size) * 2 * count,
+    )
+
+
+def reduce_middle(dkv_part, out_part, count, number):
+    dkv_piece = dkv_part.shape[1:]
+    out_piece = out_part.shape[:1] + out_part.shape[2:]
+
+    def body(dkv_ref, out_ref, dkv_sum, out_sum, out_mine, *scratch):
+        take = Taker(scratch)
         place = Place(count)
         greet(place, blk=True, core=True, half=True, corner=True)
-
-        def out_task(near, far):
-            yield from reduce_blk(place, out_ref, out_mine, *near)
+        far = take(3)
+
+        def out_task(near):
+            yield from reduce_blk(place, lambda i: out_ref.at[:, i], out_mine, *near)
             yield from exchange_group(place, out_mine, out_sum, *far)
+
+        together(
+            reduce_blk(place, dkv_ref, dkv_sum, *take(REDUCE_REFS)),
+            out_task(take(REDUCE_REFS)),
+        )
+
+    return transfer(
+        f"reduce{number}",
+        number,
+        body,
+        [dkv_part, out_part],
+        [shape(dkv_piece, jnp.bfloat16), shape(out_piece, jnp.bfloat16)],
+        [pltpu.VMEM(out_piece, jnp.bfloat16)]
+        + exchange_group_sems()
+        + reduce_blk_scratch(count, dkv_piece, jnp.bfloat16)
+        + reduce_blk_scratch(count, out_piece, jnp.bfloat16),
+        (dkv_part.size + out_part.size) * 2,
+        [pltpu.VMEM] * 2,
+    )
+
+
+def reduce_last(qkv_part, norm_part, gain_part, count, number):
+    gain_piece = gain_part.shape[1:]
+    qkv_piece, norm_piece = qkv_part.shape[1:], norm_part.shape[1:]
+
+    def body(*refs):
+        qkv_ref, norm_ref, gain_ref = refs[:3]
+        qkv_sum, norm_sum, gain_sum = refs[3:6]
+        gain_mine = refs[6]
+        take = Taker(refs[7:])
+        place = Place(count)
+        greet(place, blk=True, core=True, half=True, corner=True)
 
         def gain_task(near, far):
             yield from reduce_blk(place, gain_ref, gain_mine, *near)
             yield from reduce_group(place, gain_mine, gain_sum, *far)
 
         together(
-            gain_task(take(7), take(5)),
+            gain_task(take(REDUCE_REFS), take(5)),
+            reduce_blk(place, qkv_ref, qkv_sum, *take(REDUCE_REFS)),
             reduce_group(place, norm_ref, norm_sum, *take(5)),
-            out_task(take(7), take(3)),
-            reduce_blk(place, qkv_ref, qkv_sum, *take(7)),
         )
 
     return transfer(
         f"last{number}",
         number,
         body,
-        [qkv_part, out_part, norm_part, gain_part],
+        [qkv_part, norm_part, gain_part],
         [
             shape(qkv_piece, jnp.float32),
-            shape(out_piece, jnp.bfloat16),
             shape(norm_piece, jnp.float32),
             shape(gain_piece[1:], jnp.float32),
         ],
-        [pltpu.VMEM(out_piece, jnp.bfloat16), pltpu.VMEM(gain_piece, jnp.float32)]
-        + reduce_blk_scratch(count, gain_piece, jnp.float32)
+        [pltpu.VMEM(gain_piece, jnp.float32)]
+        + reduce_blk_scratch(count, gain_piece, jnp.float32, 1)
         + reduce_group_scratch(gain_piece[1:], jnp.float32)
-        + reduce_group_scratch(norm_piece, jnp.bfloat16)
-        + reduce_blk_scratch(count, out_piece, jnp.bfloat16)
-        + exchange_group_sems()
-        + reduce_blk_scratch(count, qkv_piece, jnp.bfloat16),
-        (qkv_part.size + out_part.size) * 2,
-        [pltpu.VMEM] * 4,
+        + reduce_blk_scratch(count, qkv_piece, jnp.bfloat16)
+        + reduce_group_scratch(norm_piece, jnp.bfloat16),
+        qkv_part.size * 2,
+        [pltpu.VMEM] * 3,
     )
 
 
@@ -665,7 +893,7 @@
     tile = rows * width * 2
     weights = 3 * hidden * width * 2
     kept = count * rows * 3 * hidden * 2
-    total = weights + kept + tile * (3 * count + outer * (inner - 1) + 2 * outer + 1) + 9 * tile
+    total = weights + kept + tile * (3 * count + outer * (inner - 1) + 2 * outer + 3) + 9 * tile
     total += 3 * LANES * (count * rows + 2 * width) * 2
     return total < 58 * 2**20 and hidden % (3 * LANES) == 0 and width % 256 == 0
 
@@ -700,6 +928,7 @@
     beside,
     along,
     held,
+    spare,
     w_sems,
     out_sems,
     *sems,
@@ -713,12 +942,7 @@
     steps = rows // slab
     columns = width // 256
     pair = inner * rows
-    sems = list(sems)
-
-    def take(amount):
-        taken = sems[:amount]
-        del sems[:amount]
-        return taken
+    take = Taker(sems)
 
     def weight_copies(i):
         units_at = pl.ds(pl.multiple_of(i * LANES, LANES), LANES)
@@ -777,15 +1001,32 @@
         split = value.astype(jnp.bfloat16).reshape((inner, steps, slab, 256))
         part[pair_pieces(k), :, :, column(n)] = split
 
+    def receive(gather, k):
+        if k == 0:
+            gather.copy.wait()
+        if not gather.evened:
+            if k + 1 < outer:
+                gather.pass_on(k + 1)
+            gather.beside_arrived(k)
+            return
+        ends = jnp.logical_not(gather.middle)
+        if k == 0:
+            gather.pass_on(1)
+            pl.when(gather.middle)(lambda: gather.pass_on(2))
+        elif k == 1:
+            pl.when(ends)(lambda: gather.pass_on(2))
+            gather.pass_extra(1)
+            pl.when(gather.middle)(lambda: gather.pass_on(3))
+        elif k == 2:
+            pl.when(ends)(lambda: gather.pass_on(3))
+            gather.pass_extra(3)
+        gather.beside_arrived(k)
+
     gather = GatherBlk(place, norm_own, lambda i: norm_all.at[i], *take(3))
     gather.start()
     lax.fori_loop(0, chunks, wait_weights, 0)
     for k in range(outer):
-        if k == 0:
-            gather.copy.wait()
-        if k + 1 < outer:
-            gather.pass_on(k + 1)
-        gather.beside_arrived(k)
+        receive(gather, k)
         at = pair_rows(k)
 
         def up_chunk(j, carry, k=k, at=at):
@@ -807,12 +1048,10 @@
 
         lax.fori_loop(0, columns, down_chunk, 0)
     gather.finish()
-    reduce = ReduceBlk(place, lambda i: part.at[i], total, beside, along, held, *take(4))
-    for k in range(outer):
-        reduce.send(k)
-    for k in range(outer - 1):
-        reduce.pass_on(k)
-    reduce.last()
+    reduce = ReduceBlk(place, lambda i: part.at[i], total, beside, along, held, spare, *take(6))
+    reduce.start()
+    for event in reduce.events():
+        event()
 
     gain_grad_ref[...] = jnp.zeros_like(gain_grad_ref)
 
@@ -838,11 +1077,7 @@
     gather = GatherBlk(place, grad_own, lambda i: grad_all.at[i], *take(3))
     gather.start()
     for k in range(outer):
-        if k == 0:
-            gather.copy.wait()
-        if k + 1 < outer:
-            gather.pass_on(k + 1)
-        gather.beside_arrived(k)
+        receive(gather, k)
         at = pair_rows(k)
 
         def back_chunk(j, carry, k=k, at=at):
@@ -869,9 +1104,8 @@
 
         lax.fori_loop(0, columns, input_chunk, 0)
     gather.finish()
-    reduce = ReduceBlk(place, lambda i: part.at[i], total, beside, along, held, *take(4))
-    for k in range(outer):
-        reduce.send(k)
+    reduce = ReduceBlk(place, lambda i: part.at[i], total, beside, along, held, spare, *take(6))
+    reduce.start()
 
     tokens = count * rows
     slots = staged.shape[0]
@@ -934,16 +1168,20 @@
         down_store(i).start()
         return carry
 
-    bounds = [chunks * k // (outer - 1) for k in range(outer)]
-    for k in range(outer - 1):
+    events = reduce.events()
+    early = len(events) - 3
+    bounds = [chunks * k // early for k in range(early + 1)]
+    for k in range(early):
         lax.fori_loop(bounds[k], bounds[k + 1], up_grad, 0)
-        reduce.pass_on(k)
+        events[k]()
     for i in range(max(0, chunks - slots), chunks):
         for copy in up_store(i):
             copy.wait()
     thirds = units // three
-    lax.fori_loop(0, thirds, down_grad, 0)
-    reduce.last()
+    bounds = [thirds * k // 3 for k in range(4)]
+    for k in range(3):
+        lax.fori_loop(bounds[k], bounds[k + 1], down_grad, 0)
+        events[early + k]()
 
     def after(i, carry):
         value, mid, cot = branch_ref[i], middle[i], cot_ref[i].astype(jnp.float32)
@@ -1002,15 +1240,15 @@
             pltpu.VMEM((3 * LANES, count * rows), bf16),
             pltpu.VMEM((slots, 3 * LANES, width), bf16),
         ]
-        + line_scratch[:3]
+        + line_scratch[:4]
         + [
             pltpu.SemaphoreType.DMA((3 * units // LANES,)),
             pltpu.SemaphoreType.DMA((slots, 3)),
         ]
         + gather_blk_sems(count)
-        + line_scratch[3:]
+        + line_scratch[4:]
         + gather_blk_sems(count)
-        + line_scratch[3:],
+        + line_scratch[4:],
         compiler_params=pltpu.CompilerParams(
             collective_id=number, has_side_effects=True, vmem_limit_bytes=67043328
         ),
@@ -1304,13 +1542,11 @@
     qkv_rows = qkv_weight.shape[0]
     qkv_slab = slabs(qkv_rows)
     qkv_piece = (qkv_rows // qkv_slab, qkv_slab, width)
-    qkv_all, out_all, tokens_all, gains_all, docs_all = gather_first(
+    qkv_all, out_mine, tokens_all, gains_all, docs_all = gather_first(
         qkv_weight, out_sent, tokens[0], gains_sent, segments.reshape(-1, 128), count, 1
     )
     gains = jnp.transpose(gains_all[:, :, :4, :gain_rows], (2, 0, 1, 3)).reshape(4, width)
     qkv_head = qkv_all.reshape(count * qkv_rows, width)
-    out_head = out_all.reshape(count, GROUPS, out_rows, head_width)
-    out_head = jnp.transpose(out_head, (1, 0, 2, 3)).reshape(width, head_width)
     docs = docs_all.reshape(2, 2, count, rows)
     key_doc = docs.reshape(2, 2 * count, 1, rows)
     own_doc = lax.dynamic_index_in_dim(docs, here, 2, keepdims=False).reshape(GROUPS, rows, 1)
@@ -1329,7 +1565,9 @@
     own_kv = sent[:, REPS:].reshape(group_rows, 2 * HEAD_DIM)
     kv_slab = slabs(group_rows)
     kv_piece = (group_rows // kv_slab, kv_slab, 2 * HEAD_DIM)
-    kv = all_gather_blk(own_kv, count, 2).reshape(count, GROUPS, rows, 2 * HEAD_DIM)
+    kv, out_all = gather_second(own_kv, out_mine, count, 2)
+    kv = kv.reshape(count, GROUPS, rows, 2 * HEAD_DIM)
+    out_head = out_all.reshape(width, head_width)
     attn, attended, totals = attention_forward(here_one, queries, kv, own_doc, key_doc)
     attn = attn.reshape(group_rows, head_width)
     branch_part = dot(attn, out_head, LAST).astype(bf16)
@@ -1372,15 +1610,15 @@
     branch_all = all_gather_group(branch_grad, 8).reshape(group_rows, width)
     attn_grad = dot(branch_all, out_head, PLAIN).astype(bf16).reshape(GROUPS, rows, head_width)
     out_part = dot(branch_all, attn, FIRST).astype(bf16)
-    out_part = jnp.transpose(out_part.reshape(GROUPS, count, out_rows, head_width), (1, 0, 2, 3))
+    out_part = out_part.reshape(GROUPS, count, out_rows, head_width)
     dq, dkv_part = attention_backward(
         here_one, queries, kv, own_doc, key_doc, attn_grad, attended, totals
     )
-    dkv = reduce_scatter_blk(dkv_part.reshape((count,) + kv_piece), count, 9)
+    dkv, out_grad = reduce_middle(dkv_part.reshape((count,) + kv_piece), out_part, count, 9)
     sent_grad = jnp.concatenate(
         [
             dq.reshape(group_rows, REPS, HEAD_DIM),
-            dkv.astype(bf16).reshape(group_rows, 2, HEAD_DIM),
+            dkv.reshape(group_rows, 2, HEAD_DIM),
         ],
         axis=1,
     ).astype(jnp.float32)
@@ -1397,9 +1635,8 @@
     gain_part = jnp.stack([gain_grad_one, gain_grad_two, gain_grad_three, gain_grad_four])
     gain_part = jnp.transpose(gain_part.reshape(4, GROUPS, count, gain_rows), (2, 1, 0, 3))
     gain_part = jnp.pad(gain_part, ((0, 0), (0, 0), (0, 4), (0, gain_lanes - gain_rows)))
-    qkv_grad, out_grad, norm_one_grad, gain_grad = reduce_last(
+    qkv_grad, norm_one_grad, gain_grad = reduce_last(
         qkv_part.reshape((count,) + qkv_piece),
-        out_part,
         norm_one_part.astype(bf16).reshape((GROUPS,) + piece),
         gain_part[:, :, None],
         count,

time: 719 us -> 679 us (0.944)
  Pallas kernels: 633 us -> 588 us
    pallas_call x1, Pallas kernels: 258 us -> 226 us  [feed_forward(): pl.pallas_call(functools.partial(feed_forward_kernel, count), name='feed_...]
    pallas_call x6, Pallas kernels: 341 us -> 328 us  [transfer(): pl.pallas_call(body, name=name, out_shape=outs, in_specs=[pl.BlockSpec(me...]
  transfers between devices with their start and end apart: 4 -> 4, of which waited for: 0 -> 0; matrix products, arithmetic and copies ran while one was open for 7% -> 8% of each run, Pallas kernels for 52% -> 54%
where the time goes in v3:
time: 679 us; the launch traced here: 670 us
  Pallas kernels  588 us (87%)
  matrix products  25.6 us (4%)
  local copies, waits for them, and re-layouts  20.6 us (3%)
  other arithmetic  18.7 us (3%)
  between operations  14.3 us (2%)
    pallas_call x6, Pallas kernels, transfer(): pl.pallas_call(body, name=name, out_shape=outs, in_specs=[pl.BlockSpec(me...  328 us
    pallas_call x1, Pallas kernels, feed_forward(): pl.pallas_call(functools.partial(feed_forward_kernel, count), name='feed_...  226 us
    dot_general x6, matrix products, dot(): lax.dot_general(left, right, (contract, ((), ())), preferred_element_type...  25.6 us
    pallas_call x1, Pallas kernels, attention_backward(): pl.pallas_call(functools.partial(attention_backward_kernel, count), name=...  19.8 us
    pallas_call x1, Pallas kernels, attention_forward(): pl.pallas_call(functools.partial(attention_forward_kernel, count), name='...  13.9 us
  transfers between devices with their start and end apart: 4, of which 0 were waited for; matrix products, arithmetic and copies ran while one was open for 8% of the time, Pallas kernels for 54%

profile of v3, /device:TPU:20, one launch (start us, length us, event | category | flops | bytes accessed | tf_op | source)
XLA Modules:
  0.0 669.7 jit_solution(17754326320470353123)
XLA Ops:
  10.1 64.0 %first1.1 = (bf16[8,128,2304]{2,1,0:T(8,128)(2,1)}, bf16[4,72,512]{2,1,0:T(8,128)(2,1)}, bf16[4,128,2304]{2,1,0:T(8,128)(2,1)}, f32[4,8,8,128]{3,2,1,0:T(8,128)}, s32[2,16,128]{2,1,0:T(8,128)}) custom-call(bf16[128,2304]{1,0:T(8,128)(2,1)} %refs_0_.1, bf16[4,72,512]{2,1,0:T(8,128)(2,1)} %bitcast.111, bf16[128,2304]{1,0:T(8,128)(2,1)} %bitcast.95, ...), custom_call_target="tpu_custom_call" | custom-call | bytes 283115520 | tf_op jit(solution)/shard_map/first1/pallas_call | solution.py:612
  77.7 2.2 multiply_reduce_fusion
  81.1 2.6 copy-done.21
  83.7 2.6 fusion.15
  91.5 68.2 %gather2.1 = (bf16[8,512,512]{2,1,0:T(8,128)(2,1)}, bf16[4,8,72,512]{3,2,1,0:T(8,128)(2,1)}) custom-call(bf16[512,512]{1,0:T(8,128)(2,1)} %copy.39.kv_ref, bf16[4,72,512]{2,1,0:T(8,128)(2,1)} %get-tuple-element.33.out_ref), custom_call_target="tpu_custom_call" | custom-call | bytes 262144000 | tf_op jit(solution)/shard_map/gather2/pallas_call | solution.py:612
  159.7 13.9 %attend.1 = (bf16[4,128,512]{2,1,0:T(8,128)(2,1)}, f32[4,128,512]{2,1,0:T(8,128)}, f32[4,256,1]{2,1,0:T(8,128)}) custom-call(s32[1]{0:T(128)} %bitcast.here_ref, bf16[4,128,512]{2,1,0:T(8,128)(2,1)} %copy.38.q_ref, bf16[8,4,128,512]{3,2,1,0:T(8,128)(2,1)} %bitcast.99, s32[4,128,1]{2,1,0:T(8,128)} %copy.27.doc_ref, s32[2,16,1,128]{3,2,1,0:T(1,128)} %bitcast.119), custom_call_target="tpu_custom_call" | custom-call | flops 1000000000 | bytes 41943040 | tf_op jit(solution)/shard_map/attend/pallas_call | solution.py:1395
  173.7 3.9 convolution_convert_fusion.1
  177.6 20.7 %fold3.1.branch_ref = f32[8,16,2304]{2,1,0:T(8,128)} custom-call(bf16[4,8,16,2304]{3,2,1,0:T(8,128)(2,1)} %bitcast.107), custom_call_target="tpu_custom_call" | custom-call | bytes 94371840 | tf_op jit(solution)/shard_map/fold3/pallas_call | solution.py:612
  198.3 226.2 %feed_forward.1 = (bf16[8,16,2304]{2,1,0:T(8,128)(2,1)}, f32[8,16,2304]{2,1,0:T(8,128)}, bf16[8,16,2304]{2,1,0:T(8,128)(2,1)}, f32[4,2304]{1,0:T(4,128)}, bf16[1...) custom-call(f32[8,16,2304]{2,1,0:T(8,128)} %fold3.1.branch_ref, bf16[8,16,2304]{2,1,0:T(8,128)(2,1)} %bitcast.96, ...), custom_call_target="tpu_custom_call" | custom-call | flops 48922361856 | bytes 524288000 | tf_op jit(solution)/shard_map/feed_forward/pallas_call | solution.py:1215
  425.7 19.6 %group8.1 = bf16[4,128,2304]{2,1,0:T(8,128)(2,1)} custom-call(bf16[128,2304]{1,0:T(8,128)(2,1)} %bitcast.116), custom_call_target="tpu_custom_call" | custom-call | bytes 94371840 | tf_op jit(solution)/shard_map/group8/pallas_call | solution.py:612
  445.3 4.5 convolution_convert_fusion.2
  449.8 19.8 %attend_back.1 = (bf16[4,128,512]{2,1,0:T(8,128)(2,1)}, bf16[8,4,128,512]{3,2,1,0:T(8,128)(2,1)}) custom-call(s32[1]{0:T(128)} %bitcast.here_ref, bf16[4,128,512]{2,1,0:T(8,128)(2,1)} %copy.38.q_ref, bf16[8,4,128,512]{3,2,1,0:T(8,128)(2,1)} %bitcast.100, s32[4,128,1]{2,1,0:T(8,128)} %copy.27.doc_ref, s32[2,16,1,128]{3,2,1,0:T(1,128)} %bitcast.120, ...), custom_call_target="tpu_custom_call" | custom-call | flops 2000000000 | bytes 83886080 | tf_op jit(solution)/shard_map/attend_back/pallas_call | solution.py:1422
  469.7 1.2 reshape.328
  471.6 3.9 fusion.2
  475.5 93.3 %reduce9.1 = (bf16[32,16,512]{2,1,0:T(8,128)(2,1)}, bf16[4,72,512]{2,1,0:T(8,128)(2,1)}) custom-call(bf16[8,32,16,512]{3,2,1,0:T(8,128)(2,1)} %bitcast.101, bf16[4,8,72,512]{3,2,1,0:T(8,128)(2,1)} %bitcast.103), custom_call_target="tpu_custom_call" | custom-call | bytes 262144000 | tf_op jit(solution)/shard_map/reduce9/pallas_call | solution.py:612
  568.8 1.2 reshape.331
  574.8 6.5 fusion.1
  582.2 4.2 convolution_convert_fusion
  586.4 62.8 %last10.1 = (f32[8,16,2304]{2,1,0:T(8,128)}, f32[8,16,2304]{2,1,0:T(8,128)}, f32[1,8,128]{2,1,0:T(8,128)}) custom-call(bf16[8,8,16,2304]{3,2,1,0:T(8,128)(2,1)} %bitcast.98, bf16[4,8,16,2304]{3,2,1,0:T(8,128)(2,1)} %bitcast.102, f32[8,4,1,8,128]{4,3,2,1,0:T(8,128)} %pad_bitcast_fusion.refs_2_), custom_call_target="tpu_custom_call" | custom-call | bytes 188743680 | tf_op jit(solution)/shard_map/last10/pallas_call | solution.py:612
  649.2 1.7 fusion.7
  650.9 1.3 slice_bitcast_fusion.1
  652.2 1.2 fusion.10
  653.4 3.0 convert_element_type.113
  656.4 4.9 convert_element_type.112
  (103 shorter events, 22.2 us)
Async XLA Ops:
  7.2 1.6 copy-start.15
  7.2 2.3 copy-start.20
  7.2 191.1 %all-gather.5.cloned.1.call-start = ((), (), s32[]{:S(2)}) async-start(), calls=%async_computation.3 | async-start | bytes 6635520 | tf_op jit(solution)/shard_map/all_gather | solution.py:1533
  7.9 190.4 %all-gather.3.cloned.1.call-start = ((), (), s32[]{:S(2)}) async-start(), calls=%async_computation.2 | async-start | bytes 13271040 | tf_op jit(solution)/shard_map/all_gather | solution.py:1532
  8.7 644.7 %reduce-scatter.5.cloned.1.call-start = ((), (), s32[]{:S(2)}) async-start(), calls=%async_computation.5 | async-start | bytes 6635520 | tf_op jit(solution)/shard_map/reduce_scatter | solution.py:1607
  74.0 6.4 copy-start
  75.3 5.8 copy-start.16
  80.5 3.2 copy-start.21
  81.1 5.2 copy-start.7
  87.4 1.8 copy-start.3
  159.7 14.0 %copy-start.22 = (bf16[4,8,72,512]{3,2,1,0:T(8,128)(2,1)S(1)}, bf16[4,8,72,512]{3,2,1,0:T(8,128)(2,1)}, u32[]{:S(2)}) copy-start(bf16[4,8,72,512]{3,2,1,0:T(8,128)(2,1)} %get-tuple-element.37) | copy-start | bytes 7077892
  424.5 231.9 %reduce-scatter.3.cloned.1.call-start = ((), (), s32[]{:S(2)}) async-start(), calls=%async_computation.4 | async-start | bytes 13271040 | tf_op jit(solution)/shard_map/reduce_scatter | solution.py:1604
  425.1 20.2 %copy-start.23 = (bf16[4,8,72,512]{3,2,1,0:T(8,128)(2,1)S(1)}, bf16[4,8,72,512]{3,2,1,0:T(8,128)(2,1)}, u32[]{:S(2)}) copy-start(bf16[4,8,72,512]{3,2,1,0:T(8,128)(2,1)} %get-tuple-element.37) | copy-start | bytes 7077892
  449.8 21.8 %copy-start.9 = (bf16[4,128,2304]{2,1,0:T(8,128)(2,1)S(1)}, bf16[4,128,2304]{2,1,0:T(8,128)(2,1)}, u32[]{:S(2)}) copy-start(bf16[4,128,2304]{2,1,0:T(8,128)(2,1)} %group8.1) | copy-start | bytes 7077892
  568.8 2.0 copy-start.14
  573.1 1.8 copy-start.1
  573.1 1.8 copy-start.19
  574.8 7.3 %copy-start.8 = (bf16[4,128,2304]{2,1,0:T(8,128)(2,1)S(1)}, bf16[4,128,2304]{2,1,0:T(8,128)(2,1)}, u32[]{:S(2)}) copy-start(bf16[4,128,2304]{2,1,0:T(8,128)(2,1)} %copy-done.7) | copy-start | bytes 7077892
  586.4 62.8 %copy-start.2 = (bf16[1,128,2304]{2,1,0:T(8,128)(2,1)S(1)}, bf16[1,128,2304]{2,1,0:T(8,128)(2,1)}, u32[]{:S(2)}) copy-start(bf16[1,128,2304]{2,1,0:T(8,128)(2,1)} %param.8) | copy-start | bytes 1769476
  586.4 62.8 %copy-start.17 = (f32[2304]{0:T(1024)S(1)}, f32[2304]{0:T(1024)}, u32[]{:S(2)}) copy-start(f32[2304]{0:T(1024)} %copy-done.16) | copy-start | bytes 27652
  586.4 65.8 %copy-start.11 = (f32[8,16,2304]{2,1,0:T(8,128)S(1)}, f32[8,16,2304]{2,1,0:T(8,128)}, u32[]{:S(2)}) copy-start(f32[8,16,2304]{2,1,0:T(8,128)} %get-tuple-element.39) | copy-start | bytes 3538948
  649.2 3.0 copy-start.5
  656.4 4.9 copy-start.13
  656.4 5.7 copy-start.12
  (5 other events, 5.1 us)
Sparse Core Ops, SparseCore 0:
  9.6 51.8 all-gather.4
  63.0 70.7 all-gather.2
  424.7 53.1 reduce-scatter.4
  480.3 85.7 reduce-scatter.2

commit v4 on v3

--- a/solution.py
+++ b/solution.py
@@ -96,6 +96,14 @@
                 next(task)
             except StopIteration:
                 tasks.remove(task)
+
+
+def waiting(task, *rounds):
+    for step, _ in enumerate(task):
+        yield
+        if step < len(rounds):
+            for _ in range(rounds[step]):
+                yield
 
 
 def near_order(outer, line):
@@ -440,49 +448,59 @@
     def spare_side(self):
         return self.side_copy(self.far(2), 1, 1, self.spare.at[3])
 
-    def start(self):
+    def opening(self):
         outer = self.place.outer
         if not self.evened:
-            for k in range(outer):
-                for h in range(self.parts):
-                    self.send(k, h)
-            return
-        self.send(0, 0)
-        for k, h in ((1, 0), (1, 1), (2, 0)):
-            self.send(k, h)
-
-        @pl.when(jnp.logical_not(self.middle))
-        def _():
+
+            def every():
+                for k in range(outer):
+                    for h in range(self.parts):
+                        self.send(k, h)
+
+            return [every]
+        ends = jnp.logical_not(self.middle)
+
+        def along():
             self.spare_first().start()
             there = self.far(0)
             self.onward(
                 there, 1, self.part(self.view(there * self.place.inner + self.place.side), 1)
             ).start()
-            for k, h in ((2, 1), (3, 0), (3, 1)):
-                self.send(k, h)
-
-    def turn(self):
-        @pl.when(self.middle)
-        def _():
+
+        todo = [lambda: self.send(0, 0), lambda: pl.when(ends)(along)]
+        todo += [lambda k=k, h=h: self.send(k, h) for k, h in ((1, 0), (1, 1), (2, 0))]
+        todo += [
+            lambda k=k, h=h: pl.when(ends)(lambda: self.send(k, h))
+            for k, h in ((2, 1), (3, 0), (3, 1))
+        ]
+        return todo
+
+    def start(self):
+        for step in self.opening():
+            step()
+
+    def turning(self):
+        def first():
             self.spare_first().wait_recv()
             add_into(self.spare.at[2], self.spare.at[0], self.spare_view(3))
             self.spare_second().start()
-            self.pass_on(0, 1)
+
+        def second():
             self.spare_second().wait_recv()
             add_into(self.spare.at[3], self.spare.at[1], self.spare_view(1))
             self.spare_side().start()
             for h in (0, 1):
                 self.send(3, h)
 
+        steps = (first, lambda: self.pass_on(0, 1), second)
+        return [lambda step=step: pl.when(self.middle)(step) for step in steps]
+
     def events(self):
         outer, parts = self.place.outer, self.parts
-        todo = []
         if self.evened:
-            todo.append(self.turn)
-            todo.append(lambda: self.pass_on(0, 0))
+            todo = self.turning() + [lambda: self.pass_on(0, 0)]
         else:
-            for h in range(parts):
-                todo.append(lambda h=h: self.pass_on(0, h))
+            todo = [lambda h=h: self.pass_on(0, h) for h in range(parts)]
         for k in range(1, outer - 1):
             for h in range(parts):
                 todo.append(lambda k=k, h=h: self.pass_on(k, h))
@@ -514,10 +532,8 @@
         part = view
         view = lambda piece: part.at[piece]
     work = ReduceBlk(place, view, out, *scratch)
-    work.start()
-    yield
-    for event in work.events():
-        event()
+    for step in work.opening() + work.events():
+        step()
         yield
     work.finish()
 
@@ -707,8 +723,8 @@
             gain_task(take(3), take(3)),
             gather_blk(place, qkv_ref, qkv_all, *take(3)),
             doc_task(*take(3)),
-            gather_group(place, tok_ref, tok_all, *take(3)),
-            exchange_group(place, out_ref, out_mine, *take(3)),
+            waiting(gather_group(place, tok_ref, tok_all, *take(3)), 2),
+            waiting(exchange_group(place, out_ref, out_mine, *take(3)), 3),
         )
 
     ins = [qkv, out_parts, tokens, gains, docs]
@@ -764,19 +780,13 @@
     dkv_piece = dkv_part.shape[1:]
     out_piece = out_part.shape[:1] + out_part.shape[2:]
 
-    def body(dkv_ref, out_ref, dkv_sum, out_sum, out_mine, *scratch):
+    def body(dkv_ref, out_ref, dkv_sum, out_sum, *scratch):
         take = Taker(scratch)
         place = Place(count)
-        greet(place, blk=True, core=True, half=True, corner=True)
-        far = take(3)
-
-        def out_task(near):
-            yield from reduce_blk(place, lambda i: out_ref.at[:, i], out_mine, *near)
-            yield from exchange_group(place, out_mine, out_sum, *far)
-
+        greet(place, blk=True)
         together(
             reduce_blk(place, dkv_ref, dkv_sum, *take(REDUCE_REFS)),
-            out_task(take(REDUCE_REFS)),
+            reduce_blk(place, lambda i: out_ref.at[:, i], out_sum, *take(REDUCE_REFS)),
         )
 
     return transfer(
@@ -785,24 +795,22 @@
         body,
         [dkv_part, out_part],
         [shape(dkv_piece, jnp.bfloat16), shape(out_piece, jnp.bfloat16)],
-        [pltpu.VMEM(out_piece, jnp.bfloat16)]
-        + exchange_group_sems()
-        + reduce_blk_scratch(count, dkv_piece, jnp.bfloat16)
+        reduce_blk_scratch(count, dkv_piece, jnp.bfloat16)
         + reduce_blk_scratch(count, out_piece, jnp.bfloat16),
         (dkv_part.size + out_part.size) * 2,
         [pltpu.VMEM] * 2,
     )
 
 
-def reduce_last(qkv_part, norm_part, gain_part, count, number):
+def reduce_last(qkv_part, norm_part, gain_part, out_sum, count, number):
     gain_piece = gain_part.shape[1:]
     qkv_piece, norm_piece = qkv_part.shape[1:], norm_part.shape[1:]
 
     def body(*refs):
-        qkv_ref, norm_ref, gain_ref = refs[:3]
-        qkv_sum, norm_sum, gain_sum = refs[3:6]
-        gain_mine = refs[6]
-        take = Taker(refs[7:])
+        qkv_ref, norm_ref, gain_ref, out_ref = refs[:4]
+        qkv_sum, norm_sum, gain_sum, out_all = refs[4:8]
+        gain_mine = refs[8]
+        take = Taker(refs[9:])
         place = Place(count)
         greet(place, blk=True, core=True, half=True, corner=True)
 
@@ -810,29 +818,34 @@
             yield from reduce_blk(place, gain_ref, gain_mine, *near)
             yield from reduce_group(place, gain_mine, gain_sum, *far)
 
+        main = reduce_blk(place, qkv_ref, qkv_sum, *take(REDUCE_REFS))
+        gain = gain_task(take(REDUCE_REFS), take(5))
         together(
-            gain_task(take(REDUCE_REFS), take(5)),
-            reduce_blk(place, qkv_ref, qkv_sum, *take(REDUCE_REFS)),
-            reduce_group(place, norm_ref, norm_sum, *take(5)),
+            waiting(gain, 11),
+            main,
+            waiting(exchange_group(place, out_ref, out_all, *take(3)), 16),
+            waiting(reduce_group(place, norm_ref, norm_sum, *take(5)), 7, 9),
         )
 
     return transfer(
         f"last{number}",
         number,
         body,
-        [qkv_part, norm_part, gain_part],
+        [qkv_part, norm_part, gain_part, out_sum],
         [
             shape(qkv_piece, jnp.float32),
             shape(norm_piece, jnp.float32),
             shape(gain_piece[1:], jnp.float32),
+            shape(out_sum.shape, jnp.bfloat16),
         ],
         [pltpu.VMEM(gain_piece, jnp.float32)]
+        + reduce_blk_scratch(count, qkv_piece, jnp.bfloat16)
         + reduce_blk_scratch(count, gain_piece, jnp.float32, 1)
         + reduce_group_scratch(gain_piece[1:], jnp.float32)
-        + reduce_blk_scratch(count, qkv_piece, jnp.bfloat16)
+        + exchange_group_sems()
         + reduce_group_scratch(norm_piece, jnp.bfloat16),
         qkv_part.size * 2,
-        [pltpu.VMEM] * 3,
+        [pltpu.VMEM] * 4,
     )
 
 
@@ -1614,7 +1627,7 @@
     dq, dkv_part = attention_backward(
         here_one, queries, kv, own_doc, key_doc, attn_grad, attended, totals
     )
-    dkv, out_grad = reduce_middle(dkv_part.reshape((count,) + kv_piece), out_part, count, 9)
+    dkv, out_sum = reduce_middle(dkv_part.reshape((count,) + kv_piece), out_part, count, 9)
     sent_grad = jnp.concatenate(
         [
             dq.reshape(group_rows, REPS, HEAD_DIM),
@@ -1635,10 +1648,11 @@
     gain_part = jnp.stack([gain_grad_one, gain_grad_two, gain_grad_three, gain_grad_four])
     gain_part = jnp.transpose(gain_part.reshape(4, GROUPS, count, gain_rows), (2, 1, 0, 3))
     gain_part = jnp.pad(gain_part, ((0, 0), (0, 0), (0, 4), (0, gain_lanes - gain_rows)))
-    qkv_grad, norm_one_grad, gain_grad = reduce_last(
+    qkv_grad, norm_one_grad, gain_grad, out_grad = reduce_last(
         qkv_part.reshape((count,) + qkv_piece),
         norm_one_part.astype(bf16).reshape((GROUPS,) + piece),
         gain_part[:, :, None],
+        out_sum,
         count,
         10,
     )

time: 679 us -> 632 us (0.931); the launches traced: 670 us -> 630 us
  Pallas kernels: 588 us -> 550 us
    pallas_call x6, Pallas kernels: 328 us -> 286 us  [transfer(): pl.pallas_call(body, name=name, out_shape=outs, in_specs=[pl.BlockSpec(me...]
  transfers between devices with their start and end apart: 4 -> 4, of which waited for: 0 -> 0; matrix products, arithmetic and copies ran while one was open for 8% -> 8% of each run, Pallas kernels for 54% -> 51%
where the time goes in v4:
time: 632 us; the launch traced here: 630 us
  Pallas kernels  550 us (87%)
  matrix products  24.9 us (4%)
  local copies, waits for them, and re-layouts  20.5 us (3%)
  other arithmetic  18.5 us (3%)
  between operations  14.3 us (2%)
    pallas_call x6, Pallas kernels, transfer(): pl.pallas_call(body, name=name, out_shape=outs, in_specs=[pl.BlockSpec(me...  286 us
    pallas_call x1, Pallas kernels, feed_forward(): pl.pallas_call(functools.partial(feed_forward_kernel, count), name='feed_...  230 us
    dot_general x6, matrix products, dot(): lax.dot_general(left, right, (contract, ((), ())), preferred_element_type...  24.9 us
    pallas_call x1, Pallas kernels, attention_backward(): pl.pallas_call(functools.partial(attention_backward_kernel, count), name=...  20.2 us
    pallas_call x1, Pallas kernels, attention_forward(): pl.pallas_call(functools.partial(attention_forward_kernel, count), name='...  13.9 us
  transfers between devices with their start and end apart: 4, of which 0 were waited for; matrix products, arithmetic and copies ran while one was open for 8% of the time, Pallas kernels for 51%

profile of v4, /device:TPU:20, one launch (start us, length us, event | category | flops | bytes accessed | tf_op | source)
XLA Modules:
  0.0 630.2 jit_solution(9136758601290143343)
XLA Ops:
  10.1 52.7 %first1.1 = (bf16[8,128,2304]{2,1,0:T(8,128)(2,1)}, bf16[4,72,512]{2,1,0:T(8,128)(2,1)}, bf16[4,128,2304]{2,1,0:T(8,128)(2,1)}, f32[4,8,8,128]{3,2,1,0:T(8,128)}, s32[2,16,128]{2,1,0:T(8,128)}) custom-call(bf16[128,2304]{1,0:T(8,128)(2,1)} %refs_0_.1, bf16[4,72,512]{2,1,0:T(8,128)(2,1)} %bitcast.111, bf16[128,2304]{1,0:T(8,128)(2,1)} %bitcast.95, ...), custom_call_target="tpu_custom_call" | custom-call | bytes 283115520 | tf_op jit(solution)/shard_map/first1/pallas_call | solution.py:628
  66.4 2.2 multiply_reduce_fusion
  69.8 3.3 copy-done.21
  73.0 2.6 fusion.15
  79.8 1.1 copy.38.q_ref
  80.9 69.4 %gather2.1 = (bf16[8,512,512]{2,1,0:T(8,128)(2,1)}, bf16[4,8,72,512]{3,2,1,0:T(8,128)(2,1)}) custom-call(bf16[512,512]{1,0:T(8,128)(2,1)} %copy.39.kv_ref, bf16[4,72,512]{2,1,0:T(8,128)(2,1)} %get-tuple-element.34.out_ref), custom_call_target="tpu_custom_call" | custom-call | bytes 262144000 | tf_op jit(solution)/shard_map/gather2/pallas_call | solution.py:628
  150.3 13.9 %attend.1 = (bf16[4,128,512]{2,1,0:T(8,128)(2,1)}, f32[4,128,512]{2,1,0:T(8,128)}, f32[4,256,1]{2,1,0:T(8,128)}) custom-call(s32[1]{0:T(128)} %bitcast.here_ref, bf16[4,128,512]{2,1,0:T(8,128)(2,1)} %copy.38.q_ref, bf16[8,4,128,512]{3,2,1,0:T(8,128)(2,1)} %bitcast.99, s32[4,128,1]{2,1,0:T(8,128)} %copy.27.doc_ref, s32[2,16,1,128]{3,2,1,0:T(1,128)} %bitcast.119), custom_call_target="tpu_custom_call" | custom-call | flops 1000000000 | bytes 41943040 | tf_op jit(solution)/shard_map/attend/pallas_call | solution.py:1408
  164.3 3.9 convolution_convert_fusion.1
  168.2 19.1 %fold3.1.branch_ref = f32[8,16,2304]{2,1,0:T(8,128)} custom-call(bf16[4,8,16,2304]{3,2,1,0:T(8,128)(2,1)} %bitcast.107), custom_call_target="tpu_custom_call" | custom-call | bytes 94371840 | tf_op jit(solution)/shard_map/fold3/pallas_call | solution.py:628
  187.4 229.5 %feed_forward.1 = (bf16[8,16,2304]{2,1,0:T(8,128)(2,1)}, f32[8,16,2304]{2,1,0:T(8,128)}, bf16[8,16,2304]{2,1,0:T(8,128)(2,1)}, f32[4,2304]{1,0:T(4,128)}, bf16[1...) custom-call(f32[8,16,2304]{2,1,0:T(8,128)} %fold3.1.branch_ref, bf16[8,16,2304]{2,1,0:T(8,128)(2,1)} %bitcast.96, ...), custom_call_target="tpu_custom_call" | custom-call | flops 48922361856 | bytes 524288000 | tf_op jit(solution)/shard_map/feed_forward/pallas_call | solution.py:1228
  418.1 16.0 %group8.1 = bf16[4,128,2304]{2,1,0:T(8,128)(2,1)} custom-call(bf16[128,2304]{1,0:T(8,128)(2,1)} %bitcast.116), custom_call_target="tpu_custom_call" | custom-call | bytes 94371840 | tf_op jit(solution)/shard_map/group8/pallas_call | solution.py:628
  434.2 3.8 convolution_convert_fusion.2
  438.0 20.2 %attend_back.1 = (bf16[4,128,512]{2,1,0:T(8,128)(2,1)}, bf16[8,4,128,512]{3,2,1,0:T(8,128)(2,1)}) custom-call(s32[1]{0:T(128)} %bitcast.here_ref, bf16[4,128,512]{2,1,0:T(8,128)(2,1)} %copy.38.q_ref, bf16[8,4,128,512]{3,2,1,0:T(8,128)(2,1)} %bitcast.100, s32[4,128,1]{2,1,0:T(8,128)} %copy.27.doc_ref, s32[2,16,1,128]{3,2,1,0:T(1,128)} %bitcast.120, ...), custom_call_target="tpu_custom_call" | custom-call | flops 2000000000 | bytes 83886080 | tf_op jit(solution)/shard_map/attend_back/pallas_call | solution.py:1435
  458.2 1.2 reshape.328
  460.1 3.9 fusion.2
  464.0 69.2 %reduce9.1 = (bf16[32,16,512]{2,1,0:T(8,128)(2,1)}, bf16[4,72,512]{2,1,0:T(8,128)(2,1)}) custom-call(bf16[8,32,16,512]{3,2,1,0:T(8,128)(2,1)} %bitcast.101, bf16[4,8,72,512]{3,2,1,0:T(8,128)(2,1)} %bitcast.103), custom_call_target="tpu_custom_call" | custom-call | bytes 262144000 | tf_op jit(solution)/shard_map/reduce9/pallas_call | solution.py:628
  533.3 1.2 reshape.331
  538.4 6.5 %fusion.1 = (f32[2304]{0:T(1024)S(1)}, bf16[512,2304]{1,0:T(8,128)(2,1)}) fusion(f32[512]{0:T(512)S(1)} %copy-done.18, bf16[4,128,2304]{2,1,0:T(8,128)(2,1)S(1)} %copy-done.1, bf16[512,1024]{0,1:T(8,128)(2,1)S(1)} %bitcast.112, bf16[1024,2304]{1,0:T(8,128)(2,1)} %bitcast.125), kind=kOutput, calls=%fused_computation.4 | convolution fusion | flops 2421815040 | bytes 10497024 | tf_op jit(solution)/shard_map/dot_general | solution.py:890
  545.7 4.2 convolution_convert_fusion
  549.9 59.8 %last10.1 = (f32[8,16,2304]{2,1,0:T(8,128)}, f32[8,16,2304]{2,1,0:T(8,128)}, f32[1,8,128]{2,1,0:T(8,128)}, bf16[4,72,512]{2,1,0:T(8,128)(2,1)}) custom-call(bf16[8,8,16,2304]{3,2,1,0:T(8,128)(2,1)} %bitcast.97, bf16[4,8,16,2304]{3,2,1,0:T(8,128)(2,1)} %bitcast.102, f32[8,4,1,8,128]{4,3,2,1,0:T(8,128)} %pad_bitcast_fusion.refs_2_, ...), custom_call_target="tpu_custom_call" | custom-call | bytes 188743680 | tf_op jit(solution)/shard_map/last10/pallas_call | solution.py:628
  609.7 1.2 convert_bitcast_fusion
  612.7 1.2 fusion.10
  614.0 3.0 convert_element_type.113
  617.0 4.9 convert_element_type.112
  (103 shorter events, 21.9 us)
Async XLA Ops:
  7.2 1.6 copy-start.14
  7.2 2.3 copy-start.19
  7.2 180.1 %all-gather.5.cloned.1.call-start = ((), (), s32[]{:S(2)}) async-start(), calls=%async_computation.3 | async-start | bytes 6635520 | tf_op jit(solution)/shard_map/all_gather | solution.py:1546
  7.9 179.4 %all-gather.3.cloned.1.call-start = ((), (), s32[]{:S(2)}) async-start(), calls=%async_computation.2 | async-start | bytes 13271040 | tf_op jit(solution)/shard_map/all_gather | solution.py:1545
  8.7 605.3 %reduce-scatter.5.cloned.1.call-start = ((), (), s32[]{:S(2)}) async-start(), calls=%async_computation.5 | async-start | bytes 6635520 | tf_op jit(solution)/shard_map/reduce_scatter | solution.py:1620
  62.8 6.3 %copy-start = (bf16[4,128,2304]{2,1,0:T(8,128)(2,1)S(1)}, bf16[4,128,2304]{2,1,0:T(8,128)(2,1)}, u32[]{:S(2)}) copy-start(bf16[4,128,2304]{2,1,0:T(8,128)(2,1)} %get-tuple-element.31) | copy-start | bytes 7077892
  64.0 5.7 copy-start.15
  69.2 3.9 copy-start.21
  69.8 5.9 copy-start.7
  76.8 1.8 copy-start.3
  150.3 14.0 %copy-start.22 = (bf16[4,8,72,512]{3,2,1,0:T(8,128)(2,1)S(1)}, bf16[4,8,72,512]{3,2,1,0:T(8,128)(2,1)}, u32[]{:S(2)}) copy-start(bf16[4,8,72,512]{3,2,1,0:T(8,128)(2,1)} %get-tuple-element.38) | copy-start | bytes 7077892
  416.9 200.1 %reduce-scatter.3.cloned.1.call-start = ((), (), s32[]{:S(2)}) async-start(), calls=%async_computation.4 | async-start | bytes 13271040 | tf_op jit(solution)/shard_map/reduce_scatter | solution.py:1617
  417.5 16.7 %copy-start.23 = (bf16[4,8,72,512]{3,2,1,0:T(8,128)(2,1)S(1)}, bf16[4,8,72,512]{3,2,1,0:T(8,128)(2,1)}, u32[]{:S(2)}) copy-start(bf16[4,8,72,512]{3,2,1,0:T(8,128)(2,1)} %get-tuple-element.38) | copy-start | bytes 7077892
  438.0 22.1 %copy-start.9 = (bf16[4,128,2304]{2,1,0:T(8,128)(2,1)S(1)}, bf16[4,128,2304]{2,1,0:T(8,128)(2,1)}, u32[]{:S(2)}) copy-start(bf16[4,128,2304]{2,1,0:T(8,128)(2,1)} %group8.1) | copy-start | bytes 7077892
  536.6 1.8 copy-start.1
  536.6 1.8 copy-start.18
  538.4 7.3 %copy-start.8 = (bf16[4,128,2304]{2,1,0:T(8,128)(2,1)S(1)}, bf16[4,128,2304]{2,1,0:T(8,128)(2,1)}, u32[]{:S(2)}) copy-start(bf16[4,128,2304]{2,1,0:T(8,128)(2,1)} %copy-done.7) | copy-start | bytes 7077892
  549.9 61.9 %copy-start.16 = (f32[2304]{0:T(1024)S(1)}, f32[2304]{0:T(1024)}, u32[]{:S(2)}) copy-start(f32[2304]{0:T(1024)} %copy-done.15) | copy-start | bytes 27652
  609.7 2.1 copy-start.2
  609.7 2.1 copy-start.5
  609.7 2.4 copy-start.20
  609.7 3.0 copy-start.11
  617.0 4.9 copy-start.13
  617.0 5.7 copy-start.12
  (5 other events, 4.9 us)
Sparse Core Ops, SparseCore 0:
  9.6 51.8 all-gather.4
  63.0 70.7 all-gather.2
  417.0 52.7 reduce-scatter.4
  472.3 85.1 reduce-scatter.2

commit v5 on v4

--- a/solution.py
+++ b/solution.py
@@ -542,26 +542,120 @@
     return [pltpu.SemaphoreType.DMA((3,)), pltpu.SemaphoreType.DMA((4,)), pltpu.SemaphoreType.DMA]
 
 
-def gather_group(place, src, out, sent, came, own):
-    copy = pltpu.make_async_copy(src, out.at[place.group], own)
-    copy.start()
+def gather_group(place, src, view, sent, came, own, through=None):
+    if not callable(view):
+        out = view
+        view = lambda g: out.at[g]
+    copy = pltpu.make_async_copy(src if through is None else through, view(place.group), own)
+    load = None if through is None else pltpu.make_async_copy(src, through, own)
     mine, other = place.group, 2 * place.core + (1 - place.half)
-    to_half = remote(src, out.at[mine], sent.at[0], came.at[mine], place.across())
-    to_core = remote(src, out.at[mine], sent.at[1], came.at[mine], place.partner())
+    to_half = remote(src, view(mine), sent.at[0], came.at[mine], place.across())
+    to_core = remote(src, view(mine), sent.at[1], came.at[mine], place.partner())
     to_half.start()
     to_core.start()
+    (load or copy).start()
     yield
-    remote(src, out.at[other], sent.at[0], came.at[other], place.across()).wait_recv()
-    relay = remote(out.at[other], out.at[other], sent.at[2], came.at[other], place.partner())
+    if load:
+        load.wait()
+        copy.start()
+    remote(src, view(other), sent.at[0], came.at[other], place.across()).wait_recv()
+    relay = remote(view(other), view(other), sent.at[2], came.at[other], place.partner())
     relay.start()
     yield
     for half in (0, 1):
         slot = 2 * (1 - place.core) + half
-        remote(src, out.at[slot], sent.at[0], came.at[slot], place.partner()).wait_recv()
+        remote(src, view(slot), sent.at[0], came.at[slot], place.partner()).wait_recv()
     to_half.wait_send()
     to_core.wait_send()
     relay.wait_send()
     copy.wait()
+
+
+def share_rows(ref, parts, p):
+    rows = ref.shape[0] // parts
+    return ref.at[pl.ds(p * rows, rows)]
+
+
+def gather_group_rows(place, src, out, parts, take):
+    def task(p, refs):
+        rows = src.shape[0] // parts
+        view = lambda g: out.at[g, pl.ds(p * rows, rows)]
+        return gather_group(place, share_rows(src, parts, p), view, *refs)
+
+    return [task(p, take(4)) for p in range(parts)]
+
+
+def gather_rows_scratch(value, parts):
+    through = pltpu.VMEM((value.shape[0] // parts, value.shape[1]), value.dtype)
+    return (gather_group_sems() + [through]) * parts
+
+
+def fold_rows_scratch(piece, parts):
+    rows, width = piece[0] // parts, piece[1]
+    bf16 = jnp.bfloat16
+    one = [
+        pltpu.VMEM((2, rows, width), bf16),
+        pltpu.VMEM((rows, width), bf16),
+        pltpu.VMEM((rows, width), bf16),
+        pltpu.VMEM((rows, width), bf16),
+        pltpu.VMEM((rows, width), jnp.float32),
+        pltpu.SemaphoreType.DMA((3,)),
+        pltpu.SemaphoreType.DMA((3,)),
+        pltpu.SemaphoreType.DMA((3,)),
+    ]
+    return one * parts
+
+
+def add_rows(out, *terms):
+    rows = slabs(out.shape[0])
+
+    def one(i, carry):
+        at = pl.ds(pl.multiple_of(i * rows, rows), rows)
+        total = terms[0][at].astype(jnp.float32)
+        for term in terms[1:]:
+            total = total + term[at].astype(jnp.float32)
+        out[at] = total.astype(out.dtype)
+        return carry
+
+    lax.fori_loop(0, out.shape[0] // rows, one, 0)
+
+
+def fold_rows(place, part, out, parts, take):
+    rows = out.shape[0] // parts
+    core, half = place.core, place.half
+    far, near = 2 * (1 - core) + (1 - half), 2 * (1 - core) + half
+    beside = 2 * core + (1 - half)
+
+    def task(p, from_core, from_half, held, mine, total, sent, came, local):
+        at = pl.ds(p * rows, rows)
+        first = remote(part.at[far, at], from_core.at[1], sent.at[0], came.at[0], place.partner())
+        second = remote(part.at[near, at], from_core.at[0], sent.at[1], came.at[1], place.partner())
+        third = remote(held, from_half, sent.at[2], came.at[2], place.across())
+        load_held = pltpu.make_async_copy(part.at[beside, at], held, local.at[0])
+        load_mine = pltpu.make_async_copy(part.at[place.group, at], mine, local.at[1])
+        store = pltpu.make_async_copy(total, out.at[at], local.at[2])
+        for copy in (first, load_held, second, load_mine):
+            copy.start()
+        yield
+        first.wait_recv()
+        load_held.wait()
+        add_rows(held, held, from_core.at[1])
+        third.start()
+        yield
+        second.wait_recv()
+        load_mine.wait()
+        third.wait_recv()
+        add_rows(total, mine, from_core.at[0], from_half)
+        store.start()
+        yield
+        for copy in (first, second, third):
+            copy.wait_send()
+        store.wait()
+
+    return [task(p, *take(8)) for p in range(parts)]
+
+
+ROW_PARTS = 3
 
 
 def reduce_group_scratch(piece, dtype):
@@ -623,13 +717,14 @@
     copy.wait()
 
 
-def transfer(name, number, body, ins, outs, scratch, moved, out_spaces=None):
+def transfer(name, number, body, ins, outs, scratch, moved, out_spaces=None, in_spaces=None):
     spaces = out_spaces or [pl.ANY] * len(outs)
+    in_spaces = in_spaces or [pltpu.VMEM] * len(ins)
     return pl.pallas_call(
         body,
         name=name,
         out_shape=outs,
-        in_specs=[pl.BlockSpec(memory_space=pltpu.VMEM)] * len(ins),
+        in_specs=[pl.BlockSpec(memory_space=space) for space in in_spaces],
         out_specs=[pl.BlockSpec(memory_space=space) for space in spaces],
         scratch_shapes=scratch,
         compiler_params=pltpu.CompilerParams(
@@ -694,12 +789,12 @@
         return taken
 
 
-def gather_first(qkv, out_parts, tokens, gains, docs, count, number):
-    names = 5
+def gather_first(qkv, out_parts, tokens, gains, docs, down, count, number):
+    names = 6
 
     def body(*refs):
-        qkv_ref, out_ref, tok_ref, gain_ref, doc_ref = refs[:names]
-        qkv_all, out_mine, tok_all, gain_all, doc_all = refs[names : 2 * names]
+        qkv_ref, out_ref, tok_ref, gain_ref, doc_ref, down_ref = refs[:names]
+        qkv_all, out_mine, tok_all, gain_all, doc_all, down_all = refs[names : 2 * names]
         gain_mine = refs[2 * names]
         take = Taker(refs[2 * names + 1 :])
         place = Place(count)
@@ -725,9 +820,15 @@
             doc_task(*take(3)),
             waiting(gather_group(place, tok_ref, tok_all, *take(3)), 2),
             waiting(exchange_group(place, out_ref, out_mine, *take(3)), 3),
+            *(
+                waiting(task, 2 + p, 4)
+                for p, task in enumerate(
+                    gather_group_rows(place, down_ref, down_all, ROW_PARTS, take)
+                )
+            ),
         )
 
-    ins = [qkv, out_parts, tokens, gains, docs]
+    ins = [qkv, out_parts, tokens, gains, docs, down]
     return transfer(
         f"first{number}",
         number,
@@ -739,6 +840,7 @@
             shape((GROUPS,) + tokens.shape, tokens.dtype),
             shape((GROUPS, count) + gains.shape, gains.dtype),
             shape((2,) + docs.shape, docs.dtype),
+            shape((GROUPS,) + down.shape, down.dtype),
         ],
         [pltpu.VMEM((count,) + gains.shape, gains.dtype)]
         + gather_blk_sems(count, 1)
@@ -746,19 +848,28 @@
         + gather_blk_sems(count)
         + [pltpu.SemaphoreType.DMA] * 3
         + gather_group_sems()
-        + exchange_group_sems(),
+        + exchange_group_sems()
+        + gather_rows_scratch(down, ROW_PARTS),
         (qkv.size + out_parts.size) * 2 * count,
+        None,
+        [pltpu.VMEM] * 5 + [pl.ANY],
     )
 
 
-def gather_second(kv, out_mine, count, number):
-    def body(kv_ref, out_ref, kv_all, out_all, *sems):
+def gather_second(kv, out_mine, gate_up, count, number):
+    def body(kv_ref, out_ref, gate_up_ref, kv_all, out_all, gate_up_all, *sems):
         take = Taker(sems)
         place = Place(count)
-        greet(place, blk=True)
+        greet(place, blk=True, core=True, half=True)
         together(
             gather_blk(place, kv_ref, kv_all, *take(3)),
             gather_blk(place, out_ref, lambda i: out_all.at[:, i], *take(3)),
+            *(
+                waiting(task, 2 + p, 4)
+                for p, task in enumerate(
+                    gather_group_rows(place, gate_up_ref, gate_up_all, ROW_PARTS, take)
+                )
+            ),
         )
 
     groups, rows, width = out_mine.shape
@@ -766,51 +877,69 @@
         f"gather{number}",
         number,
         body,
-        [kv, out_mine],
+        [kv, out_mine, gate_up],
         [
             shape((count,) + kv.shape, kv.dtype),
             shape((groups, count, rows, width), out_mine.dtype),
+            shape((GROUPS,) + gate_up.shape, gate_up.dtype),
         ],
-        gather_blk_sems(count) + gather_blk_sems(count),
+        gather_blk_sems(count) + gather_blk_sems(count) + gather_rows_scratch(gate_up, ROW_PARTS),
         (kv.size + out_mine.size) * 2 * count,
+        None,
+        [pltpu.VMEM, pltpu.VMEM, pl.ANY],
     )
 
 
-def reduce_middle(dkv_part, out_part, count, number):
+def reduce_middle(dkv_part, out_part, gate_up_part, count, number):
     dkv_piece = dkv_part.shape[1:]
     out_piece = out_part.shape[:1] + out_part.shape[2:]
 
-    def body(dkv_ref, out_ref, dkv_sum, out_sum, *scratch):
+    gate_up_piece = gate_up_part.shape[1:]
+
+    def body(dkv_ref, out_ref, gate_up_ref, dkv_sum, out_sum, gate_up_sum, *scratch):
         take = Taker(scratch)
         place = Place(count)
-        greet(place, blk=True)
+        greet(place, blk=True, core=True, half=True)
         together(
             reduce_blk(place, dkv_ref, dkv_sum, *take(REDUCE_REFS)),
             reduce_blk(place, lambda i: out_ref.at[:, i], out_sum, *take(REDUCE_REFS)),
+            *(
+                waiting(task, *rounds)
+                for rounds, task in zip(
+                    ((6, 5, 5), (8, 5, 3), (10, 6, 0)),
+                    fold_rows(place, gate_up_ref, gate_up_sum, ROW_PARTS, take),
+                )
+            ),
         )
 
     return transfer(
         f"reduce{number}",
         number,
         body,
-        [dkv_part, out_part],
-        [shape(dkv_piece, jnp.bfloat16), shape(out_piece, jnp.bfloat16)],
+        [dkv_part, out_part, gate_up_part],
+        [
+            shape(dkv_piece, jnp.bfloat16),
+            shape(out_piece, jnp.bfloat16),
+            shape(gate_up_piece, jnp.float32),
+        ],
         reduce_blk_scratch(count, dkv_piece, jnp.bfloat16)
-        + reduce_blk_scratch(count, out_piece, jnp.bfloat16),
+        + reduce_blk_scratch(count, out_piece, jnp.bfloat16)
+        + fold_rows_scratch(gate_up_piece, ROW_PARTS),
         (dkv_part.size + out_part.size) * 2,
-        [pltpu.VMEM] * 2,
+        [pltpu.VMEM, pltpu.VMEM, pl.ANY],
+        [pltpu.VMEM, pltpu.VMEM, pl.ANY],
     )
 
 
-def reduce_last(qkv_part, norm_part, gain_part, out_sum, count, number):
+def reduce_last(qkv_part, norm_part, gain_part, out_sum, down_part, count, number):
     gain_piece = gain_part.shape[1:]
     qkv_piece, norm_piece = qkv_part.shape[1:], norm_part.shape[1:]
 
     def body(*refs):
-        qkv_ref, norm_ref, gain_ref, out_ref = refs[:4]
-        qkv_sum, norm_sum, gain_sum, out_all = refs[4:8]
-        gain_mine = refs[8]
-        take = Taker(refs[9:])
+        qkv_ref, norm_ref, gain_ref, out_ref, down_ref = refs[:5]
+        qkv_sum, norm_sum, gain_sum, out_all, down_sum = refs[5:10]
+        gain_mine = refs[10]
+        take = Taker(refs[11:])
         place = Place(count)
         greet(place, blk=True, core=True, half=True, corner=True)
 
@@ -825,27 +954,37 @@
             main,
             waiting(exchange_group(place, out_ref, out_all, *take(3)), 16),
             waiting(reduce_group(place, norm_ref, norm_sum, *take(5)), 7, 9),
+            *(
+                waiting(task, *rounds)
+                for rounds, task in zip(
+                    ((7, 7, 2), (8, 8, 0), (9, 9, 0)),
+                    fold_rows(place, down_ref, down_sum, ROW_PARTS, take),
+                )
+            ),
         )
 
     return transfer(
         f"last{number}",
         number,
         body,
-        [qkv_part, norm_part, gain_part, out_sum],
+        [qkv_part, norm_part, gain_part, out_sum, down_part],
         [
             shape(qkv_piece, jnp.float32),
             shape(norm_piece, jnp.float32),
             shape(gain_piece[1:], jnp.float32),
             shape(out_sum.shape, jnp.bfloat16),
+            shape(down_part.shape[1:], jnp.float32),
         ],
         [pltpu.VMEM(gain_piece, jnp.float32)]
         + reduce_blk_scratch(count, qkv_piece, jnp.bfloat16)
         + reduce_blk_scratch(count, gain_piece, jnp.float32, 1)
         + reduce_group_scratch(gain_piece[1:], jnp.float32)
         + exchange_group_sems()
-        + reduce_group_scratch(norm_piece, jnp.bfloat16),
+        + reduce_group_scratch(norm_piece, jnp.bfloat16)
+        + fold_rows_scratch(down_part.shape[1:], ROW_PARTS),
         qkv_part.size * 2,
-        [pltpu.VMEM] * 4,
+        [pltpu.VMEM] * 4 + [pl.ANY],
+        [pltpu.VMEM] * 4 + [pl.ANY],
     )
 
 
@@ -1542,9 +1681,6 @@
     slab = slabs(rows)
     piece = (rows // slab, slab, width)
 
-    gate_up_all = lax.all_gather(gate_up_weight, ("dp", "head"), axis=0, tiled=True)
-    down_all = lax.all_gather(down_weight, ("dp", "head"), axis=0, tiled=True)
-
     gain_rows = norm_gains.shape[0]
     gain_lanes = -(-gain_rows // 128) * 128
     gains_sent = jnp.pad(
@@ -1555,9 +1691,17 @@
     qkv_rows = qkv_weight.shape[0]
     qkv_slab = slabs(qkv_rows)
     qkv_piece = (qkv_rows // qkv_slab, qkv_slab, width)
-    qkv_all, out_mine, tokens_all, gains_all, docs_all = gather_first(
-        qkv_weight, out_sent, tokens[0], gains_sent, segments.reshape(-1, 128), count, 1
+    qkv_all, out_mine, tokens_all, gains_all, docs_all, down_all = gather_first(
+        qkv_weight,
+        out_sent,
+        tokens[0],
+        gains_sent,
+        segments.reshape(-1, 128),
+        down_weight,
+        count,
+        1,
     )
+    down_all = down_all.reshape(-1, width)
     gains = jnp.transpose(gains_all[:, :, :4, :gain_rows], (2, 0, 1, 3)).reshape(4, width)
     qkv_head = qkv_all.reshape(count * qkv_rows, width)
     docs = docs_all.reshape(2, 2, count, rows)
@@ -1578,7 +1722,8 @@
     own_kv = sent[:, REPS:].reshape(group_rows, 2 * HEAD_DIM)
     kv_slab = slabs(group_rows)
     kv_piece = (group_rows // kv_slab, kv_slab, 2 * HEAD_DIM)
-    kv, out_all = gather_second(own_kv, out_mine, count, 2)
+    kv, out_all, gate_up_all = gather_second(own_kv, out_mine, gate_up_weight, count, 2)
+    gate_up_all = gate_up_all.reshape(-1, 2 * width)
     kv = kv.reshape(count, GROUPS, rows, 2 * HEAD_DIM)
     out_head = out_all.reshape(width, head_width)
     attn, attended, totals = attention_forward(here_one, queries, kv, own_doc, key_doc)
@@ -1614,12 +1759,6 @@
         ) = feed_forward_apart(
             branch_slabs, inputs, cotangent, gains, gate_up_all, down_all, count, piece
         )
-    gate_up_grad = lax.psum_scatter(
-        gate_up_part, ("dp", "head"), scatter_dimension=0, tiled=True
-    ).astype(jnp.float32)
-    down_grad = lax.psum_scatter(
-        down_part, ("dp", "head"), scatter_dimension=0, tiled=True
-    ).astype(jnp.float32)
     branch_all = all_gather_group(branch_grad, 8).reshape(group_rows, width)
     attn_grad = dot(branch_all, out_head, PLAIN).astype(bf16).reshape(GROUPS, rows, head_width)
     out_part = dot(branch_all, attn, FIRST).astype(bf16)
@@ -1627,7 +1766,13 @@
     dq, dkv_part = attention_backward(
         here_one, queries, kv, own_doc, key_doc, attn_grad, attended, totals
     )
-    dkv, out_sum = reduce_middle(dkv_part.reshape((count,) + kv_piece), out_part, count, 9)
+    dkv, out_sum, gate_up_grad = reduce_middle(
+        dkv_part.reshape((count,) + kv_piece),
+        out_part,
+        gate_up_part.reshape((GROUPS,) + gate_up_weight.shape),
+        count,
+        9,
+    )
     sent_grad = jnp.concatenate(
         [
             dq.reshape(group_rows, REPS, HEAD_DIM),
@@ -1648,11 +1793,12 @@
     gain_part = jnp.stack([gain_grad_one, gain_grad_two, gain_grad_three, gain_grad_four])
     gain_part = jnp.transpose(gain_part.reshape(4, GROUPS, count, gain_rows), (2, 1, 0, 3))
     gain_part = jnp.pad(gain_part, ((0, 0), (0, 0), (0, 4), (0, gain_lanes - gain_rows)))
-    qkv_grad, norm_one_grad, gain_grad, out_grad = reduce_last(
+    qkv_grad, norm_one_grad, gain_grad, out_grad, down_grad = reduce_last(
         qkv_part.reshape((count,) + qkv_piece),
         norm_one_part.astype(bf16).reshape((GROUPS,) + piece),
         gain_part[:, :, None],
         out_sum,
+        down_part.reshape((GROUPS,) + down_weight.shape),
         count,
         10,
     )

time: 632 us -> 627 us (level)
  between operations: 14.3 us -> 1.06 us
  local copies, waits for them, and re-layouts: 20.5 us -> 30.1 us
  Pallas kernels: 550 us -> 558 us
  other arithmetic: 18.5 us -> 11.5 us
    pallas_call x6, Pallas kernels: 286 us -> 297 us  [transfer(): pl.pallas_call(body, name=name, out_shape=outs, in_specs=[pl.BlockSpec(me...]
    convert_element_type x2 -> x0, other arithmetic: 7.89 us -> none  [the longest x1 4.9 us: shards(): gate_up_grad = lax.psum_scatter(gate_up_part, ('dp', 'head'), scatter_dim...]
    unnamed x50 -> x48, local copies, waits for them, and re-layouts: 7.42 us -> 13.1 us
  transfers between devices with their start and end apart: 4 -> 0, of which waited for: 0 -> 0; matrix products, arithmetic and copies ran while one was open for 8% -> 0% of each run, Pallas kernels for 51% -> 0%
where the time goes in v5:
time: 627 us; the launch traced here: 626 us
  Pallas kernels  558 us (89%)
  local copies, waits for them, and re-layouts  30.1 us (5%)
  matrix products  24.9 us (4%)
  other arithmetic  11.5 us (2%)
    pallas_call x6, Pallas kernels, transfer(): pl.pallas_call(body, name=name, out_shape=outs, in_specs=[pl.BlockSpec(me...  297 us
    pallas_call x1, Pallas kernels, feed_forward(): pl.pallas_call(functools.partial(feed_forward_kernel, count), name='feed_...  227 us
    dot_general x6, matrix products, dot(): lax.dot_general(left, right, (contract, ((), ())), preferred_element_type...  24.9 us
    pallas_call x1, Pallas kernels, attention_backward(): pl.pallas_call(functools.partial(attention_backward_kernel, count), name=...  19.8 us
    pallas_call x1, Pallas kernels, attention_forward(): pl.pallas_call(functools.partial(attention_forward_kernel, count), name='...  13.9 us
    unnamed x48, local copies, waits for them, and re-layouts  13.1 us

profile of v5, /device:TPU:20, one launch (start us, length us, event | category | flops | bytes accessed | tf_op | source)
XLA Modules:
  0.0 625.8 jit_solution(13669664183044199860)
XLA Ops:
  2.0 1.7 copy.44
  5.7 53.6 %first1.1 = (bf16[8,128,2304]{2,1,0:T(8,128)(2,1)}, bf16[4,72,512]{2,1,0:T(8,128)(2,1)}, bf16[4,128,2304]{2,1,0:T(8,128)(2,1)}, f32[4,8,8,128]{3,2,1,0:T(8,128)}...) custom-call(bf16[128,2304]{1,0:T(8,128)(2,1)} %refs_0_.1, bf16[4,72,512]{2,1,0:T(8,128)(2,1)} %bitcast.117, ...), custom_call_target="tpu_custom_call" | custom-call | bytes 283115520 | tf_op jit(solution)/shard_map/first1/pallas_call | solution.py:723
  60.3 1.3 constant_dynamic-slice_fusion
  61.7 2.2 multiply_reduce_fusion
  65.3 1.5 copy.27.doc_ref
  67.5 2.6 copy-done.19
  70.1 2.6 fusion.15
  75.9 71.2 %gather2.1 = (bf16[8,512,512]{2,1,0:T(8,128)(2,1)}, bf16[4,8,72,512]{3,2,1,0:T(8,128)(2,1)}, bf16[4,288,4608]{2,1,0:T(8,128)(2,1)}) custom-call(bf16[512,512]{1,0:T(8,128)(2,1)} %copy.39.kv_ref, bf16[4,72,512]{2,1,0:T(8,128)(2,1)} %get-tuple-element.38.out_ref, bf16[288,4608]{1,0:T(8,128)(2,1)} %gate_up_ref.1), custom_call_target="tpu_custom_call" | custom-call | bytes 262144000 | tf_op jit(solution)/shard_map/gather2/pallas_call | solution.py:723
  147.1 13.9 %attend.1 = (bf16[4,128,512]{2,1,0:T(8,128)(2,1)}, f32[4,128,512]{2,1,0:T(8,128)}, f32[4,256,1]{2,1,0:T(8,128)}) custom-call(s32[1]{0:T(128)} %bitcast.here_ref, bf16[4,128,512]{2,1,0:T(8,128)(2,1)} %copy.38.q_ref, bf16[8,4,128,512]{3,2,1,0:T(8,128)(2,1)} %bitcast.105, s32[4,128,1]{2,1,0:T(8,128)} %copy.27.doc_ref, s32[2,16,1,128]{3,2,1,0:T(1,128)} %bitcast.125), custom_call_target="tpu_custom_call" | custom-call | flops 1000000000 | bytes 41943040 | tf_op jit(solution)/shard_map/attend/pallas_call | solution.py:1547
  161.0 3.9 convolution_convert_fusion.1
  164.9 20.7 %fold3.1.branch_ref = f32[8,16,2304]{2,1,0:T(8,128)} custom-call(bf16[4,8,16,2304]{3,2,1,0:T(8,128)(2,1)} %bitcast.111), custom_call_target="tpu_custom_call" | custom-call | bytes 94371840 | tf_op jit(solution)/shard_map/fold3/pallas_call | solution.py:723
  185.6 227.4 %feed_forward.1 = (bf16[8,16,2304]{2,1,0:T(8,128)(2,1)}, f32[8,16,2304]{2,1,0:T(8,128)}, bf16[8,16,2304]{2,1,0:T(8,128)(2,1)}, f32[4,2304]{1,0:T(4,128)}, bf16[1...) custom-call(f32[8,16,2304]{2,1,0:T(8,128)} %fold3.1.branch_ref, bf16[8,16,2304]{2,1,0:T(8,128)(2,1)} %bitcast.101, ...), custom_call_target="tpu_custom_call" | custom-call | flops 48922361856 | bytes 524288000 | tf_op jit(solution)/shard_map/feed_forward/pallas_call | solution.py:1367
  414.1 18.1 %group8.1 = bf16[4,128,2304]{2,1,0:T(8,128)(2,1)} custom-call(bf16[128,2304]{1,0:T(8,128)(2,1)} %bitcast.122), custom_call_target="tpu_custom_call" | custom-call | bytes 94371840 | tf_op jit(solution)/shard_map/group8/pallas_call | solution.py:723
  432.2 3.8 convolution_convert_fusion.2
  436.1 19.8 %attend_back.1 = (bf16[4,128,512]{2,1,0:T(8,128)(2,1)}, bf16[8,4,128,512]{3,2,1,0:T(8,128)(2,1)}) custom-call(s32[1]{0:T(128)} %bitcast.here_ref, bf16[4,128,512]{2,1,0:T(8,128)(2,1)} %copy.38.q_ref, bf16[8,4,128,512]{3,2,1,0:T(8,128)(2,1)} %bitcast.106, s32[4,128,1]{2,1,0:T(8,128)} %copy.27.doc_ref, s32[2,16,1,128]{3,2,1,0:T(1,128)} %bitcast.126, ...), custom_call_target="tpu_custom_call" | custom-call | flops 2000000000 | bytes 83886080 | tf_op jit(solution)/shard_map/attend_back/pallas_call | solution.py:1574
  457.9 3.9 fusion.2
  461.7 71.4 %reduce9.1 = (bf16[32,16,512]{2,1,0:T(8,128)(2,1)}, bf16[4,72,512]{2,1,0:T(8,128)(2,1)}, f32[288,4608]{1,0:T(8,128)}) custom-call(bf16[8,32,16,512]{3,2,1,0:T(8,128)(2,1)} %bitcast.107, bf16[4,8,72,512]{3,2,1,0:T(8,128)(2,1)} %bitcast.113, bf16[4,288,4608]{2,1,0:T(8,128)(2,1)} %bitcast.99), custom_call_target="tpu_custom_call" | custom-call | bytes 262144000 | tf_op jit(solution)/shard_map/reduce9/pallas_call | solution.py:723
  538.3 6.5 %fusion.1 = (f32[2304]{0:T(1024)S(1)}, bf16[512,2304]{1,0:T(8,128)(2,1)}) fusion(f32[512]{0:T(512)S(1)} %copy-done.18, bf16[4,128,2304]{2,1,0:T(8,128)(2,1)S(1)} %copy-done.1, bf16[512,1024]{0,1:T(8,128)(2,1)S(1)} %bitcast.118, bf16[1024,2304]{1,0:T(8,128)(2,1)} %bitcast.133), kind=kOutput, calls=%fused_computation.4 | convolution fusion | flops 2421815040 | bytes 10497024 | tf_op jit(solution)/shard_map/dot_general | solution.py:1029
  545.6 4.2 convolution_convert_fusion
  549.8 62.0 %last10.1 = (f32[8,16,2304]{2,1,0:T(8,128)}, f32[8,16,2304]{2,1,0:T(8,128)}, f32[1,8,128]{2,1,0:T(8,128)}, bf16[4,72,512]{2,1,0:T(8,128)(2,1)}, f32[288,2304]{1,0:T(8,128)}) custom-call(bf16[8,8,16,2304]{3,2,1,0:T(8,128)(2,1)} %bitcast.103, bf16[4,8,16,2304]{3,2,1,0:T(8,128)(2,1)} %bitcast.112, f32[8,4,1,8,128]{4,3,2,1,0:T(8,128)} %pad_bitcast_fusion.refs_2_, ...), custom_call_target="tpu_custom_call" | custom-call | bytes 188743680 | tf_op jit(solution)/shard_map/last10/pallas_call | solution.py:723
  611.9 1.4 slice_bitcast_fusion.1
  613.2 1.6 fusion.7
  618.9 5.4 copy.51
  624.3 1.5 copy.52
  (87 shorter events, 22.4 us)
Async XLA Ops:
  4.7 68.3 %copy-start.3 = (f32[512,256]{0,1:T(8,128)}, f32[512,256]{0,1:T(8,128)S(1)}, u32[]{:S(2)}) copy-start(f32[512,256]{0,1:T(8,128)S(1)} %pad_maximum_fusion.2) | copy-start | bytes 1572868
  59.3 7.6 %copy-start = (bf16[4,128,2304]{2,1,0:T(8,128)(2,1)S(1)}, bf16[4,128,2304]{2,1,0:T(8,128)(2,1)}, u32[]{:S(2)}) copy-start(bf16[4,128,2304]{2,1,0:T(8,128)(2,1)} %get-tuple-element.35) | copy-start | bytes 7077892
  64.6 2.9 copy-start.16
  66.9 3.2 copy-start.19
  67.5 5.2 copy-start.8
  147.1 14.0 %copy-start.20 = (bf16[4,8,72,512]{3,2,1,0:T(8,128)(2,1)S(1)}, bf16[4,8,72,512]{3,2,1,0:T(8,128)(2,1)}, u32[]{:S(2)}) copy-start(bf16[4,8,72,512]{3,2,1,0:T(8,128)(2,1)} %get-tuple-element.42) | copy-start | bytes 7077892
  413.0 19.2 %copy-start.21 = (bf16[4,8,72,512]{3,2,1,0:T(8,128)(2,1)S(1)}, bf16[4,8,72,512]{3,2,1,0:T(8,128)(2,1)}, u32[]{:S(2)}) copy-start(bf16[4,8,72,512]{3,2,1,0:T(8,128)(2,1)} %get-tuple-element.42) | copy-start | bytes 7077892
  436.1 21.8 %copy-start.10 = (bf16[4,128,2304]{2,1,0:T(8,128)(2,1)S(1)}, bf16[4,128,2304]{2,1,0:T(8,128)(2,1)}, u32[]{:S(2)}) copy-start(bf16[4,128,2304]{2,1,0:T(8,128)(2,1)} %group8.1) | copy-start | bytes 7077892
  535.1 0.8 copy-start.6
  535.3 1.1 copy-start.4
  535.3 1.2 copy-start.11
  536.5 0.9 slice-start
  536.5 1.8 copy-start.1
  536.5 1.8 copy-start.18
  538.3 7.3 %copy-start.9 = (bf16[4,128,2304]{2,1,0:T(8,128)(2,1)S(1)}, bf16[4,128,2304]{2,1,0:T(8,128)(2,1)}, u32[]{:S(2)}) copy-start(bf16[4,128,2304]{2,1,0:T(8,128)(2,1)} %copy-done.8) | copy-start | bytes 7077892
  549.8 63.4 %copy-start.2 = (bf16[1,128,2304]{2,1,0:T(8,128)(2,1)S(1)}, bf16[1,128,2304]{2,1,0:T(8,128)(2,1)}, u32[]{:S(2)}) copy-start(bf16[1,128,2304]{2,1,0:T(8,128)(2,1)} %param.8) | copy-start | bytes 1769476
  549.8 63.4 %copy-start.17 = (f32[2304]{0:T(1024)S(1)}, f32[2304]{0:T(1024)}, u32[]{:S(2)}) copy-start(f32[2304]{0:T(1024)} %copy-done.16) | copy-start | bytes 27652
  549.8 65.1 %copy-start.12 = (f32[8,16,2304]{2,1,0:T(8,128)S(1)}, f32[8,16,2304]{2,1,0:T(8,128)}, u32[]{:S(2)}) copy-start(f32[8,16,2304]{2,1,0:T(8,128)} %get-tuple-element.46) | copy-start | bytes 3538948
  611.9 3.0 copy-start.5
  613.2 2.9 copy-start.15
  614.9 2.2 copy-start.14
  616.1 1.8 copy-start.13
  618.9 5.4 copy-start.7

commit v6 on v5

--- a/solution.py
+++ b/solution.py
@@ -856,37 +856,273 @@
     )
 
 
-def gather_second(kv, out_mine, gate_up, count, number):
-    def body(kv_ref, out_ref, gate_up_ref, kv_all, out_all, gate_up_all, *sems):
-        take = Taker(sems)
+def attend_block(count, g, here, q_ref, kv_ref, doc_ref, key_doc_ref, attn_ref, full_ref, total_ref):
+    rows = q_ref.shape[1]
+    sequence, half = g // 2, g % 2
+    block = half * count + here
+    q2, position, doc = stacked_queries(g, block, q_ref, doc_ref)
+
+    def one(key_block, carry):
+        total, acc = carry
+        key_half = (key_block >= count).astype(jnp.int32)
+        at = pl.ds(pl.multiple_of((2 * sequence + key_half) * rows, rows), rows)
+        kv = kv_ref.at[key_block - key_half * count, at]
+        _, weights = attention_scores(
+            q2, kv[:, :HEAD_DIM], position, doc, key_block, key_doc_ref[sequence, key_block], rows
+        )
+        total = total + jnp.sum(weights, axis=-1, keepdims=True)
+        acc = acc + jnp.dot(
+            weights.astype(jnp.bfloat16), kv[:, HEAD_DIM:], preferred_element_type=jnp.float32
+        )
+        return total, acc
+
+    start = (
+        jnp.zeros((REPS * rows, 1), jnp.float32),
+        jnp.zeros((REPS * rows, HEAD_DIM), jnp.float32),
+    )
+    total, acc = lax.fori_loop(jnp.maximum(block - count, 0), block + 1, one, start)
+    attended = acc / total
+    attended = jnp.concatenate([attended[:rows], attended[rows:]], axis=1)
+    full_ref[g] = attended
+    attn_ref[g] = attended.astype(jnp.bfloat16)
+    total_ref[g] = total
+
+
+def stacked_queries(g, block, q_ref, doc_ref):
+    rows = q_ref.shape[1]
+    q2 = jnp.concatenate([q_ref[g, :, :HEAD_DIM], q_ref[g, :, HEAD_DIM:]], axis=0)
+    inside = lax.broadcasted_iota(jnp.int32, (rows, 1), 0)
+    position = block * rows + jnp.concatenate([inside, inside], axis=0)
+    doc = jnp.concatenate([doc_ref[g], doc_ref[g]], axis=0)
+    return q2, position, doc
+
+
+def gather_attend(kv, out_mine, gate_up, queries, doc, key_doc, count, number):
+    def body(*refs):
+        kv_ref, out_ref, gate_up_ref, q_ref, doc_ref, key_doc_ref = refs[:6]
+        kv_all, out_all, gate_up_all, attn_ref, full_ref, total_ref = refs[6:12]
+        take = Taker(refs[12:])
         place = Place(count)
         greet(place, blk=True, core=True, half=True)
-        together(
-            gather_blk(place, kv_ref, kv_all, *take(3)),
-            gather_blk(place, out_ref, lambda i: out_all.at[:, i], *take(3)),
-            *(
-                waiting(task, 2 + p, 4)
-                for p, task in enumerate(
-                    gather_group_rows(place, gate_up_ref, gate_up_all, ROW_PARTS, take)
-                )
-            ),
-        )
-
-    groups, rows, width = out_mine.shape
+        gathers = (
+            GatherBlk(place, kv_ref, lambda i: kv_all.at[i], *take(3)),
+            GatherBlk(place, out_ref, lambda i: out_all.at[:, i], *take(3)),
+        )
+        groups = gather_group_rows(place, gate_up_ref, gate_up_all, ROW_PARTS, take)
+        for gather in gathers:
+            gather.start()
+        for task in groups:
+            next(task)
+        for k in range(1, place.outer):
+            for gather in gathers:
+                gather.pass_on(k)
+            if k == place.outer - 2:
+                for gather in gathers:
+                    gather.pass_extra(1)
+                next(groups[0])
+        for gather in gathers:
+            gather.pass_extra(place.outer - 1)
+        next(groups[1])
+        gathers[0].copy.wait()
+        for k in range(place.outer):
+            gathers[0].beside_arrived(k)
+
+        def attend(g, carry):
+            attend_block(
+                count,
+                g,
+                place.here,
+                q_ref,
+                kv_all,
+                doc_ref,
+                key_doc_ref,
+                attn_ref,
+                full_ref,
+                total_ref,
+            )
+            return carry
+
+        lax.fori_loop(0, GROUPS, attend, 0)
+        next(groups[2])
+        gathers[1].copy.wait()
+        for k in range(place.outer):
+            gathers[1].beside_arrived(k)
+        for gather in gathers:
+            gather.finish()
+        together(*groups)
+
+    groups, out_rows, width = out_mine.shape
+    rows = queries.shape[1]
     return transfer(
-        f"gather{number}",
+        f"attend{number}",
         number,
         body,
-        [kv, out_mine, gate_up],
+        [kv, out_mine, gate_up, queries, doc, key_doc],
         [
             shape((count,) + kv.shape, kv.dtype),
-            shape((groups, count, rows, width), out_mine.dtype),
+            shape((groups, count, out_rows, width), out_mine.dtype),
             shape((GROUPS,) + gate_up.shape, gate_up.dtype),
+            shape((GROUPS, rows, width), jnp.bfloat16),
+            shape((GROUPS, rows, width), jnp.float32),
+            shape((GROUPS, REPS * rows, 1), jnp.float32),
         ],
         gather_blk_sems(count) + gather_blk_sems(count) + gather_rows_scratch(gate_up, ROW_PARTS),
         (kv.size + out_mine.size) * 2 * count,
-        None,
-        [pltpu.VMEM, pltpu.VMEM, pl.ANY],
+        [pltpu.VMEM, pl.ANY, pl.ANY, pltpu.VMEM, pltpu.VMEM, pltpu.VMEM],
+        [pltpu.VMEM, pltpu.VMEM, pl.ANY, pltpu.VMEM, pltpu.VMEM, pltpu.VMEM],
+    )
+
+
+def attend_back_block(
+    count, g, here, q_ref, kv_ref, doc_ref, key_doc_ref, grad_ref, full_ref, total_ref, dq_ref, key_acc
+):
+    rows = q_ref.shape[1]
+    sequence, half = g // 2, g % 2
+    block = half * count + here
+    q2, position, doc = stacked_queries(g, block, q_ref, doc_ref)
+    total = total_ref[g]
+    grad = grad_ref[g].astype(jnp.float32)
+    grad2 = jnp.concatenate([grad[:, :HEAD_DIM], grad[:, HEAD_DIM:]], axis=0)
+    full2 = jnp.concatenate([full_ref[g, :, :HEAD_DIM], full_ref[g, :, HEAD_DIM:]], axis=0)
+    total_grad = -jnp.sum(grad2 * full2, axis=-1, keepdims=True) / total
+    sums_grad = (grad2 / total).astype(jnp.bfloat16)
+
+    def one(key_block, acc):
+        key_half = (key_block >= count).astype(jnp.int32)
+        inner = key_block - key_half * count
+        at = pl.ds(pl.multiple_of((2 * sequence + key_half) * rows, rows), rows)
+        kv = kv_ref.at[inner, at]
+        keys = kv[:, :HEAD_DIM]
+        capped, weights = attention_scores(
+            q2, keys, position, doc, key_block, key_doc_ref[sequence, key_block], rows
+        )
+        exp_grad = dot(sums_grad, kv[:, HEAD_DIM:], LAST)
+        raw_grad = (
+            weights * (exp_grad + total_grad) * (1.0 - capped * capped) * SCORE_SCALE
+        ).astype(jnp.bfloat16)
+        slot = inner * 2 + key_half
+        key_acc[slot, :, :HEAD_DIM] += dot(raw_grad, q2, FIRST)
+        key_acc[slot, :, HEAD_DIM:] += dot(weights.astype(jnp.bfloat16), sums_grad, FIRST)
+        return acc + dot(raw_grad, keys, PLAIN)
+
+    dq = lax.fori_loop(
+        jnp.maximum(block - count, 0),
+        block + 1,
+        one,
+        jnp.zeros((REPS * rows, HEAD_DIM), jnp.float32),
+    )
+    dq_ref[g] = jnp.concatenate([dq[:rows], dq[rows:]], axis=1).astype(jnp.bfloat16)
+
+
+def attend_back_fits(count):
+    return count == 8
+
+
+def attend_back_reduce(
+    queries, kv, doc, key_doc, grad, full, totals, out_part, gate_up_part, kv_piece, count, number
+):
+    out_piece = out_part.shape[:1] + out_part.shape[2:]
+    gate_up_piece = gate_up_part.shape[1:]
+    rows = queries.shape[1]
+    steps = rows // kv_piece[1]
+    bf16 = jnp.bfloat16
+
+    def body(*refs):
+        q_ref, kv_ref, doc_ref, key_doc_ref, grad_ref, full_ref, total_ref = refs[:7]
+        out_ref, gate_up_ref = refs[7:9]
+        dq_ref, dkv_sum, out_sum, gate_up_sum, dkv_part, key_acc = refs[9:15]
+        take = Taker(refs[15:])
+        place = Place(count)
+        greet(place, blk=True, core=True, half=True)
+        dkv = ReduceBlk(place, lambda i: dkv_part.at[i], dkv_sum, *take(REDUCE_REFS))
+        out = ReduceBlk(place, lambda i: out_ref.at[:, i], out_sum, *take(REDUCE_REFS))
+        folds = fold_rows(place, gate_up_ref, gate_up_sum, ROW_PARTS, take)
+        out_events = out.events()
+
+        def back(g):
+            attend_back_block(
+                count,
+                g,
+                place.here,
+                q_ref,
+                kv_ref,
+                doc_ref,
+                key_doc_ref,
+                grad_ref,
+                full_ref,
+                total_ref,
+                dq_ref,
+                key_acc,
+            )
+
+        def clear(i, carry):
+            key_acc[i] = jnp.zeros(key_acc.shape[1:], jnp.float32)
+            return carry
+
+        def put(sequence):
+            def one(i, carry):
+                for k in (0, 1):
+                    value = key_acc[i * 2 + k].astype(bf16).reshape((steps,) + kv_piece[1:])
+                    dkv_part[i, pl.ds((2 * sequence + k) * steps, steps)] = value
+                return carry
+
+            lax.fori_loop(0, count, one, 0)
+
+        out.start()
+        for fold in folds:
+            next(fold)
+        lax.fori_loop(0, 2 * count, clear, 0)
+        back(0)
+        next(folds[0])
+        out_events[0]()
+        back(1)
+        put(0)
+        out_events[1]()
+        out_events[2]()
+        next(folds[1])
+        lax.fori_loop(0, 2 * count, clear, 0)
+        back(2)
+        out_events[3]()
+        back(3)
+        put(1)
+        dkv.start()
+        dkv_events = dkv.events()
+        order = [(out_events, i) for i in range(4, 8)]
+        order += [(folds, 2), (dkv_events, 0), (dkv_events, 1), (dkv_events, 2)]
+        order += [(out_events, 8), (out_events, 9), (dkv_events, 3), (dkv_events, 4)]
+        order += [(folds, 0), (dkv_events, 5), (dkv_events, 6), (folds, 1)]
+        order += [(dkv_events, 7), (dkv_events, 8), (dkv_events, 9), (folds, 2)]
+        for events, i in order:
+            if events is folds:
+                next(folds[i])
+            else:
+                events[i]()
+        out.finish()
+        dkv.finish()
+        together(*folds)
+
+    vmem = pltpu.VMEM
+    return transfer(
+        f"attend_back{number}",
+        number,
+        body,
+        [queries, kv, doc, key_doc, grad, full, totals, out_part, gate_up_part],
+        [
+            shape(queries.shape, bf16),
+            shape(kv_piece, bf16),
+            shape(out_piece, bf16),
+            shape(gate_up_piece, jnp.float32),
+        ],
+        [
+            vmem((count,) + kv_piece, bf16),
+            vmem((2 * count, rows, 2 * HEAD_DIM), jnp.float32),
+        ]
+        + reduce_blk_scratch(count, kv_piece, bf16)
+        + reduce_blk_scratch(count, out_piece, bf16)
+        + fold_rows_scratch(gate_up_piece, ROW_PARTS),
+        (kv.size + out_part.size) * 2,
+        [vmem, vmem, vmem, pl.ANY],
+        [vmem] * 8 + [pl.ANY],
     )
 
 
@@ -1430,34 +1666,6 @@
     return block, q2, position, doc
 
 
-def attention_forward_kernel(
-    count, here_ref, q_ref, kv_ref, doc_ref, key_doc_ref, attn_ref, full_ref, total_ref, acc, tot
-):
-    rows = q_ref.shape[1]
-    block, q2, position, doc = attention_query(q_ref, doc_ref, here_ref[0], count, rows)
-    acc[...] = jnp.zeros_like(acc)
-    tot[...] = jnp.zeros_like(tot)
-
-    def one(key_block, carry):
-        key_half = (key_block >= count).astype(jnp.int32)
-        kv = kv_ref.at[key_block - key_half * count, key_half]
-        _, weights = attention_scores(
-            q2, kv[:, :HEAD_DIM], position, doc, key_block, key_doc_ref[0, key_block], rows
-        )
-        tot[...] += jnp.sum(weights, axis=-1, keepdims=True)
-        acc[...] += jnp.dot(
-            weights.astype(jnp.bfloat16), kv[:, HEAD_DIM:], preferred_element_type=jnp.float32
-        )
-        return carry
-
-    lax.fori_loop(jnp.maximum(block - count, 0), block + 1, one, 0)
-    attended = acc[...] / tot[...]
-    attended = jnp.concatenate([attended[:rows], attended[rows:]], axis=1)
-    full_ref[0] = attended
-    attn_ref[0] = attended.astype(jnp.bfloat16)
-    total_ref[0] = tot[...]
-
-
 def attention_backward_kernel(
     count,
     here_ref,
@@ -1538,33 +1746,6 @@
     key_doc = pl.BlockSpec((1, 2 * count, 1, rows), lambda s, h, here: (s, 0, 0, 0))
     total = pl.BlockSpec((1, REPS * rows, 1), lambda s, h, here: (2 * s + h, 0, 0))
     return query, keys, doc, key_doc, total
-
-
-def attention_forward(here, q, kv, doc, key_doc):
-    count, _, rows, _ = kv.shape
-    width = REPS * HEAD_DIM
-    query, keys, doc_spec, key_doc_spec, total = attention_specs(count, rows, width)
-    return pl.pallas_call(
-        functools.partial(attention_forward_kernel, count),
-        name="attend",
-        grid_spec=pltpu.PrefetchScalarGridSpec(
-            num_scalar_prefetch=1,
-            grid=(2, 2),
-            in_specs=[query, keys, doc_spec, key_doc_spec],
-            out_specs=[query, query, total],
-            scratch_shapes=[
-                pltpu.VMEM((REPS * rows, HEAD_DIM), jnp.float32),
-                pltpu.VMEM((REPS * rows, 1), jnp.float32),
-            ],
-        ),
-        out_shape=[
-            shape((GROUPS, rows, width), jnp.bfloat16),
-            shape((GROUPS, rows, width), jnp.float32),
-            shape((GROUPS, REPS * rows, 1), jnp.float32),
-        ],
-        compiler_params=pltpu.CompilerParams(vmem_limit_bytes=VMEM_LIMIT),
-        cost_estimate=pl.CostEstimate(flops=10**9, bytes_accessed=40 * 2**20, transcendentals=0),
-    )(here, q, kv, doc, key_doc)
 
 
 def attention_backward(here, q, kv, doc, key_doc, grad, full, totals):
@@ -1722,11 +1903,11 @@
     own_kv = sent[:, REPS:].reshape(group_rows, 2 * HEAD_DIM)
     kv_slab = slabs(group_rows)
     kv_piece = (group_rows // kv_slab, kv_slab, 2 * HEAD_DIM)
-    kv, out_all, gate_up_all = gather_second(own_kv, out_mine, gate_up_weight, count, 2)
+    kv, out_all, gate_up_all, attn, attended, totals = gather_attend(
+        own_kv, out_mine, gate_up_weight, queries, own_doc, key_doc, count, 2
+    )
     gate_up_all = gate_up_all.reshape(-1, 2 * width)
-    kv = kv.reshape(count, GROUPS, rows, 2 * HEAD_DIM)
     out_head = out_all.reshape(width, head_width)
-    attn, attended, totals = attention_forward(here_one, queries, kv, own_doc, key_doc)
     attn = attn.reshape(group_rows, head_width)
     branch_part = dot(attn, out_head, LAST).astype(bf16)
     branch_slabs = reduce_scatter_group(branch_part.reshape((GROUPS,) + piece), 3)
@@ -1763,16 +1944,30 @@
     attn_grad = dot(branch_all, out_head, PLAIN).astype(bf16).reshape(GROUPS, rows, head_width)
     out_part = dot(branch_all, attn, FIRST).astype(bf16)
     out_part = out_part.reshape(GROUPS, count, out_rows, head_width)
-    dq, dkv_part = attention_backward(
-        here_one, queries, kv, own_doc, key_doc, attn_grad, attended, totals
-    )
-    dkv, out_sum, gate_up_grad = reduce_middle(
-        dkv_part.reshape((count,) + kv_piece),
-        out_part,
-        gate_up_part.reshape((GROUPS,) + gate_up_weight.shape),
-        count,
-        9,
-    )
+    gate_up_part = gate_up_part.reshape((GROUPS,) + gate_up_weight.shape)
+    if attend_back_fits(count):
+        dq, dkv, out_sum, gate_up_grad = attend_back_reduce(
+            queries,
+            kv,
+            own_doc,
+            key_doc,
+            attn_grad,
+            attended,
+            totals,
+            out_part,
+            gate_up_part,
+            kv_piece,
+            count,
+            9,
+        )
+    else:
+        kv = kv.reshape(count, GROUPS, rows, 2 * HEAD_DIM)
+        dq, dkv_part = attention_backward(
+            here_one, queries, kv, own_doc, key_doc, attn_grad, attended, totals
+        )
+        dkv, out_sum, gate_up_grad = reduce_middle(
+            dkv_part.reshape((count,) + kv_piece), out_part, gate_up_part, count, 9
+        )
     sent_grad = jnp.concatenate(
         [
             dq.reshape(group_rows, REPS, HEAD_DIM),

time: 627 us -> 616 us (0.982)
  Pallas kernels: 558 us -> 549 us
    pallas_call x2 -> x0, Pallas kernels: 33.8 us -> none  [the longest x1 19.8 us: attention_backward(): pl.pallas_call(functools.partial(attention_backward_kernel, count), name=...]
    pallas_call x6, Pallas kernels: 297 us -> 320 us  [transfer(): pl.pallas_call(body, name=name, out_shape=outs, in_specs=[pl.BlockSpec(me...]
    unnamed x48 -> x50, local copies, waits for them, and re-layouts: 13.1 us -> 13.1 us
where the time goes in v6:
time: 616 us; the launch traced here: 615 us
  Pallas kernels  549 us (89%)
  local copies, waits for them, and re-layouts  29.1 us (5%)
  matrix products  24.8 us (4%)
  other arithmetic  11.4 us (2%)
    pallas_call x6, Pallas kernels, transfer(): pl.pallas_call(body, name=name, out_shape=outs, in_specs=[pl.BlockSpec(me...  320 us
    pallas_call x1, Pallas kernels, feed_forward(): pl.pallas_call(functools.partial(feed_forward_kernel, count), name='feed_...  228 us
    dot_general x6, matrix products, dot(): lax.dot_general(left, right, (contract, ((), ())), preferred_element_type...  24.8 us
    unnamed x50, local copies, waits for them, and re-layouts  13.1 us

profile of v6, /device:TPU:20, one launch (start us, length us, event | category | flops | bytes accessed | tf_op | source)
XLA Modules:
  0.0 615.2 jit_solution(16660882309986660926)
XLA Ops:
  0.7 1.3 pad_convert_fusion.refs_3_
  2.0 1.7 copy.44
  5.7 53.6 %first1.1 = (bf16[8,128,2304]{2,1,0:T(8,128)(2,1)}, bf16[4,72,512]{2,1,0:T(8,128)(2,1)}, bf16[4,128,2304]{2,1,0:T(8,128)(2,1)}, f32[4,8,8,128]{3,2,1,0:T(8,128)}...) custom-call(bf16[128,2304]{1,0:T(8,128)(2,1)} %refs_0_.1, bf16[4,72,512]{2,1,0:T(8,128)(2,1)} %bitcast.111, ...), custom_call_target="tpu_custom_call" | custom-call | bytes 283115520 | tf_op jit(solution)/shard_map/first1/pallas_call | solution.py:723
  60.3 1.3 constant_dynamic-slice_fusion
  61.7 2.2 multiply_reduce_fusion
  65.3 1.5 copy.27.refs_4_.refs_2_
  67.5 2.6 copy-done.20
  70.1 2.6 fusion.16
  75.9 82.6 %attend2.1 = (bf16[8,512,512]{2,1,0:T(8,128)(2,1)}, bf16[4,8,72,512]{3,2,1,0:T(8,128)(2,1)}, bf16[4,288,4608]{2,1,0:T(8,128)(2,1)}, bf16[4,128,512]{2,1,0:T(8,12...) custom-call(bf16[512,512]{1,0:T(8,128)(2,1)} %copy.38.refs_0_, bf16[4,72,512]{2,1,0:T(8,128)(2,1)} %get-tuple-element.37.refs_1_, ...), custom_call_target="tpu_custom_call" | custom-call | bytes 262144000 | tf_op jit(solution)/shard_map/attend2/pallas_call | solution.py:723
  158.4 4.7 convolution_convert_fusion.1
  163.1 20.7 %fold3.1.branch_ref = f32[8,16,2304]{2,1,0:T(8,128)} custom-call(bf16[4,8,16,2304]{3,2,1,0:T(8,128)(2,1)} %bitcast.105), custom_call_target="tpu_custom_call" | custom-call | bytes 94371840 | tf_op jit(solution)/shard_map/fold3/pallas_call | solution.py:723
  183.8 228.5 %feed_forward.1 = (bf16[8,16,2304]{2,1,0:T(8,128)(2,1)}, f32[8,16,2304]{2,1,0:T(8,128)}, bf16[8,16,2304]{2,1,0:T(8,128)(2,1)}, f32[4,2304]{1,0:T(4,128)}, bf16[1...) custom-call(f32[8,16,2304]{2,1,0:T(8,128)} %fold3.1.branch_ref, bf16[8,16,2304]{2,1,0:T(8,128)(2,1)} %bitcast.98, ...), custom_call_target="tpu_custom_call" | custom-call | flops 48922361856 | bytes 524288000 | tf_op jit(solution)/shard_map/feed_forward/pallas_call | solution.py:1603
  413.3 18.0 %group8.1 = bf16[4,128,2304]{2,1,0:T(8,128)(2,1)} custom-call(bf16[128,2304]{1,0:T(8,128)(2,1)} %bitcast.116), custom_call_target="tpu_custom_call" | custom-call | bytes 94371840 | tf_op jit(solution)/shard_map/group8/pallas_call | solution.py:723
  431.3 4.0 convolution_convert_fusion.2
  435.3 2.8 fusion.2
  438.2 85.5 %attend_back9.1 = (bf16[4,128,512]{2,1,0:T(8,128)(2,1)}, bf16[32,16,512]{2,1,0:T(8,128)(2,1)}, bf16[4,72,512]{2,1,0:T(8,128)(2,1)}, f32[288,4608]{1,0:T(8,128)}) custom-call(bf16[4,128,512]{2,1,0:T(8,128)(2,1)} %copy.39.refs_3_.refs_0_, bf16[8,512,512]{2,1,0:T(8,128)(2,1)} %get-tuple-element.45.refs_1_, s32[4,128,1]{2,1,0:T(8,128)} %copy.27.refs_4_.refs_2_, ...), custom_call_target="tpu_custom_call" | custom-call | bytes 262144000 | tf_op jit(solution)/shard_map/attend_back9/pallas_call | solution.py:723
  529.8 6.5 %fusion.1 = (f32[2304]{0:T(1024)S(1)}, bf16[512,2304]{1,0:T(8,128)(2,1)}) fusion(f32[512]{0:T(512)S(1)} %copy-done.19, bf16[4,128,2304]{2,1,0:T(8,128)(2,1)S(1)} %copy-done.1, bf16[512,1024]{0,1:T(8,128)(2,1)S(1)} %bitcast.112, bf16[1024,2304]{1,0:T(8,128)(2,1)} %bitcast.128), kind=kOutput, calls=%fused_computation.4 | convolution fusion | flops 2421815040 | bytes 10497024 | tf_op jit(solution)/shard_map/dot_general | solution.py:1265
  537.1 4.2 convolution_convert_fusion
  541.3 60.0 %last10.1 = (f32[8,16,2304]{2,1,0:T(8,128)}, f32[8,16,2304]{2,1,0:T(8,128)}, f32[1,8,128]{2,1,0:T(8,128)}, bf16[4,72,512]{2,1,0:T(8,128)(2,1)}, f32[288,2304]{1,0:T(8,128)}) custom-call(bf16[8,8,16,2304]{3,2,1,0:T(8,128)(2,1)} %bitcast.100, bf16[4,8,16,2304]{3,2,1,0:T(8,128)(2,1)} %bitcast.106, f32[8,4,1,8,128]{4,3,2,1,0:T(8,128)} %pad_bitcast_fusion.refs_2_, ...), custom_call_target="tpu_custom_call" | custom-call | bytes 188743680 | tf_op jit(solution)/shard_map/last10/pallas_call | solution.py:723
  601.3 1.3 slice_bitcast_fusion.1
  602.7 1.6 fusion.7
  604.4 1.2 fusion.10
  608.4 5.4 copy.51
  613.7 1.5 copy.52
  (87 shorter events, 18.9 us)
Async XLA Ops:
  4.7 68.3 %copy-start.3 = (f32[512,256]{0,1:T(8,128)}, f32[512,256]{0,1:T(8,128)S(1)}, u32[]{:S(2)}) copy-start(f32[512,256]{0,1:T(8,128)S(1)} %pad_maximum_fusion.2) | copy-start | bytes 1572868
  59.3 7.6 %copy-start = (bf16[4,128,2304]{2,1,0:T(8,128)(2,1)S(1)}, bf16[4,128,2304]{2,1,0:T(8,128)(2,1)}, u32[]{:S(2)}) copy-start(bf16[4,128,2304]{2,1,0:T(8,128)(2,1)} %get-tuple-element.34) | copy-start | bytes 7077892
  64.6 2.9 copy-start.17
  66.9 3.2 copy-start.20
  67.5 5.2 copy-start.8
  412.2 19.1 %copy-start.21 = (bf16[4,8,72,512]{3,2,1,0:T(8,128)(2,1)S(1)}, bf16[4,8,72,512]{3,2,1,0:T(8,128)(2,1)}, u32[]{:S(2)}) copy-start(bf16[4,8,72,512]{3,2,1,0:T(8,128)(2,1)} %get-tuple-element.40) | copy-start | bytes 7077892
  431.3 4.0 copy-start.10
  431.3 4.0 copy-start.22
  523.7 2.0 copy-start.15
  526.6 0.8 copy-start.6
  526.8 1.1 copy-start.4
  526.8 1.2 copy-start.11
  528.0 0.9 slice-start
  528.0 1.8 copy-start.1
  528.0 1.8 copy-start.19
  529.8 7.3 %copy-start.9 = (bf16[4,128,2304]{2,1,0:T(8,128)(2,1)S(1)}, bf16[4,128,2304]{2,1,0:T(8,128)(2,1)}, u32[]{:S(2)}) copy-start(bf16[4,128,2304]{2,1,0:T(8,128)(2,1)} %copy-done.8) | copy-start | bytes 7077892
  541.3 61.4 %copy-start.2 = (bf16[1,128,2304]{2,1,0:T(8,128)(2,1)S(1)}, bf16[1,128,2304]{2,1,0:T(8,128)(2,1)}, u32[]{:S(2)}) copy-start(bf16[1,128,2304]{2,1,0:T(8,128)(2,1)} %param.8) | copy-start | bytes 1769476
  541.3 61.4 %copy-start.18 = (f32[2304]{0:T(1024)S(1)}, f32[2304]{0:T(1024)}, u32[]{:S(2)}) copy-start(f32[2304]{0:T(1024)} %copy-done.17) | copy-start | bytes 27652
  541.3 63.0 %copy-start.12 = (f32[8,16,2304]{2,1,0:T(8,128)S(1)}, f32[8,16,2304]{2,1,0:T(8,128)}, u32[]{:S(2)}) copy-start(f32[8,16,2304]{2,1,0:T(8,128)} %get-tuple-element.44) | copy-start | bytes 3538948
  601.3 3.0 copy-start.5
  602.7 2.9 copy-start.16
  604.4 2.2 copy-start.14
  605.6 1.8 copy-start.13
  608.4 5.4 copy-start.7

commit v7 on v6

--- a/solution.py
+++ b/solution.py
@@ -239,6 +239,31 @@
             def _():
                 self.extra(1).wait_send()
                 self.extra(self.place.outer - 1).wait_send()
+
+
+def advance(gathers, k):
+    place = gathers[0].place
+
+    def each(name, *args):
+        for gather in gathers:
+            getattr(gather, name)(*args)
+
+    if not gathers[0].evened:
+        if k + 1 < place.outer:
+            each("pass_on", k + 1)
+        return
+    middle = gathers[0].middle
+    ends = jnp.logical_not(middle)
+    if k == 0:
+        each("pass_on", 1)
+        pl.when(middle)(lambda: each("pass_on", 2))
+    elif k == 1:
+        pl.when(ends)(lambda: each("pass_on", 2))
+        each("pass_extra", 1)
+        pl.when(middle)(lambda: each("pass_on", 3))
+    elif k == 2:
+        pl.when(ends)(lambda: each("pass_on", 3))
+        each("pass_extra", 3)
 
 
 def gather_blk(place, src, view, sent, came, own):
@@ -373,24 +398,29 @@
         line, outer = self.place.line, self.place.outer
         return ((there < line) & (line == outer - 1)) | ((there > line) & (line == 0))
 
-    def pass_on(self, k, h):
+    def pass_on(self, k, h, middle=None):
         place = self.place
         line = place.line
         there = self.far(k)
         terms = self.terms(k, h)
         held = self.part(self.held.at[there], h)
-        starts = self.starts(there)
-
-        @pl.when(starts)
-        def _():
+
+        def first():
             add_into(held, *terms)
 
-        @pl.when(jnp.logical_not(starts))
-        def _():
+        def later():
             back = jnp.where(there < line, line + 1, line - 1)
             self.line_copy(there, there, back, h).wait_recv()
             add_into(held, self.part(self.along.at[there], h), *terms)
 
+        if middle is None:
+            starts = self.starts(there)
+            pl.when(starts)(first)
+            pl.when(jnp.logical_not(starts))(later)
+        elif middle:
+            later()
+        else:
+            first()
         self.onward(there, h).start()
 
     def last(self, h):
@@ -492,13 +522,14 @@
             for h in (0, 1):
                 self.send(3, h)
 
-        steps = (first, lambda: self.pass_on(0, 1), second)
-        return [lambda step=step: pl.when(self.middle)(step) for step in steps]
+        steps = (first, lambda: self.pass_on(0, 1, True), second)
+        return steps
 
     def events(self):
         outer, parts = self.place.outer, self.parts
         if self.evened:
-            todo = self.turning() + [lambda: self.pass_on(0, 0)]
+            todo = [lambda step=step: pl.when(self.middle)(step) for step in self.turning()]
+            todo.append(lambda: self.pass_on(0, 0))
         else:
             todo = [lambda h=h: self.pass_on(0, h) for h in range(parts)]
         for k in range(1, outer - 1):
@@ -576,13 +607,13 @@
     return ref.at[pl.ds(p * rows, rows)]
 
 
-def gather_group_rows(place, src, out, parts, take):
+def gather_group_rows(place, src, out, parts, take, through=True):
     def task(p, refs):
         rows = src.shape[0] // parts
         view = lambda g: out.at[g, pl.ds(p * rows, rows)]
         return gather_group(place, share_rows(src, parts, p), view, *refs)
 
-    return [task(p, take(4)) for p in range(parts)]
+    return [task(p, take(4 if through else 3)) for p in range(parts)]
 
 
 def gather_rows_scratch(value, parts):
@@ -668,22 +699,25 @@
     ]
 
 
-def reduce_group(place, part, out, from_core, from_half, held, sent, came):
+def reduce_group(place, view, out, from_core, from_half, held, sent, came):
+    if not callable(view):
+        part = view
+        view = lambda g: part.at[g]
     far = 2 * (1 - place.core) + (1 - place.half)
     near = 2 * (1 - place.core) + place.half
-    first = remote(part.at[far], from_core.at[1], sent.at[0], came.at[0], place.partner())
-    second = remote(part.at[near], from_core.at[0], sent.at[1], came.at[1], place.partner())
+    first = remote(view(far), from_core.at[1], sent.at[0], came.at[0], place.partner())
+    second = remote(view(near), from_core.at[0], sent.at[1], came.at[1], place.partner())
     first.start()
     second.start()
     yield
     first.wait_recv()
-    add_into(held, part.at[2 * place.core + (1 - place.half)], from_core.at[1])
+    add_into(held, view(2 * place.core + (1 - place.half)), from_core.at[1])
     third = remote(held, from_half, sent.at[2], came.at[2], place.across())
     third.start()
     yield
     second.wait_recv()
     third.wait_recv()
-    add_into(out, part.at[place.group], from_core.at[0], from_half)
+    add_into(out, view(place.group), from_core.at[0], from_half)
     first.wait_send()
     second.wait_send()
     third.wait_send()
@@ -856,36 +890,20 @@
     )
 
 
-def attend_block(count, g, here, q_ref, kv_ref, doc_ref, key_doc_ref, attn_ref, full_ref, total_ref):
+def attend_step(count, g, here, key_half, key_at, q_ref, kv_ref, doc_ref, key_doc_ref, acc, tot):
     rows = q_ref.shape[1]
     sequence, half = g // 2, g % 2
-    block = half * count + here
-    q2, position, doc = stacked_queries(g, block, q_ref, doc_ref)
-
-    def one(key_block, carry):
-        total, acc = carry
-        key_half = (key_block >= count).astype(jnp.int32)
-        at = pl.ds(pl.multiple_of((2 * sequence + key_half) * rows, rows), rows)
-        kv = kv_ref.at[key_block - key_half * count, at]
-        _, weights = attention_scores(
-            q2, kv[:, :HEAD_DIM], position, doc, key_block, key_doc_ref[sequence, key_block], rows
-        )
-        total = total + jnp.sum(weights, axis=-1, keepdims=True)
-        acc = acc + jnp.dot(
-            weights.astype(jnp.bfloat16), kv[:, HEAD_DIM:], preferred_element_type=jnp.float32
-        )
-        return total, acc
-
-    start = (
-        jnp.zeros((REPS * rows, 1), jnp.float32),
-        jnp.zeros((REPS * rows, HEAD_DIM), jnp.float32),
+    q2, position, doc = stacked_queries(g, half * count + here, q_ref, doc_ref)
+    key_block = key_half * count + key_at
+    at = pl.ds(pl.multiple_of((2 * sequence + key_half) * rows, rows), rows)
+    kv = kv_ref.at[key_at, at]
+    _, weights = attention_scores(
+        q2, kv[:, :HEAD_DIM], position, doc, key_block, key_doc_ref[sequence, key_block], rows
     )
-    total, acc = lax.fori_loop(jnp.maximum(block - count, 0), block + 1, one, start)
-    attended = acc / total
-    attended = jnp.concatenate([attended[:rows], attended[rows:]], axis=1)
-    full_ref[g] = attended
-    attn_ref[g] = attended.astype(jnp.bfloat16)
-    total_ref[g] = total
+    tot[g] += jnp.sum(weights, axis=-1, keepdims=True)
+    acc[g] += jnp.dot(
+        weights.astype(jnp.bfloat16), kv[:, HEAD_DIM:], preferred_element_type=jnp.float32
+    )
 
 
 def stacked_queries(g, block, q_ref, doc_ref):
@@ -898,10 +916,14 @@
 
 
 def gather_attend(kv, out_mine, gate_up, queries, doc, key_doc, count, number):
+    groups, out_rows, width = out_mine.shape
+    rows = queries.shape[1]
+
     def body(*refs):
         kv_ref, out_ref, gate_up_ref, q_ref, doc_ref, key_doc_ref = refs[:6]
         kv_all, out_all, gate_up_all, attn_ref, full_ref, total_ref = refs[6:12]
-        take = Taker(refs[12:])
+        acc, tot = refs[12:14]
+        take = Taker(refs[14:])
         place = Place(count)
         greet(place, blk=True, core=True, half=True)
         gathers = (
@@ -913,36 +935,55 @@
             gather.start()
         for task in groups:
             next(task)
-        for k in range(1, place.outer):
-            for gather in gathers:
-                gather.pass_on(k)
-            if k == place.outer - 2:
-                for gather in gathers:
-                    gather.pass_extra(1)
-                next(groups[0])
-        for gather in gathers:
-            gather.pass_extra(place.outer - 1)
-        next(groups[1])
+        acc[...] = jnp.zeros_like(acc)
+        tot[...] = jnp.zeros_like(tot)
+        here, inner = place.here, place.inner
+
+        def attend(k):
+            def one(c, carry):
+                key_at = place.near(k) * inner + c // 6
+                sequence, kind = (c % 6) // 3, c % 3
+                half = jnp.minimum(kind, 1)
+                needed = jnp.where(kind == 1, key_at >= here, key_at <= here)
+
+                @pl.when(needed)
+                def _():
+                    attend_step(
+                        count,
+                        2 * sequence + half,
+                        here,
+                        kind // 2,
+                        key_at,
+                        q_ref,
+                        kv_all,
+                        doc_ref,
+                        key_doc_ref,
+                        acc,
+                        tot,
+                    )
+
+                return carry
+
+            lax.fori_loop(0, inner * 6, one, 0)
+
         gathers[0].copy.wait()
         for k in range(place.outer):
+            advance(gathers, k)
             gathers[0].beside_arrived(k)
-
-        def attend(g, carry):
-            attend_block(
-                count,
-                g,
-                place.here,
-                q_ref,
-                kv_all,
-                doc_ref,
-                key_doc_ref,
-                attn_ref,
-                full_ref,
-                total_ref,
-            )
+            if 0 < k < place.outer - 1 and k <= 2:
+                next(groups[k - 1])
+            attend(k)
+
+        def put(g, carry):
+            total = tot[g]
+            attended = acc[g] / total
+            attended = jnp.concatenate([attended[:rows], attended[rows:]], axis=1)
+            full_ref[g] = attended
+            attn_ref[g] = attended.astype(jnp.bfloat16)
+            total_ref[g] = total
             return carry
 
-        lax.fori_loop(0, GROUPS, attend, 0)
+        lax.fori_loop(0, GROUPS, put, 0)
         next(groups[2])
         gathers[1].copy.wait()
         for k in range(place.outer):
@@ -951,8 +992,6 @@
             gather.finish()
         together(*groups)
 
-    groups, out_rows, width = out_mine.shape
-    rows = queries.shape[1]
     return transfer(
         f"attend{number}",
         number,
@@ -966,7 +1005,13 @@
             shape((GROUPS, rows, width), jnp.float32),
             shape((GROUPS, REPS * rows, 1), jnp.float32),
         ],
-        gather_blk_sems(count) + gather_blk_sems(count) + gather_rows_scratch(gate_up, ROW_PARTS),
+        [
+            pltpu.VMEM((GROUPS, REPS * rows, HEAD_DIM), jnp.float32),
+            pltpu.VMEM((GROUPS, REPS * rows, 1), jnp.float32),
+        ]
+        + gather_blk_sems(count)
+        + gather_blk_sems(count)
+        + gather_rows_scratch(gate_up, ROW_PARTS),
         (kv.size + out_mine.size) * 2 * count,
         [pltpu.VMEM, pl.ANY, pl.ANY, pltpu.VMEM, pltpu.VMEM, pltpu.VMEM],
         [pltpu.VMEM, pltpu.VMEM, pl.ANY, pltpu.VMEM, pltpu.VMEM, pltpu.VMEM],
@@ -1068,27 +1113,47 @@
 
             lax.fori_loop(0, count, one, 0)
 
+        ends = jnp.logical_not(out.middle)
+
+        turning = out.turning()
+
+        def middle(*steps):
+            @pl.when(out.middle)
+            def _():
+                for step in steps:
+                    if isinstance(step, int):
+                        turning[step]()
+                    else:
+                        out.pass_on(*step, True)
+
+        def outside(*steps):
+            @pl.when(ends)
+            def _():
+                for step in steps:
+                    out.pass_on(*step, False)
+
         out.start()
         for fold in folds:
             next(fold)
         lax.fori_loop(0, 2 * count, clear, 0)
         back(0)
         next(folds[0])
-        out_events[0]()
+        middle(0)
         back(1)
         put(0)
-        out_events[1]()
-        out_events[2]()
+        middle(1, 2)
+        outside((0, 0), (1, 0), (1, 1))
         next(folds[1])
         lax.fori_loop(0, 2 * count, clear, 0)
         back(2)
-        out_events[3]()
+        outside((2, 0), (2, 1))
+        middle((0, 0))
         back(3)
         put(1)
+        middle((1, 0), (1, 1), (2, 0), (2, 1))
         dkv.start()
         dkv_events = dkv.events()
-        order = [(out_events, i) for i in range(4, 8)]
-        order += [(folds, 2), (dkv_events, 0), (dkv_events, 1), (dkv_events, 2)]
+        order = [(folds, 2), (dkv_events, 0), (dkv_events, 1), (dkv_events, 2)]
         order += [(out_events, 8), (out_events, 9), (dkv_events, 3), (dkv_events, 4)]
         order += [(folds, 0), (dkv_events, 5), (dkv_events, 6), (folds, 1)]
         order += [(dkv_events, 7), (dkv_events, 8), (dkv_events, 9), (folds, 2)]
@@ -1224,11 +1289,16 @@
     )
 
 
+GROUP_PARTS = 4
+
+
 def all_gather_group(value, number):
+    parts = GROUP_PARTS
+
     def body(src, out, *sems):
         place = Place(lax.axis_size("blk"))
         greet(place, core=True, half=True)
-        together(gather_group(place, src, out, *sems))
+        together(*gather_group_rows(place, src, out, parts, Taker(sems), False))
 
     return transfer(
         f"group{number}",
@@ -1236,18 +1306,26 @@
         body,
         [value],
         [shape((GROUPS,) + value.shape, value.dtype)],
-        gather_group_sems(),
+        gather_group_sems() * parts,
         value.size * 8,
     )[0]
 
 
 def reduce_scatter_group(value, number):
     piece = value.shape[1:]
+    parts = GROUP_PARTS
+    steps = piece[0] // parts
 
     def body(part, out, *scratch):
+        take = Taker(scratch)
         place = Place(lax.axis_size("blk"))
         greet(place, core=True, half=True)
-        together(reduce_group(place, part, out, *scratch))
+
+        def task(p):
+            at = pl.ds(p * steps, steps)
+            return reduce_group(place, lambda g: part.at[g, at], out.at[at], *take(5))
+
+        together(*[task(p) for p in range(parts)])
 
     return transfer(
         f"fold{number}",
@@ -1255,7 +1333,7 @@
         body,
         [value],
         [shape(piece, jnp.float32)],
-        reduce_group_scratch(piece, value.dtype),
+        reduce_group_scratch((steps,) + piece[1:], value.dtype) * parts,
         value.size * 2,
         [pltpu.VMEM],
     )[0]
@@ -1392,22 +1470,7 @@
     def receive(gather, k):
         if k == 0:
             gather.copy.wait()
-        if not gather.evened:
-            if k + 1 < outer:
-                gather.pass_on(k + 1)
-            gather.beside_arrived(k)
-            return
-        ends = jnp.logical_not(gather.middle)
-        if k == 0:
-            gather.pass_on(1)
-            pl.when(gather.middle)(lambda: gather.pass_on(2))
-        elif k == 1:
-            pl.when(ends)(lambda: gather.pass_on(2))
-            gather.pass_extra(1)
-            pl.when(gather.middle)(lambda: gather.pass_on(3))
-        elif k == 2:
-            pl.when(ends)(lambda: gather.pass_on(3))
-            gather.pass_extra(3)
+        advance([gather], k)
         gather.beside_arrived(k)
 
     gather = GatherBlk(place, norm_own, lambda i: norm_all.at[i], *take(3))

time: 616 us -> 607 us (0.985); the launches traced: 615 us -> 598 us
  Pallas kernels: 549 us -> 531 us
    pallas_call x6, Pallas kernels: 320 us -> 304 us  [transfer(): pl.pallas_call(body, name=name, out_shape=outs, in_specs=[pl.BlockSpec(me...]
where the time goes in v7:
time: 607 us; the launch traced here: 598 us
  Pallas kernels  531 us (87%)
  local copies, waits for them, and re-layouts  29.1 us (5%)
  matrix products  24.8 us (4%)
  other arithmetic  11.4 us (2%)
    pallas_call x6, Pallas kernels, transfer(): pl.pallas_call(body, name=name, out_shape=outs, in_specs=[pl.BlockSpec(me...  304 us
    pallas_call x1, Pallas kernels, feed_forward(): pl.pallas_call(functools.partial(feed_forward_kernel, count), name='feed_...  227 us
    dot_general x6, matrix products, dot(): lax.dot_general(left, right, (contract, ((), ())), preferred_element_type...  24.8 us
    unnamed x50, local copies, waits for them, and re-layouts  13.1 us

profile of v7, /device:TPU:20, one launch (start us, length us, event | category | flops | bytes accessed | tf_op | source)
XLA Modules:
  0.0 598.2 jit_solution(11171423717542916372)
XLA Ops:
  0.7 1.3 pad_convert_fusion.refs_3_
  2.0 1.7 copy.44
  5.7 53.6 %first1.1 = (bf16[8,128,2304]{2,1,0:T(8,128)(2,1)}, bf16[4,72,512]{2,1,0:T(8,128)(2,1)}, bf16[4,128,2304]{2,1,0:T(8,128)(2,1)}, f32[4,8,8,128]{3,2,1,0:T(8,128)}...) custom-call(bf16[128,2304]{1,0:T(8,128)(2,1)} %refs_0_.1, bf16[4,72,512]{2,1,0:T(8,128)(2,1)} %bitcast.111, ...), custom_call_target="tpu_custom_call" | custom-call | bytes 283115520 | tf_op jit(solution)/shard_map/first1/pallas_call | solution.py:757
  60.3 1.3 constant_dynamic-slice_fusion
  61.7 2.2 multiply_reduce_fusion
  65.3 1.5 copy.27.refs_4_.refs_2_
  67.5 2.6 copy-done.20
  70.1 2.6 fusion.16
  75.9 74.8 %attend2.1 = (bf16[8,512,512]{2,1,0:T(8,128)(2,1)}, bf16[4,8,72,512]{3,2,1,0:T(8,128)(2,1)}, bf16[4,288,4608]{2,1,0:T(8,128)(2,1)}, bf16[4,128,512]{2,1,0:T(8,12...) custom-call(bf16[512,512]{1,0:T(8,128)(2,1)} %copy.38.refs_0_, bf16[4,72,512]{2,1,0:T(8,128)(2,1)} %get-tuple-element.37.refs_1_, ...), custom_call_target="tpu_custom_call" | custom-call | bytes 262144000 | tf_op jit(solution)/shard_map/attend2/pallas_call | solution.py:757
  150.7 4.7 convolution_convert_fusion.1
  155.4 19.9 %fold3.1.branch_ref = f32[8,16,2304]{2,1,0:T(8,128)} custom-call(bf16[4,8,16,2304]{3,2,1,0:T(8,128)(2,1)} %bitcast.105), custom_call_target="tpu_custom_call" | custom-call | bytes 94371840 | tf_op jit(solution)/shard_map/fold3/pallas_call | solution.py:757
  175.3 226.9 %feed_forward.1 = (bf16[8,16,2304]{2,1,0:T(8,128)(2,1)}, f32[8,16,2304]{2,1,0:T(8,128)}, bf16[8,16,2304]{2,1,0:T(8,128)(2,1)}, f32[4,2304]{1,0:T(4,128)}, bf16[1...) custom-call(f32[8,16,2304]{2,1,0:T(8,128)} %fold3.1.branch_ref, bf16[8,16,2304]{2,1,0:T(8,128)(2,1)} %bitcast.98, ...), custom_call_target="tpu_custom_call" | custom-call | flops 48922361856 | bytes 524288000 | tf_op jit(solution)/shard_map/feed_forward/pallas_call | solution.py:1666
  403.3 17.5 %group8.1 = bf16[4,128,2304]{2,1,0:T(8,128)(2,1)} custom-call(bf16[128,2304]{1,0:T(8,128)(2,1)} %bitcast.116), custom_call_target="tpu_custom_call" | custom-call | bytes 94371840 | tf_op jit(solution)/shard_map/group8/pallas_call | solution.py:757
  420.9 4.0 convolution_convert_fusion.2
  424.9 2.8 fusion.2
  427.7 76.2 %attend_back9.1 = (bf16[4,128,512]{2,1,0:T(8,128)(2,1)}, bf16[32,16,512]{2,1,0:T(8,128)(2,1)}, bf16[4,72,512]{2,1,0:T(8,128)(2,1)}, f32[288,4608]{1,0:T(8,128)}) custom-call(bf16[4,128,512]{2,1,0:T(8,128)(2,1)} %copy.39.refs_3_.refs_0_, bf16[8,512,512]{2,1,0:T(8,128)(2,1)} %get-tuple-element.45.refs_1_, s32[4,128,1]{2,1,0:T(8,128)} %copy.27.refs_4_.refs_2_, ...), custom_call_target="tpu_custom_call" | custom-call | bytes 262144000 | tf_op jit(solution)/shard_map/attend_back9/pallas_call | solution.py:757
  510.0 6.5 %fusion.1 = (f32[2304]{0:T(1024)S(1)}, bf16[512,2304]{1,0:T(8,128)(2,1)}) fusion(f32[512]{0:T(512)S(1)} %copy-done.19, bf16[4,128,2304]{2,1,0:T(8,128)(2,1)S(1)} %copy-done.1, bf16[512,1024]{0,1:T(8,128)(2,1)S(1)} %bitcast.112, bf16[1024,2304]{1,0:T(8,128)(2,1)} %bitcast.128), kind=kOutput, calls=%fused_computation.4 | convolution fusion | flops 2421815040 | bytes 10497024 | tf_op jit(solution)/shard_map/dot_general | solution.py:1343
  517.3 4.2 convolution_convert_fusion
  521.5 62.4 %last10.1 = (f32[8,16,2304]{2,1,0:T(8,128)}, f32[8,16,2304]{2,1,0:T(8,128)}, f32[1,8,128]{2,1,0:T(8,128)}, bf16[4,72,512]{2,1,0:T(8,128)(2,1)}, f32[288,2304]{1,0:T(8,128)}) custom-call(bf16[8,8,16,2304]{3,2,1,0:T(8,128)(2,1)} %bitcast.100, bf16[4,8,16,2304]{3,2,1,0:T(8,128)(2,1)} %bitcast.106, f32[8,4,1,8,128]{4,3,2,1,0:T(8,128)} %pad_bitcast_fusion.refs_2_, ...), custom_call_target="tpu_custom_call" | custom-call | bytes 188743680 | tf_op jit(solution)/shard_map/last10/pallas_call | solution.py:757
  583.9 1.3 slice_bitcast_fusion.1
  585.2 1.6 fusion.7
  586.9 1.2 fusion.10
  590.9 5.4 copy.51
  596.3 1.5 copy.52
  (87 shorter events, 18.9 us)
Async XLA Ops:
  4.7 68.3 %copy-start.3 = (f32[512,256]{0,1:T(8,128)}, f32[512,256]{0,1:T(8,128)S(1)}, u32[]{:S(2)}) copy-start(f32[512,256]{0,1:T(8,128)S(1)} %pad_maximum_fusion.2) | copy-start | bytes 1572868
  59.3 7.6 %copy-start = (bf16[4,128,2304]{2,1,0:T(8,128)(2,1)S(1)}, bf16[4,128,2304]{2,1,0:T(8,128)(2,1)}, u32[]{:S(2)}) copy-start(bf16[4,128,2304]{2,1,0:T(8,128)(2,1)} %get-tuple-element.34) | copy-start | bytes 7077892
  64.6 2.9 copy-start.17
  66.9 3.2 copy-start.20
  67.5 5.2 copy-start.8
  402.2 18.6 %copy-start.21 = (bf16[4,8,72,512]{3,2,1,0:T(8,128)(2,1)S(1)}, bf16[4,8,72,512]{3,2,1,0:T(8,128)(2,1)}, u32[]{:S(2)}) copy-start(bf16[4,8,72,512]{3,2,1,0:T(8,128)(2,1)} %get-tuple-element.40) | copy-start | bytes 7077892
  420.8 4.0 copy-start.10
  420.9 4.0 copy-start.22
  503.9 2.0 copy-start.15
  506.8 0.8 copy-start.6
  507.0 1.1 copy-start.4
  507.0 1.2 copy-start.11
  508.2 0.9 slice-start
  508.2 1.8 copy-start.1
  508.2 1.8 copy-start.19
  510.0 7.3 %copy-start.9 = (bf16[4,128,2304]{2,1,0:T(8,128)(2,1)S(1)}, bf16[4,128,2304]{2,1,0:T(8,128)(2,1)}, u32[]{:S(2)}) copy-start(bf16[4,128,2304]{2,1,0:T(8,128)(2,1)} %copy-done.8) | copy-start | bytes 7077892
  521.5 63.7 %copy-start.2 = (bf16[1,128,2304]{2,1,0:T(8,128)(2,1)S(1)}, bf16[1,128,2304]{2,1,0:T(8,128)(2,1)}, u32[]{:S(2)}) copy-start(bf16[1,128,2304]{2,1,0:T(8,128)(2,1)} %param.8) | copy-start | bytes 1769476
  521.5 63.7 %copy-start.18 = (f32[2304]{0:T(1024)S(1)}, f32[2304]{0:T(1024)}, u32[]{:S(2)}) copy-start(f32[2304]{0:T(1024)} %copy-done.17) | copy-start | bytes 27652
  521.5 65.4 %copy-start.12 = (f32[8,16,2304]{2,1,0:T(8,128)S(1)}, f32[8,16,2304]{2,1,0:T(8,128)}, u32[]{:S(2)}) copy-start(f32[8,16,2304]{2,1,0:T(8,128)} %get-tuple-element.44) | copy-start | bytes 3538948
  583.9 3.0 copy-start.5
  585.2 2.9 copy-start.16
  586.9 2.2 copy-start.14
  588.1 1.8 copy-start.13
  590.9 5.4 copy-start.7

commit v8 on v7

--- a/solution.py
+++ b/solution.py
@@ -39,6 +39,12 @@
         found = jnp.int32(orders[0])
         for line in range(1, self.outer):
             found = jnp.where(self.line == line, jnp.int32(orders[line]), found)
+        return found
+
+    def near_at(self, k):
+        found = self.near(0)
+        for static in range(1, self.outer):
+            found = jnp.where(k == static, self.near(static), found)
         return found
 
     def at(self, line, side):
@@ -287,14 +293,21 @@
 
 
 def add_into(out, *terms):
+    lanes = out.shape[-1]
+    parts = 3 if lanes % 384 == 0 and lanes > 1024 else 1
+    step = lanes // parts
+
     def one(i, carry):
-        total = terms[0][i].astype(jnp.float32)
+        at = i if parts == 1 else i // parts
+        columns = pl.ds(pl.multiple_of((i % parts) * step, step), step) if parts > 1 else slice(None)
+        index = (at,) + (slice(None),) * (len(out.shape) - 2) + (columns,)
+        total = terms[0][index].astype(jnp.float32)
         for term in terms[1:]:
-            total = total + term[i].astype(jnp.float32)
-        out[i] = total.astype(out.dtype)
+            total = total + term[index].astype(jnp.float32)
+        out[index] = total.astype(out.dtype)
         return carry
 
-    lax.fori_loop(0, out.shape[0], one, 0)
+    lax.fori_loop(0, out.shape[0] * parts, one, 0)
 
 
 def reduce_blk_scratch(place_count, piece, dtype, parts=2):
@@ -427,30 +440,21 @@
         place = self.place
         line, outer = place.line, place.outer
         terms = self.terms(outer - 1, h)
-        below, above = line > 0, line < outer - 1
-        from_above = self.part(self.along.at[line], h)
-        from_below = self.part(self.along.at[outer], h)
         out = self.part(self.out, h)
 
-        @pl.when(above)
+        @pl.when(self.middle)
         def _():
             self.line_copy(line, line, line + 1, h).wait_recv()
-
-        @pl.when(below)
+            self.line_copy(line, outer, line - 1, h).wait_recv()
+            from_above = self.part(self.along.at[line], h)
+            add_into(out, from_above, self.part(self.along.at[outer], h), *terms)
+
+        @pl.when(jnp.logical_not(self.middle))
         def _():
-            self.line_copy(line, outer, line - 1, h).wait_recv()
-
-        @pl.when(above & below)
-        def _():
-            add_into(out, from_above, from_below, *terms)
-
-        @pl.when(above & jnp.logical_not(below))
-        def _():
-            add_into(out, from_above, *terms)
-
-        @pl.when(jnp.logical_not(above) & below)
-        def _():
-            add_into(out, from_below, *terms)
+            slot = jnp.where(line == 0, line, outer)
+            back = jnp.where(line == 0, line + 1, line - 1)
+            self.line_copy(line, slot, back, h).wait_recv()
+            add_into(out, self.part(self.along.at[slot], h), *terms)
 
 
     def spare_view(self, k):
@@ -1360,7 +1364,7 @@
     weights = 3 * hidden * width * 2
     kept = count * rows * 3 * hidden * 2
     total = weights + kept + tile * (3 * count + outer * (inner - 1) + 2 * outer + 3) + 9 * tile
-    total += 3 * LANES * (count * rows + 2 * width) * 2
+    total += 6 * LANES * (count * rows + 3 * 256) * 2
     return total < 58 * 2**20 and hidden % (3 * LANES) == 0 and width % 256 == 0
 
 
@@ -1455,10 +1459,10 @@
     greet(place, blk=True)
 
     def pair_rows(k):
-        return pl.ds(pl.multiple_of(place.near(k) * pair, pair), pair)
+        return pl.ds(pl.multiple_of(place.near_at(k) * pair, pair), pair)
 
     def pair_pieces(k):
-        return pl.ds(place.near(k) * inner, inner)
+        return pl.ds(place.near_at(k) * inner, inner)
 
     def column(n):
         return pl.ds(pl.multiple_of(n * 256, 256), 256)
@@ -1468,19 +1472,23 @@
         part[pair_pieces(k), :, :, column(n)] = split
 
     def receive(gather, k):
-        if k == 0:
-            gather.copy.wait()
-        advance([gather], k)
-        gather.beside_arrived(k)
+        def one(static):
+            if static == 0:
+                gather.copy.wait()
+            advance([gather], static)
+            gather.beside_arrived(static)
+
+        for static in range(outer):
+            pl.when(k == static)(lambda static=static: one(static))
 
     gather = GatherBlk(place, norm_own, lambda i: norm_all.at[i], *take(3))
     gather.start()
     lax.fori_loop(0, chunks, wait_weights, 0)
-    for k in range(outer):
+    def forward(k, carry):
         receive(gather, k)
         at = pair_rows(k)
 
-        def up_chunk(j, carry, k=k, at=at):
+        def up_chunk(j, carry):
             x = norm_all[pair_pieces(k)].reshape(pair, width)
             both = dot(x, w_gate_up[j], LAST)
             act[at, column(j)] = both.astype(jnp.bfloat16)
@@ -1493,11 +1501,14 @@
 
         lax.fori_loop(0, chunks, up_chunk, 0)
 
-        def down_chunk(n, carry, k=k, at=at):
+        def down_chunk(n, carry):
             put_part(k, n, dot(hidden[at, :], w_down[:, column(n)], PLAIN))
             return carry
 
         lax.fori_loop(0, columns, down_chunk, 0)
+        return carry
+
+    lax.fori_loop(0, outer, forward, 0)
     gather.finish()
     reduce = ReduceBlk(place, lambda i: part.at[i], total, beside, along, held, spare, *take(6))
     reduce.start()
@@ -1527,11 +1538,11 @@
 
     gather = GatherBlk(place, grad_own, lambda i: grad_all.at[i], *take(3))
     gather.start()
-    for k in range(outer):
+    def backward(k, carry):
         receive(gather, k)
         at = pair_rows(k)
 
-        def back_chunk(j, carry, k=k, at=at):
+        def back_chunk(j, carry):
             g = grad_all[pair_pieces(k)].reshape(pair, width)
             units_at = pl.ds(pl.multiple_of(j * LANES, LANES), LANES)
             grad = dot(g, w_down[units_at], LAST)
@@ -1548,90 +1559,97 @@
 
         lax.fori_loop(0, chunks, back_chunk, 0)
 
-        def input_chunk(n, carry, k=k, at=at):
+        def input_chunk(n, carry):
             w = w_gate_up[:, :, column(n)].reshape(2 * units, 256)
             put_part(k, n, dot(act[at, :], w, PLAIN))
             return carry
 
         lax.fori_loop(0, columns, input_chunk, 0)
+        return carry
+
+    lax.fori_loop(0, outer, backward, 0)
     gather.finish()
     reduce = ReduceBlk(place, lambda i: part.at[i], total, beside, along, held, spare, *take(6))
     reduce.start()
 
     tokens = count * rows
     slots = staged.shape[0]
-
-    def up_store(i):
-        slot = lax.rem(i, slots)
-        units_at = pl.ds(pl.multiple_of(i * LANES, LANES), LANES)
+    three = 3 * LANES
+
+    def up_store(step):
+        slot = lax.rem(step, slots)
+        i, n = step // columns, lax.rem(step, columns)
         return [
             pltpu.make_async_copy(
-                staged.at[slot, pl.ds(h * LANES, LANES)],
-                gate_up_grad_hbm.at[units_at, pl.ds(h * width, width)],
-                out_sems.at[slot, h],
+                staged.at[slot, pl.ds((2 * q + h) * LANES, LANES)],
+                gate_up_grad_hbm.at[
+                    pl.ds(pl.multiple_of((3 * i + q) * LANES, LANES), LANES),
+                    pl.ds(pl.multiple_of(h * width + n * 256, 256), 256),
+                ],
+                out_sems.at[slot, 2 * q + h],
             )
+            for q in range(3)
             for h in (0, 1)
         ]
 
-    def up_grad(i, carry):
-        @pl.when(i >= slots)
+    def up_grad(step, carry):
+        slot = lax.rem(step, slots)
+        i, n = step // columns, lax.rem(step, columns)
+
+        @pl.when(step >= slots)
         def _():
-            for copy in up_store(i - slots):
+            for copy in up_store(step - slots):
                 copy.wait()
 
-        turned[pl.ds(0, 256)] = jnp.transpose(act[:, column(i)])
-
-        def one(n, c):
-            x = norm_all[:, :, column(n)].reshape(tokens, 256)
-            staged[lax.rem(i, slots), pl.ds(0, 256), column(n)] = dot(
-                turned[pl.ds(0, 256)], x, PLAIN
-            ).astype(jnp.bfloat16)
-            return c
-
-        lax.fori_loop(0, columns, one, 0)
-        for copy in up_store(i):
+        @pl.when(n == 0)
+        def _():
+            turned[...] = jnp.transpose(act[:, pl.ds(pl.multiple_of(2 * i * three, three), 2 * three)])
+
+        x = norm_all[:, :, column(n)].reshape(tokens, 256)
+        staged[slot] = dot(turned[...], x, PLAIN).astype(jnp.bfloat16)
+        for copy in up_store(step):
             copy.start()
         return carry
 
-    three = 3 * LANES
-
-    def down_store(i):
-        slot = lax.rem(i, slots)
+    def down_store(step):
+        slot = lax.rem(step, slots)
+        i, n = step // columns, lax.rem(step, columns)
         return pltpu.make_async_copy(
-            staged.at[slot],
-            down_grad_hbm.at[pl.ds(pl.multiple_of(i * three, three), three)],
-            out_sems.at[slot, 2],
+            staged.at[slot, pl.ds(0, three)],
+            down_grad_hbm.at[pl.ds(pl.multiple_of(i * three, three), three), column(n)],
+            out_sems.at[slot, 6],
         )
 
-    def down_grad(i, carry):
-        @pl.when(i >= slots)
+    def down_grad(step, carry):
+        slot = lax.rem(step, slots)
+        i, n = step // columns, lax.rem(step, columns)
+
+        @pl.when(step >= slots)
         def _():
-            down_store(i - slots).wait()
-
-        turned[...] = jnp.transpose(hidden[:, pl.ds(pl.multiple_of(i * three, three), three)])
-
-        def one(n, c):
-            x = grad_all[:, :, column(n)].reshape(tokens, 256)
-            staged[lax.rem(i, slots), :, column(n)] = dot(turned[...], x, PLAIN).astype(jnp.bfloat16)
-            return c
-
-        lax.fori_loop(0, columns, one, 0)
-        down_store(i).start()
+            down_store(step - slots).wait()
+
+        @pl.when(n == 0)
+        def _():
+            turned[pl.ds(0, three)] = jnp.transpose(
+                hidden[:, pl.ds(pl.multiple_of(i * three, three), three)]
+            )
+
+        x = grad_all[:, :, column(n)].reshape(tokens, 256)
+        staged[slot, pl.ds(0, three)] = dot(turned[pl.ds(0, three)], x, PLAIN).astype(jnp.bfloat16)
+        down_store(step).start()
         return carry
 
+    ups, downs = chunks // 3 * columns, units // three * columns
     events = reduce.events()
     early = len(events) - 3
-    bounds = [chunks * k // early for k in range(early + 1)]
     for k in range(early):
-        lax.fori_loop(bounds[k], bounds[k + 1], up_grad, 0)
+        lax.fori_loop(ups * k // early, ups * (k + 1) // early, up_grad, 0)
         events[k]()
-    for i in range(max(0, chunks - slots), chunks):
-        for copy in up_store(i):
+    for step in range(max(0, ups - slots), ups):
+        for copy in up_store(step):
             copy.wait()
-    thirds = units // three
-    bounds = [thirds * k // 3 for k in range(4)]
     for k in range(3):
-        lax.fori_loop(bounds[k], bounds[k + 1], down_grad, 0)
+        lax.fori_loop(downs * k // 3, downs * (k + 1) // 3, down_grad, 0)
         events[early + k]()
 
     def after(i, carry):
@@ -1647,8 +1665,8 @@
 
     lax.fori_loop(0, steps, after, 0)
     reduce.finish()
-    for i in range(max(0, thirds - slots), thirds):
-        down_store(i).wait()
+    for step in range(max(0, downs - slots), downs):
+        down_store(step).wait()
 
 
 def feed_forward(branch, tokens, cotangent, gains, gate_up_all, down_all, count, number):
@@ -1661,7 +1679,7 @@
     bf16, f32 = jnp.bfloat16, jnp.float32
     vmem = pl.BlockSpec(memory_space=pltpu.VMEM)
     anywhere = pl.BlockSpec(memory_space=pl.ANY)
-    slots = 2
+    slots = 3
     line_scratch = reduce_blk_scratch(count, piece, bf16)
     return pl.pallas_call(
         functools.partial(feed_forward_kernel, count),
@@ -1688,13 +1706,13 @@
             pltpu.VMEM((rows, width), bf16),
             pltpu.VMEM((rows, width), bf16),
             pltpu.VMEM(piece, f32),
-            pltpu.VMEM((3 * LANES, count * rows), bf16),
-            pltpu.VMEM((slots, 3 * LANES, width), bf16),
+            pltpu.VMEM((6 * LANES, count * rows), bf16),
+            pltpu.VMEM((slots, 6 * LANES, 256), bf16),
         ]
         + line_scratch[:4]
         + [
             pltpu.SemaphoreType.DMA((3 * units // LANES,)),
-            pltpu.SemaphoreType.DMA((slots, 3)),
+            pltpu.SemaphoreType.DMA((slots, 7)),
         ]
         + gather_blk_sems(count)
         + line_scratch[4:]

time: 607 us -> 596 us (0.982); the launches traced: 598 us -> 596 us
  no operation moved by 1% of the time
where the time goes in v8:
time: 596 us
  Pallas kernels  529 us (89%)
  local copies, waits for them, and re-layouts  29.1 us (5%)
  matrix products  24.8 us (4%)
  other arithmetic  11.4 us (2%)
    pallas_call x6, Pallas kernels, transfer(): pl.pallas_call(body, name=name, out_shape=outs, in_specs=[pl.BlockSpec(me...  305 us
    pallas_call x1, Pallas kernels, feed_forward(): pl.pallas_call(functools.partial(feed_forward_kernel, count), name='feed_...  224 us
    dot_general x6, matrix products, dot(): lax.dot_general(left, right, (contract, ((), ())), preferred_element_type...  24.8 us
    unnamed x50, local copies, waits for them, and re-layouts  13.1 us

profile of v8, /device:TPU:20, one launch (start us, length us, event | category | flops | bytes accessed | tf_op | source)
XLA Modules:
  0.0 595.8 jit_solution(599046439928796253)
XLA Ops:
  0.7 1.3 pad_convert_fusion.refs_3_
  2.0 1.7 copy.44
  5.7 53.6 %first1.1 = (bf16[8,128,2304]{2,1,0:T(8,128)(2,1)}, bf16[4,72,512]{2,1,0:T(8,128)(2,1)}, bf16[4,128,2304]{2,1,0:T(8,128)(2,1)}, f32[4,8,8,128]{3,2,1,0:T(8,128)}...) custom-call(bf16[128,2304]{1,0:T(8,128)(2,1)} %refs_0_.1, bf16[4,72,512]{2,1,0:T(8,128)(2,1)} %bitcast.111, ...), custom_call_target="tpu_custom_call" | custom-call | bytes 283115520 | tf_op jit(solution)/shard_map/first1/pallas_call | solution.py:761
  60.3 1.3 constant_dynamic-slice_fusion
  61.7 2.2 multiply_reduce_fusion
  65.3 1.5 copy.27.refs_4_.refs_2_
  67.5 2.6 copy-done.20
  70.1 2.6 fusion.16
  75.9 74.8 %attend2.1 = (bf16[8,512,512]{2,1,0:T(8,128)(2,1)}, bf16[4,8,72,512]{3,2,1,0:T(8,128)(2,1)}, bf16[4,288,4608]{2,1,0:T(8,128)(2,1)}, bf16[4,128,512]{2,1,0:T(8,12...) custom-call(bf16[512,512]{1,0:T(8,128)(2,1)} %copy.38.refs_0_, bf16[4,72,512]{2,1,0:T(8,128)(2,1)} %get-tuple-element.37.refs_1_, ...), custom_call_target="tpu_custom_call" | custom-call | bytes 262144000 | tf_op jit(solution)/shard_map/attend2/pallas_call | solution.py:761
  150.7 4.7 convolution_convert_fusion.1
  155.4 20.0 %fold3.1.branch_ref = f32[8,16,2304]{2,1,0:T(8,128)} custom-call(bf16[4,8,16,2304]{3,2,1,0:T(8,128)(2,1)} %bitcast.105), custom_call_target="tpu_custom_call" | custom-call | bytes 94371840 | tf_op jit(solution)/shard_map/fold3/pallas_call | solution.py:761
  175.4 224.3 %feed_forward.1 = (bf16[8,16,2304]{2,1,0:T(8,128)(2,1)}, f32[8,16,2304]{2,1,0:T(8,128)}, bf16[8,16,2304]{2,1,0:T(8,128)(2,1)}, f32[4,2304]{1,0:T(4,128)}, bf16[1...) custom-call(f32[8,16,2304]{2,1,0:T(8,128)} %fold3.1.branch_ref, bf16[8,16,2304]{2,1,0:T(8,128)(2,1)} %bitcast.98, ...), custom_call_target="tpu_custom_call" | custom-call | flops 48922361856 | bytes 524288000 | tf_op jit(solution)/shard_map/feed_forward/pallas_call | solution.py:1684
  400.8 17.5 %group8.1 = bf16[4,128,2304]{2,1,0:T(8,128)(2,1)} custom-call(bf16[128,2304]{1,0:T(8,128)(2,1)} %bitcast.116), custom_call_target="tpu_custom_call" | custom-call | bytes 94371840 | tf_op jit(solution)/shard_map/group8/pallas_call | solution.py:761
  418.3 4.0 convolution_convert_fusion.2
  422.3 2.8 fusion.2
  425.2 76.2 %attend_back9.1 = (bf16[4,128,512]{2,1,0:T(8,128)(2,1)}, bf16[32,16,512]{2,1,0:T(8,128)(2,1)}, bf16[4,72,512]{2,1,0:T(8,128)(2,1)}, f32[288,4608]{1,0:T(8,128)}) custom-call(bf16[4,128,512]{2,1,0:T(8,128)(2,1)} %copy.39.refs_3_.refs_0_, bf16[8,512,512]{2,1,0:T(8,128)(2,1)} %get-tuple-element.45.refs_1_, s32[4,128,1]{2,1,0:T(8,128)} %copy.27.refs_4_.refs_2_, ...), custom_call_target="tpu_custom_call" | custom-call | bytes 262144000 | tf_op jit(solution)/shard_map/attend_back9/pallas_call | solution.py:761
  507.5 6.5 %fusion.1 = (f32[2304]{0:T(1024)S(1)}, bf16[512,2304]{1,0:T(8,128)(2,1)}) fusion(f32[512]{0:T(512)S(1)} %copy-done.19, bf16[4,128,2304]{2,1,0:T(8,128)(2,1)S(1)} %copy-done.1, bf16[512,1024]{0,1:T(8,128)(2,1)S(1)} %bitcast.112, bf16[1024,2304]{1,0:T(8,128)(2,1)} %bitcast.128), kind=kOutput, calls=%fused_computation.4 | convolution fusion | flops 2421815040 | bytes 10497024 | tf_op jit(solution)/shard_map/dot_general | solution.py:1347
  514.8 4.2 convolution_convert_fusion
  519.0 62.9 %last10.1 = (f32[8,16,2304]{2,1,0:T(8,128)}, f32[8,16,2304]{2,1,0:T(8,128)}, f32[1,8,128]{2,1,0:T(8,128)}, bf16[4,72,512]{2,1,0:T(8,128)(2,1)}, f32[288,2304]{1,0:T(8,128)}) custom-call(bf16[8,8,16,2304]{3,2,1,0:T(8,128)(2,1)} %bitcast.100, bf16[4,8,16,2304]{3,2,1,0:T(8,128)(2,1)} %bitcast.106, f32[8,4,1,8,128]{4,3,2,1,0:T(8,128)} %pad_bitcast_fusion.refs_2_, ...), custom_call_target="tpu_custom_call" | custom-call | bytes 188743680 | tf_op jit(solution)/shard_map/last10/pallas_call | solution.py:761
  581.9 1.3 slice_bitcast_fusion.1
  583.3 1.6 fusion.7
  585.0 1.2 fusion.10
  589.0 5.4 copy.51
  594.3 1.5 copy.52
  (87 shorter events, 18.9 us)
Async XLA Ops:
  4.7 68.3 %copy-start.3 = (f32[512,256]{0,1:T(8,128)}, f32[512,256]{0,1:T(8,128)S(1)}, u32[]{:S(2)}) copy-start(f32[512,256]{0,1:T(8,128)S(1)} %pad_maximum_fusion.2) | copy-start | bytes 1572868
  59.3 7.6 %copy-start = (bf16[4,128,2304]{2,1,0:T(8,128)(2,1)S(1)}, bf16[4,128,2304]{2,1,0:T(8,128)(2,1)}, u32[]{:S(2)}) copy-start(bf16[4,128,2304]{2,1,0:T(8,128)(2,1)} %get-tuple-element.34) | copy-start | bytes 7077892
  64.6 2.9 copy-start.17
  66.9 3.2 copy-start.20
  67.5 5.2 copy-start.8
  399.7 18.6 %copy-start.21 = (bf16[4,8,72,512]{3,2,1,0:T(8,128)(2,1)S(1)}, bf16[4,8,72,512]{3,2,1,0:T(8,128)(2,1)}, u32[]{:S(2)}) copy-start(bf16[4,8,72,512]{3,2,1,0:T(8,128)(2,1)} %get-tuple-element.40) | copy-start | bytes 7077892
  418.3 4.0 copy-start.10
  418.3 4.0 copy-start.22
  501.4 2.0 copy-start.15
  504.3 0.8 copy-start.6
  504.4 1.1 copy-start.4
  504.5 1.2 copy-start.11
  505.7 0.9 slice-start
  505.7 1.8 copy-start.1
  505.7 1.8 copy-start.19
  507.5 7.3 %copy-start.9 = (bf16[4,128,2304]{2,1,0:T(8,128)(2,1)S(1)}, bf16[4,128,2304]{2,1,0:T(8,128)(2,1)}, u32[]{:S(2)}) copy-start(bf16[4,128,2304]{2,1,0:T(8,128)(2,1)} %copy-done.8) | copy-start | bytes 7077892
  519.0 64.3 %copy-start.2 = (bf16[1,128,2304]{2,1,0:T(8,128)(2,1)S(1)}, bf16[1,128,2304]{2,1,0:T(8,128)(2,1)}, u32[]{:S(2)}) copy-start(bf16[1,128,2304]{2,1,0:T(8,128)(2,1)} %param.8) | copy-start | bytes 1769476
  519.0 64.3 %copy-start.18 = (f32[2304]{0:T(1024)S(1)}, f32[2304]{0:T(1024)}, u32[]{:S(2)}) copy-start(f32[2304]{0:T(1024)} %copy-done.17) | copy-start | bytes 27652
  519.0 65.9 %copy-start.12 = (f32[8,16,2304]{2,1,0:T(8,128)S(1)}, f32[8,16,2304]{2,1,0:T(8,128)}, u32[]{:S(2)}) copy-start(f32[8,16,2304]{2,1,0:T(8,128)} %get-tuple-element.44) | copy-start | bytes 3538948
  581.9 3.0 copy-start.5
  583.3 2.9 copy-start.16
  584.9 2.2 copy-start.14
  586.2 1.8 copy-start.13
  589.0 5.4 copy-start.7

commit v9 on v8

--- a/solution.py
+++ b/solution.py
@@ -712,6 +712,7 @@
     first = remote(view(far), from_core.at[1], sent.at[0], came.at[0], place.partner())
     second = remote(view(near), from_core.at[0], sent.at[1], came.at[1], place.partner())
     first.start()
+    yield
     second.start()
     yield
     first.wait_recv()
@@ -1258,7 +1259,7 @@
             waiting(gain, 11),
             main,
             waiting(exchange_group(place, out_ref, out_all, *take(3)), 16),
-            waiting(reduce_group(place, norm_ref, norm_sum, *take(5)), 7, 9),
+            waiting(reduce_group(place, norm_ref, norm_sum, *take(5)), 0, 6, 9),
             *(
                 waiting(task, *rounds)
                 for rounds, task in zip(
@@ -1315,30 +1316,46 @@
     )[0]
 
 
-def reduce_scatter_group(value, number):
-    piece = value.shape[1:]
-    parts = GROUP_PARTS
-    steps = piece[0] // parts
-
-    def body(part, out, *scratch):
+def project_group(attn, weight, piece, number):
+    width = weight.shape[0]
+    parts = 3 if width % 768 == 0 else 1
+    columns = width // parts
+    bf16 = jnp.bfloat16
+
+    def body(attn_ref, weight_ref, out, part, *scratch):
         take = Taker(scratch)
         place = Place(lax.axis_size("blk"))
         greet(place, core=True, half=True)
 
+        def multiply(n, carry):
+            at = pl.ds(pl.multiple_of(n * 256, 256), 256)
+            left = attn_ref[...].reshape(-1, attn.shape[-1])
+            value = dot(left, weight_ref[at], LAST).astype(bf16)
+            part[:, :, :, at] = value.reshape((GROUPS,) + piece[:2] + (256,))
+            return carry
+
         def task(p):
-            at = pl.ds(p * steps, steps)
-            return reduce_group(place, lambda g: part.at[g, at], out.at[at], *take(5))
-
-        together(*[task(p) for p in range(parts)])
+            at = pl.ds(p * columns, columns)
+            return reduce_group(
+                place, lambda g: part.at[g, :, :, at], out.at[:, :, at], *take(5)
+            )
+
+        tasks = [task(p) for p in range(parts)]
+        for p in range(parts):
+            lax.fori_loop(p * columns // 256, (p + 1) * columns // 256, multiply, 0)
+            next(tasks[p])
+            next(tasks[p])
+        together(*tasks)
 
     return transfer(
         f"fold{number}",
         number,
         body,
-        [value],
+        [attn, weight],
         [shape(piece, jnp.float32)],
-        reduce_group_scratch((steps,) + piece[1:], value.dtype) * parts,
-        value.size * 2,
+        [pltpu.VMEM((GROUPS,) + piece, bf16)]
+        + reduce_group_scratch(piece[:2] + (columns,), bf16) * parts,
+        attn.size * 8,
         [pltpu.VMEM],
     )[0]
 
@@ -1990,8 +2007,7 @@
     gate_up_all = gate_up_all.reshape(-1, 2 * width)
     out_head = out_all.reshape(width, head_width)
     attn = attn.reshape(group_rows, head_width)
-    branch_part = dot(attn, out_head, LAST).astype(bf16)
-    branch_slabs = reduce_scatter_group(branch_part.reshape((GROUPS,) + piece), 3)
+    branch_slabs = project_group(attn.reshape(queries.shape), out_head, piece, 3)
     inputs = tokens[0].astype(jnp.float32)
     if feed_forward_fits(count, rows, width, down_all.shape[0]):
         output, middle_grad, branch_grad, gain_rest, gate_up_part, down_part = feed_forward(

time: 596 us -> 592 us (level)
    dot_general x6 -> x5, matrix products: 24.8 us -> 20.1 us  [dot(): lax.dot_general(left, right, (contract, ((), ())), preferred_element_type...]
where the time goes in v9:
time: 592 us; the launch traced here: 591 us
  Pallas kernels  529 us (89%)
  local copies, waits for them, and re-layouts  29.1 us (5%)
  matrix products  20.1 us (3%)
  other arithmetic  11.4 us (2%)
    pallas_call x6, Pallas kernels, transfer(): pl.pallas_call(body, name=name, out_shape=outs, in_specs=[pl.BlockSpec(me...  305 us
    pallas_call x1, Pallas kernels, feed_forward(): pl.pallas_call(functools.partial(feed_forward_kernel, count), name='feed_...  224 us
    dot_general x5, matrix products, dot(): lax.dot_general(left, right, (contract, ((), ())), preferred_element_type...  20.1 us
    unnamed x50, local copies, waits for them, and re-layouts  13.1 us

profile of v9, /device:TPU:20, one launch (start us, length us, event | category | flops | bytes accessed | tf_op | source)
XLA Modules:
  0.0 591.3 jit_solution(9467187185723688303)
XLA Ops:
  0.7 1.3 pad_convert_fusion.refs_3_
  2.0 1.7 copy.44
  5.7 53.6 %first1.1 = (bf16[8,128,2304]{2,1,0:T(8,128)(2,1)}, bf16[4,72,512]{2,1,0:T(8,128)(2,1)}, bf16[4,128,2304]{2,1,0:T(8,128)(2,1)}, f32[4,8,8,128]{3,2,1,0:T(8,128)}...) custom-call(bf16[128,2304]{1,0:T(8,128)(2,1)} %refs_0_.1, bf16[4,72,512]{2,1,0:T(8,128)(2,1)} %bitcast.108, ...), custom_call_target="tpu_custom_call" | custom-call | bytes 283115520 | tf_op jit(solution)/shard_map/first1/pallas_call | solution.py:762
  60.3 1.3 constant_dynamic-slice_fusion
  61.7 2.2 multiply_reduce_fusion
  65.3 1.5 copy.27.refs_4_.refs_2_
  67.5 2.6 copy-done.22
  70.1 2.6 fusion.16
  75.9 74.8 %attend2.1 = (bf16[8,512,512]{2,1,0:T(8,128)(2,1)}, bf16[4,8,72,512]{3,2,1,0:T(8,128)(2,1)}, bf16[4,288,4608]{2,1,0:T(8,128)(2,1)}, bf16[4,128,512]{2,1,0:T(8,12...) custom-call(bf16[512,512]{1,0:T(8,128)(2,1)} %copy.38.refs_0_, bf16[4,72,512]{2,1,0:T(8,128)(2,1)} %get-tuple-element.37.refs_1_, ...), custom_call_target="tpu_custom_call" | custom-call | bytes 262144000 | tf_op jit(solution)/shard_map/attend2/pallas_call | solution.py:762
  150.7 21.8 %fold3.1.branch_ref = f32[8,16,2304]{2,1,0:T(8,128)} custom-call(bf16[4,128,512]{2,1,0:T(8,128)(2,1)} %get-tuple-element.39.attn_ref, bf16[2304,512]{1,0:T(8,128)(2,1)} %bitcast.100), custom_call_target="tpu_custom_call" | custom-call | bytes 83886080 | tf_op jit(solution)/shard_map/fold3/pallas_call | solution.py:762
  172.6 224.0 %feed_forward.1 = (bf16[8,16,2304]{2,1,0:T(8,128)(2,1)}, f32[8,16,2304]{2,1,0:T(8,128)}, bf16[8,16,2304]{2,1,0:T(8,128)(2,1)}, f32[4,2304]{1,0:T(4,128)}, bf16[1...) custom-call(f32[8,16,2304]{2,1,0:T(8,128)} %fold3.1.branch_ref, bf16[8,16,2304]{2,1,0:T(8,128)(2,1)} %bitcast.94, ...), custom_call_target="tpu_custom_call" | custom-call | flops 48922361856 | bytes 524288000 | tf_op jit(solution)/shard_map/feed_forward/pallas_call | solution.py:1701
  397.6 17.6 %group8.1 = bf16[4,128,2304]{2,1,0:T(8,128)(2,1)} custom-call(bf16[128,2304]{1,0:T(8,128)(2,1)} %bitcast.113), custom_call_target="tpu_custom_call" | custom-call | bytes 94371840 | tf_op jit(solution)/shard_map/group8/pallas_call | solution.py:762
  415.2 4.0 convolution_convert_fusion.1
  419.2 2.8 fusion.2
  422.1 76.4 %attend_back9.1 = (bf16[4,128,512]{2,1,0:T(8,128)(2,1)}, bf16[32,16,512]{2,1,0:T(8,128)(2,1)}, bf16[4,72,512]{2,1,0:T(8,128)(2,1)}, f32[288,4608]{1,0:T(8,128)}) custom-call(bf16[4,128,512]{2,1,0:T(8,128)(2,1)} %copy.39.refs_3_.refs_0_, bf16[8,512,512]{2,1,0:T(8,128)(2,1)} %get-tuple-element.45.refs_1_, s32[4,128,1]{2,1,0:T(8,128)} %copy.27.refs_4_.refs_2_, ...), custom_call_target="tpu_custom_call" | custom-call | bytes 262144000 | tf_op jit(solution)/shard_map/attend_back9/pallas_call | solution.py:762
  498.5 1.2 reshape.326
  504.6 6.5 %fusion.1 = (f32[2304]{0:T(1024)S(1)}, bf16[512,2304]{1,0:T(8,128)(2,1)}) fusion(f32[512]{0:T(512)S(1)} %copy-done.21, bf16[4,128,2304]{2,1,0:T(8,128)(2,1)S(1)} %copy-done.1, bf16[512,1024]{0,1:T(8,128)(2,1)S(1)} %bitcast.109, bf16[1024,2304]{1,0:T(8,128)(2,1)} %bitcast.125), kind=kOutput, calls=%fused_computation.4 | convolution fusion | flops 2421815040 | bytes 10497024 | tf_op jit(solution)/shard_map/dot_general | solution.py:1364
  511.9 4.2 convolution_convert_fusion
  516.1 61.2 %last10.1 = (f32[8,16,2304]{2,1,0:T(8,128)}, f32[8,16,2304]{2,1,0:T(8,128)}, f32[1,8,128]{2,1,0:T(8,128)}, bf16[4,72,512]{2,1,0:T(8,128)(2,1)}, f32[288,2304]{1,0:T(8,128)}) custom-call(bf16[8,8,16,2304]{3,2,1,0:T(8,128)(2,1)} %bitcast.96, bf16[4,8,16,2304]{3,2,1,0:T(8,128)(2,1)} %bitcast.103, f32[8,4,1,8,128]{4,3,2,1,0:T(8,128)} %pad_bitcast_fusion.refs_2_, ...), custom_call_target="tpu_custom_call" | custom-call | bytes 188743680 | tf_op jit(solution)/shard_map/last10/pallas_call | solution.py:762
  577.3 1.3 slice_bitcast_fusion.1
  578.7 1.6 fusion.7
  580.4 1.2 fusion.10
  584.4 5.4 copy.51
  589.7 1.5 copy.52
  (86 shorter events, 17.7 us)
Async XLA Ops:
  4.7 68.3 %copy-start.3 = (f32[512,256]{0,1:T(8,128)}, f32[512,256]{0,1:T(8,128)S(1)}, u32[]{:S(2)}) copy-start(f32[512,256]{0,1:T(8,128)S(1)} %pad_maximum_fusion.2) | copy-start | bytes 1572868
  59.3 7.6 %copy-start = (bf16[4,128,2304]{2,1,0:T(8,128)(2,1)S(1)}, bf16[4,128,2304]{2,1,0:T(8,128)(2,1)}, u32[]{:S(2)}) copy-start(bf16[4,128,2304]{2,1,0:T(8,128)(2,1)} %get-tuple-element.34) | copy-start | bytes 7077892
  64.6 2.9 copy-start.19
  66.9 3.2 copy-start.22
  67.5 5.2 copy-start.8
  396.5 18.7 %copy-start.10 = (bf16[4,8,72,512]{3,2,1,0:T(8,128)(2,1)S(1)}, bf16[4,8,72,512]{3,2,1,0:T(8,128)(2,1)}, u32[]{:S(2)}) copy-start(bf16[4,8,72,512]{3,2,1,0:T(8,128)(2,1)} %get-tuple-element.40) | copy-start | bytes 7077892
  415.2 4.0 copy-start.11
  415.2 4.0 copy-start.17
  498.5 2.0 copy-start.16
  501.4 0.8 copy-start.6
  501.6 1.1 copy-start.4
  501.6 1.2 copy-start.12
  502.8 0.9 slice-start
  502.8 1.8 copy-start.1
  502.8 1.8 copy-start.21
  504.6 7.3 %copy-start.9 = (bf16[4,128,2304]{2,1,0:T(8,128)(2,1)S(1)}, bf16[4,128,2304]{2,1,0:T(8,128)(2,1)}, u32[]{:S(2)}) copy-start(bf16[4,128,2304]{2,1,0:T(8,128)(2,1)} %copy-done.8) | copy-start | bytes 7077892
  516.1 62.6 %copy-start.2 = (bf16[1,128,2304]{2,1,0:T(8,128)(2,1)S(1)}, bf16[1,128,2304]{2,1,0:T(8,128)(2,1)}, u32[]{:S(2)}) copy-start(bf16[1,128,2304]{2,1,0:T(8,128)(2,1)} %param.8) | copy-start | bytes 1769476
  516.1 62.6 %copy-start.20 = (f32[2304]{0:T(1024)S(1)}, f32[2304]{0:T(1024)}, u32[]{:S(2)}) copy-start(f32[2304]{0:T(1024)} %copy-done.19) | copy-start | bytes 27652
  516.1 64.2 %copy-start.13 = (f32[8,16,2304]{2,1,0:T(8,128)S(1)}, f32[8,16,2304]{2,1,0:T(8,128)}, u32[]{:S(2)}) copy-start(f32[8,16,2304]{2,1,0:T(8,128)} %get-tuple-element.44) | copy-start | bytes 3538948
  577.3 3.0 copy-start.5
  578.7 2.9 copy-start.18
  580.4 2.2 copy-start.15
  581.6 1.8 copy-start.14
  584.4 5.4 copy-start.7

commit v10 on v9

--- a/solution.py
+++ b/solution.py
@@ -69,7 +69,7 @@
     )
 
 
-def greet(place, blk=False, core=False, half=False, corner=False):
+def greet(place, blk=False, core=False, half=False, corner=False, meanwhile=None):
     sem = pltpu.get_barrier_semaphore()
     amount = jnp.int32(0)
 
@@ -91,6 +91,8 @@
         if wanted:
             hello(device)
             amount = amount + 1
+    if meanwhile:
+        meanwhile()
     pl.semaphore_wait(sem, amount)
 
 
@@ -1472,8 +1474,7 @@
         norm_own[slab_rows(i)] = (mid * scale_of(mid) * gain_ref[2:3]).astype(jnp.bfloat16)
         return carry
 
-    lax.fori_loop(0, steps, before, 0)
-    greet(place, blk=True)
+    greet(place, blk=True, meanwhile=lambda: lax.fori_loop(0, steps, before, 0))
 
     def pair_rows(k):
         return pl.ds(pl.multiple_of(place.near_at(k) * pair, pair), pair)

time: 592 us -> 590 us (level)
  no operation moved by 1% of the time
where the time goes in v10:
time: 590 us
  Pallas kernels  528 us (89%)
  local copies, waits for them, and re-layouts  29.1 us (5%)
  matrix products  20.1 us (3%)
  other arithmetic  11.4 us (2%)
    pallas_call x6, Pallas kernels, transfer(): pl.pallas_call(body, name=name, out_shape=outs, in_specs=[pl.BlockSpec(me...  305 us
    pallas_call x1, Pallas kernels, feed_forward(): pl.pallas_call(functools.partial(feed_forward_kernel, count), name='feed_...  222 us
    dot_general x5, matrix products, dot(): lax.dot_general(left, right, (contract, ((), ())), preferred_element_type...  20.1 us
    unnamed x50, local copies, waits for them, and re-layouts  13.1 us

profile of v10, /device:TPU:20, one launch (start us, length us, event | category | flops | bytes accessed | tf_op | source)
XLA Modules:
  0.0 589.6 jit_solution(5831390523152777115)
XLA Ops:
  0.7 1.3 pad_convert_fusion.refs_3_
  2.0 1.7 copy.44
  5.7 53.6 %first1.1 = (bf16[8,128,2304]{2,1,0:T(8,128)(2,1)}, bf16[4,72,512]{2,1,0:T(8,128)(2,1)}, bf16[4,128,2304]{2,1,0:T(8,128)(2,1)}, f32[4,8,8,128]{3,2,1,0:T(8,128)}...) custom-call(bf16[128,2304]{1,0:T(8,128)(2,1)} %refs_0_.1, bf16[4,72,512]{2,1,0:T(8,128)(2,1)} %bitcast.108, ...), custom_call_target="tpu_custom_call" | custom-call | bytes 283115520 | tf_op jit(solution)/shard_map/first1/pallas_call | solution.py:764
  60.3 1.3 constant_dynamic-slice_fusion
  61.7 2.2 multiply_reduce_fusion
  65.3 1.5 copy.27.refs_4_.refs_2_
  67.5 2.6 copy-done.22
  70.1 2.6 fusion.16
  75.9 74.8 %attend2.1 = (bf16[8,512,512]{2,1,0:T(8,128)(2,1)}, bf16[4,8,72,512]{3,2,1,0:T(8,128)(2,1)}, bf16[4,288,4608]{2,1,0:T(8,128)(2,1)}, bf16[4,128,512]{2,1,0:T(8,12...) custom-call(bf16[512,512]{1,0:T(8,128)(2,1)} %copy.38.refs_0_, bf16[4,72,512]{2,1,0:T(8,128)(2,1)} %get-tuple-element.37.refs_1_, ...), custom_call_target="tpu_custom_call" | custom-call | bytes 262144000 | tf_op jit(solution)/shard_map/attend2/pallas_call | solution.py:764
  150.7 21.8 %fold3.1.branch_ref = f32[8,16,2304]{2,1,0:T(8,128)} custom-call(bf16[4,128,512]{2,1,0:T(8,128)(2,1)} %get-tuple-element.39.attn_ref, bf16[2304,512]{1,0:T(8,128)(2,1)} %bitcast.100), custom_call_target="tpu_custom_call" | custom-call | bytes 83886080 | tf_op jit(solution)/shard_map/fold3/pallas_call | solution.py:764
  172.6 222.4 %feed_forward.1 = (bf16[8,16,2304]{2,1,0:T(8,128)(2,1)}, f32[8,16,2304]{2,1,0:T(8,128)}, bf16[8,16,2304]{2,1,0:T(8,128)(2,1)}, f32[4,2304]{1,0:T(4,128)}, bf16[1...) custom-call(f32[8,16,2304]{2,1,0:T(8,128)} %fold3.1.branch_ref, bf16[8,16,2304]{2,1,0:T(8,128)(2,1)} %bitcast.94, ...), custom_call_target="tpu_custom_call" | custom-call | flops 48922361856 | bytes 524288000 | tf_op jit(solution)/shard_map/feed_forward/pallas_call | solution.py:1702
  396.0 17.6 %group8.1 = bf16[4,128,2304]{2,1,0:T(8,128)(2,1)} custom-call(bf16[128,2304]{1,0:T(8,128)(2,1)} %bitcast.113), custom_call_target="tpu_custom_call" | custom-call | bytes 94371840 | tf_op jit(solution)/shard_map/group8/pallas_call | solution.py:764
  413.6 4.0 convolution_convert_fusion.1
  417.6 2.8 fusion.2
  420.4 76.4 %attend_back9.1 = (bf16[4,128,512]{2,1,0:T(8,128)(2,1)}, bf16[32,16,512]{2,1,0:T(8,128)(2,1)}, bf16[4,72,512]{2,1,0:T(8,128)(2,1)}, f32[288,4608]{1,0:T(8,128)}) custom-call(bf16[4,128,512]{2,1,0:T(8,128)(2,1)} %copy.39.refs_3_.refs_0_, bf16[8,512,512]{2,1,0:T(8,128)(2,1)} %get-tuple-element.45.refs_1_, s32[4,128,1]{2,1,0:T(8,128)} %copy.27.refs_4_.refs_2_, ...), custom_call_target="tpu_custom_call" | custom-call | bytes 262144000 | tf_op jit(solution)/shard_map/attend_back9/pallas_call | solution.py:764
  496.9 1.2 reshape.326
  502.9 6.5 %fusion.1 = (f32[2304]{0:T(1024)S(1)}, bf16[512,2304]{1,0:T(8,128)(2,1)}) fusion(f32[512]{0:T(512)S(1)} %copy-done.21, bf16[4,128,2304]{2,1,0:T(8,128)(2,1)S(1)} %copy-done.1, bf16[512,1024]{0,1:T(8,128)(2,1)S(1)} %bitcast.109, bf16[1024,2304]{1,0:T(8,128)(2,1)} %bitcast.125), kind=kOutput, calls=%fused_computation.4 | convolution fusion | flops 2421815040 | bytes 10497024 | tf_op jit(solution)/shard_map/dot_general | solution.py:1366
  510.3 4.2 convolution_convert_fusion
  514.5 61.2 %last10.1 = (f32[8,16,2304]{2,1,0:T(8,128)}, f32[8,16,2304]{2,1,0:T(8,128)}, f32[1,8,128]{2,1,0:T(8,128)}, bf16[4,72,512]{2,1,0:T(8,128)(2,1)}, f32[288,2304]{1,0:T(8,128)}) custom-call(bf16[8,8,16,2304]{3,2,1,0:T(8,128)(2,1)} %bitcast.96, bf16[4,8,16,2304]{3,2,1,0:T(8,128)(2,1)} %bitcast.103, f32[8,4,1,8,128]{4,3,2,1,0:T(8,128)} %pad_bitcast_fusion.refs_2_, ...), custom_call_target="tpu_custom_call" | custom-call | bytes 188743680 | tf_op jit(solution)/shard_map/last10/pallas_call | solution.py:764
  575.7 1.3 slice_bitcast_fusion.1
  577.1 1.6 fusion.7
  578.7 1.2 fusion.10
  582.7 5.4 copy.51
  588.1 1.5 copy.52
  (86 shorter events, 17.7 us)
Async XLA Ops:
  4.7 68.3 %copy-start.3 = (f32[512,256]{0,1:T(8,128)}, f32[512,256]{0,1:T(8,128)S(1)}, u32[]{:S(2)}) copy-start(f32[512,256]{0,1:T(8,128)S(1)} %pad_maximum_fusion.2) | copy-start | bytes 1572868
  59.3 7.6 %copy-start = (bf16[4,128,2304]{2,1,0:T(8,128)(2,1)S(1)}, bf16[4,128,2304]{2,1,0:T(8,128)(2,1)}, u32[]{:S(2)}) copy-start(bf16[4,128,2304]{2,1,0:T(8,128)(2,1)} %get-tuple-element.34) | copy-start | bytes 7077892
  64.6 2.9 copy-start.19
  66.9 3.2 copy-start.22
  67.5 5.2 copy-start.8
  394.9 18.7 %copy-start.10 = (bf16[4,8,72,512]{3,2,1,0:T(8,128)(2,1)S(1)}, bf16[4,8,72,512]{3,2,1,0:T(8,128)(2,1)}, u32[]{:S(2)}) copy-start(bf16[4,8,72,512]{3,2,1,0:T(8,128)(2,1)} %get-tuple-element.40) | copy-start | bytes 7077892
  413.6 4.0 copy-start.11
  413.6 4.0 copy-start.17
  496.9 2.0 copy-start.16
  499.8 0.8 copy-start.6
  499.9 1.1 copy-start.4
  500.0 1.2 copy-start.12
  501.2 0.9 slice-start
  501.2 1.8 copy-start.1
  501.2 1.8 copy-start.21
  502.9 7.3 %copy-start.9 = (bf16[4,128,2304]{2,1,0:T(8,128)(2,1)S(1)}, bf16[4,128,2304]{2,1,0:T(8,128)(2,1)}, u32[]{:S(2)}) copy-start(bf16[4,128,2304]{2,1,0:T(8,128)(2,1)} %copy-done.8) | copy-start | bytes 7077892
  514.5 62.6 %copy-start.2 = (bf16[1,128,2304]{2,1,0:T(8,128)(2,1)S(1)}, bf16[1,128,2304]{2,1,0:T(8,128)(2,1)}, u32[]{:S(2)}) copy-start(bf16[1,128,2304]{2,1,0:T(8,128)(2,1)} %param.8) | copy-start | bytes 1769476
  514.5 62.6 %copy-start.20 = (f32[2304]{0:T(1024)S(1)}, f32[2304]{0:T(1024)}, u32[]{:S(2)}) copy-start(f32[2304]{0:T(1024)} %copy-done.19) | copy-start | bytes 27652
  514.5 64.2 %copy-start.13 = (f32[8,16,2304]{2,1,0:T(8,128)S(1)}, f32[8,16,2304]{2,1,0:T(8,128)}, u32[]{:S(2)}) copy-start(f32[8,16,2304]{2,1,0:T(8,128)} %get-tuple-element.44) | copy-start | bytes 3538948
  575.7 3.0 copy-start.5
  577.1 2.9 copy-start.18
  578.7 2.2 copy-start.15
  580.0 1.8 copy-start.14
  582.7 5.4 copy-start.7
